TPU v7x, 32 devices: a whole 2x2x4 slice. The times are simulated.
32 devices in a mesh: fsdp: 2 (over x), ctx: 4 (over y, core), tp: 4 (over z).
Axes of the slice: x: 2, y: 2, z: 4, core: 2. Of those that a mesh axis runs over, the one named last changes fastest.
Arguments:
- prompt_in: bfloat16 [4, 1024, 2048], P('fsdp', 'ctx', 'tp'), may hold values from -6 to 6
- cont_in: bfloat16 [16, 128, 2048], P(('fsdp', 'ctx'), None, 'tp'), may hold values from -6 to 6
- prompt_mask: int32 [4, 1024], P('fsdp', 'ctx'), may hold values 0 or 1
- cont_mask: int32 [16, 128], P(('fsdp', 'ctx')), may hold values 0 or 1
- cont_prompt: int32 [16], P(('fsdp', 'ctx')), may hold values from 0 to 3, as said below
- cont_start: int32 [16], P(('fsdp', 'ctx')), may hold values from 1024 to 2047
- gain_attn: bfloat16 [2048], P('tp'), may hold values from 0.5 to 1.5
- gain_ffn: bfloat16 [2048], P('tp'), may hold values from 0.5 to 1.5
- router: bfloat16 [2048], P('tp'), may hold values from -0.125 to 0.125
- w_query: bfloat16 [2048, 2048], P('fsdp', 'tp'), may hold values from -0.125 to 0.125
- key_projection: bfloat16 [2048, 512], P('fsdp', 'tp'), may hold values from -0.125 to 0.125
- w_value: bfloat16 [2048, 512], P('fsdp', 'tp'), may hold values from -0.125 to 0.125
- w_out: bfloat16 [2048, 2048], P('tp', 'fsdp'), may hold values from -1.5 to 1.5
- w_gate: bfloat16 [2048, 8192], P('fsdp', 'tp'), may hold values from -0.125 to 0.125
- w_up: bfloat16 [2048, 8192], P('fsdp', 'tp'), may hold values from -0.125 to 0.125
- w_down: bfloat16 [8192, 2048], P('tp', 'fsdp'), may hold values from -0.0625 to 0.0625
- prompt_cot: bfloat16 [4, 1024, 2048], P('fsdp', 'ctx', 'tp'), may hold values from -6 to 6
- cont_cot: bfloat16 [16, 128, 2048], P(('fsdp', 'ctx'), None, 'tp'), may hold values from -6 to 6
Outputs:
- prompt_out: bfloat16 [4, 1024, 2048], P('fsdp', 'ctx', 'tp')
- cont_out: bfloat16 [16, 128, 2048], P(('fsdp', 'ctx'), None, 'tp')
- prompt_grad: float32 [4, 1024, 2048], P('fsdp', 'ctx', 'tp')
- cont_grad: float32 [16, 128, 2048], P(('fsdp', 'ctx'), None, 'tp')
- grad_gain_attn: float32 [2048], P('tp')
- grad_gain_ffn: float32 [2048], P('tp')
- grad_router: float32 [2048], P('tp')
- grad_query: float32 [2048, 2048], P('fsdp', 'tp')
- grad_key: float32 [2048, 512], P('fsdp', 'tp')
- grad_value: float32 [2048, 512], P('fsdp', 'tp')
- grad_out: float32 [2048, 2048], P('tp', 'fsdp')
- grad_gate: float32 [2048, 8192], P('fsdp', 'tp')
- grad_up: float32 [2048, 8192], P('fsdp', 'tp')
- grad_down: float32 [8192, 2048], P('tp', 'fsdp')
Inputs may be any that keep to these rules, and one draw needn't show every extreme that they name: `cont_prompt`: continuation c names a prompt of its own block: (c // 8) * 2 plus a value below 2; each prompt is named by exactly 4 continuations.
All inputs are finite; a program needn't handle non-finite values. No bound on the sum of `prompt_mask` or of `cont_mask` on one device may be relied on, other than what follows from the above.
Results may differ from a plain program's by a relative error of at most 0.014.
Values may be sent and summed in bfloat16 or wider, within the bound.
No kernel may reach another device: no remote copies, remote signals or barrier semaphores. Data moves between devices by JAX's collectives and lax.ppermute only.
A program may use at most 256 MiB of HBM per device.

v0:
```python
import jax
import jax.numpy as jnp
from jax import lax
from jax.sharding import PartitionSpec as P

HEAD_SIZE = 64
CONTINUATION_LEN = 128


EPSILON = 1e-05
ROPE_BASE = 500000.0


def product(left, right):
    return jnp.dot(left, right, preferred_element_type=jnp.float32)


def apply_rotation(values, token_positions, head_count, direction):
    head_width = values.shape[-1] // head_count
    half_width = head_width // 2
    frequency = ROPE_BASE ** (-jnp.arange(half_width, dtype=jnp.float32) * 2.0 / head_width)
    angles = token_positions.astype(jnp.float32)[:, None] * frequency[None, :]
    cosine = jnp.cos(angles)[:, None, :]
    sine_part = direction * jnp.sin(angles)[:, None, :]
    shaped = values.reshape(values.shape[0], head_count, head_width)
    first_half = shaped[..., :half_width]
    second_half = shaped[..., half_width:]
    turned = jnp.concatenate(
        [
            first_half * cosine - second_half * sine_part,
            second_half * cosine + first_half * sine_part,
        ],
        axis=-1,
    )
    return turned.reshape(values.shape)


def row_sums(stacked):
    return lax.psum(stacked, "tp")


def widen(local_part):
    return lax.all_gather(local_part, "tp", axis=1, tiled=True)


def narrow(partial_sum):
    return lax.psum_scatter(partial_sum, "tp", scatter_dimension=1, tiled=True)


def attend_scores(query_split, key_split, allowed):
    scores = (
        jnp.einsum("gqkrd,gskd->gkrqs", query_split, key_split, preferred_element_type=jnp.float32)
        * 0.125
    )
    return jnp.where(allowed, scores, -1e30)


def attend_forward(query_split, key_split, value_split, allowed):
    scores = attend_scores(query_split, key_split, allowed)
    row_max = jnp.max(scores, axis=-1, keepdims=True)
    exponent = jnp.exp(scores - row_max)
    total = jnp.sum(exponent, axis=-1, keepdims=True)
    prob_low = (exponent / total).astype(jnp.bfloat16)
    result = jnp.einsum(
        "gkrqs,gskd->gqkrd", prob_low, value_split, preferred_element_type=jnp.float32
    ).astype(jnp.bfloat16)
    return (result.reshape(result.shape[0], result.shape[1], -1), row_max + jnp.log(total))


def attend_backward(query_split, key_split, value_split, allowed, log_total, out_grad):
    grad_split = out_grad.reshape(query_split.shape)
    scores = attend_scores(query_split, key_split, allowed)
    prob_full = jnp.exp(scores - log_total)
    prob_low = prob_full.astype(jnp.bfloat16)
    value_grad = jnp.einsum(
        "gkrqs,gqkrd->gskd", prob_low, grad_split, preferred_element_type=jnp.float32
    )
    prob_grad = jnp.einsum(
        "gqkrd,gskd->gkrqs", grad_split, value_split, preferred_element_type=jnp.float32
    )
    score_grad = (
        prob_full * (prob_grad - jnp.sum(prob_grad * prob_full, axis=-1, keepdims=True))
    ).astype(jnp.bfloat16)
    query_grad = (
        jnp.einsum("gkrqs,gskd->gqkrd", score_grad, key_split, preferred_element_type=jnp.float32)
        * 0.125
    )
    key_grad = (
        jnp.einsum("gkrqs,gqkrd->gskd", score_grad, query_split, preferred_element_type=jnp.float32)
        * 0.125
    )
    batch_count = query_split.shape[0]
    return (
        query_grad.reshape(batch_count, query_split.shape[1], -1),
        key_grad.reshape(batch_count, key_split.shape[1], -1),
        value_grad.reshape(batch_count, key_split.shape[1], -1),
    )


def body(
    prompt_in,
    cont_in,
    prompt_mask,
    cont_mask,
    cont_prompt,
    cont_start,
    gain_attn,
    gain_ffn,
    router,
    w_query,
    key_projection,
    w_value,
    w_out,
    w_gate,
    w_up,
    w_down,
    prompt_cot,
    cont_cot,
):
    group_number = prompt_in.shape[0]
    prompt_rows = prompt_in.shape[1]
    width_local = prompt_in.shape[2]
    continuation_count = cont_in.shape[0]
    model_width = width_local * lax.axis_size("tp")
    ctx_index = lax.axis_index("ctx")
    fsdp_index = lax.axis_index("fsdp")
    query_heads = w_query.shape[1] // HEAD_SIZE
    key_heads = key_projection.shape[1] // HEAD_SIZE
    group_width = query_heads // key_heads
    key_width = key_projection.shape[1]
    prompt_tokens = group_number * prompt_rows
    cont_tokens = continuation_count * CONTINUATION_LEN
    token_low = jnp.concatenate(
        [prompt_in.reshape(prompt_tokens, width_local), cont_in.reshape(cont_tokens, width_local)],
        axis=0,
    )
    tokens = token_low.astype(jnp.float32)
    row_index = jnp.arange(prompt_rows, dtype=jnp.int32)
    query_place = ctx_index * prompt_rows + row_index
    cont_pos = (
        cont_start[:, None] + jnp.arange(CONTINUATION_LEN, dtype=jnp.int32)[None, :]
    ).reshape(-1)
    token_positions = jnp.concatenate([jnp.tile(query_place, group_number), cont_pos], axis=0)
    gates_on = jnp.concatenate([prompt_mask.reshape(-1), cont_mask.reshape(-1)], axis=0).astype(
        jnp.float32
    )
    shard_apply = cont_prompt - fsdp_index * group_number
    gain_one = gain_attn.astype(jnp.float32)
    gain_two = gain_ffn.astype(jnp.float32)
    router_vec = router.astype(jnp.float32)
    wide_query, wide_key, wide_value, wide_out, wide_gate, wide_up, wide_down = (
        lax.all_gather(w_query, "fsdp", axis=0, tiled=True),
        lax.all_gather(key_projection, "fsdp", axis=0, tiled=True),
        lax.all_gather(w_value, "fsdp", axis=0, tiled=True),
        lax.all_gather(w_out, "fsdp", axis=1, tiled=True),
        lax.all_gather(w_gate, "fsdp", axis=0, tiled=True),
        lax.all_gather(w_up, "fsdp", axis=0, tiled=True),
        lax.all_gather(w_down, "fsdp", axis=1, tiled=True),
    )
    first_stats = row_sums(
        jnp.stack(
            [
                jnp.sum(tokens * tokens, axis=1),
                jnp.dot(token_low, router, preferred_element_type=jnp.float32),
            ]
        )
    )
    scale_attn = lax.rsqrt(first_stats[0] / model_width + EPSILON)
    router_gate = jax.nn.sigmoid(first_stats[1])
    mixing = gates_on * router_gate
    normed_attn = widen((tokens * scale_attn[:, None] * gain_one).astype(jnp.bfloat16))
    query_rows = apply_rotation(
        product(normed_attn, wide_query), token_positions, query_heads, 1.0
    ).astype(jnp.bfloat16)
    key_rows = apply_rotation(
        product(normed_attn, wide_key), token_positions, key_heads, 1.0
    ).astype(jnp.bfloat16)
    value_rows = product(normed_attn, wide_value).astype(jnp.bfloat16)
    key_gathered, value_gathered = (
        lax.all_gather(
            key_rows[:prompt_tokens].reshape(group_number, prompt_rows, key_width),
            "ctx",
            axis=1,
            tiled=True,
        ),
        lax.all_gather(
            value_rows[:prompt_tokens].reshape(group_number, prompt_rows, key_width),
            "ctx",
            axis=1,
            tiled=True,
        ),
    )
    prompt_length = key_gathered.shape[1]
    prompt_query = query_rows[:prompt_tokens].reshape(
        group_number, prompt_rows, key_heads, group_width, HEAD_SIZE
    )
    prompt_key_rows = key_gathered.reshape(group_number, prompt_length, key_heads, HEAD_SIZE)
    prompt_value_rows = value_gathered.reshape(group_number, prompt_length, key_heads, HEAD_SIZE)
    prompt_allowed = jnp.arange(prompt_length, dtype=jnp.int32)[None, :] <= query_place[:, None]
    cont_query = query_rows[prompt_tokens:].reshape(
        continuation_count, CONTINUATION_LEN, key_heads, group_width, HEAD_SIZE
    )
    continuation_keys = jnp.concatenate(
        [
            jnp.take(key_gathered, shard_apply, axis=0),
            key_rows[prompt_tokens:].reshape(continuation_count, CONTINUATION_LEN, key_width),
        ],
        axis=1,
    ).reshape(continuation_count, prompt_length + CONTINUATION_LEN, key_heads, HEAD_SIZE)
    continuation_values = jnp.concatenate(
        [
            jnp.take(value_gathered, shard_apply, axis=0),
            value_rows[prompt_tokens:].reshape(continuation_count, CONTINUATION_LEN, key_width),
        ],
        axis=1,
    ).reshape(continuation_count, prompt_length + CONTINUATION_LEN, key_heads, HEAD_SIZE)
    cont_allowed = jnp.concatenate(
        [
            jnp.ones((CONTINUATION_LEN, prompt_length), dtype=bool),
            jnp.arange(CONTINUATION_LEN)[None, :] <= jnp.arange(CONTINUATION_LEN)[:, None],
        ],
        axis=1,
    )
    prompt_att, prompt_total = attend_forward(
        prompt_query, prompt_key_rows, prompt_value_rows, prompt_allowed
    )
    cont_att, cont_total = attend_forward(
        cont_query, continuation_keys, continuation_values, cont_allowed
    )
    attended = jnp.concatenate(
        [prompt_att.reshape(prompt_tokens, -1), cont_att.reshape(cont_tokens, -1)], axis=0
    )
    branch_attn = narrow(product(attended, wide_out))
    hidden = tokens + branch_attn
    second_stats = row_sums(jnp.sum(hidden * hidden, axis=1)[None, :])
    scale_ffn = lax.rsqrt(second_stats[0] / model_width + EPSILON)
    normed_ffn = widen((hidden * scale_ffn[:, None] * gain_two).astype(jnp.bfloat16))
    gate_pre = product(normed_ffn, wide_gate)
    up_pre = product(normed_ffn, wide_up)
    sigmoid_gate = jax.nn.sigmoid(gate_pre)
    inner_act = (gate_pre * sigmoid_gate * up_pre).astype(jnp.bfloat16)
    branch_ffn = narrow(product(inner_act, wide_down))
    branch_sum = branch_attn + branch_ffn
    output = tokens + mixing[:, None] * branch_sum
    back_query, back_key, back_value, back_out, back_gate, back_up, back_down = (
        lax.all_gather(w_query, "fsdp", axis=0, tiled=True),
        lax.all_gather(key_projection, "fsdp", axis=0, tiled=True),
        lax.all_gather(w_value, "fsdp", axis=0, tiled=True),
        lax.all_gather(w_out, "fsdp", axis=1, tiled=True),
        lax.all_gather(w_gate, "fsdp", axis=0, tiled=True),
        lax.all_gather(w_up, "fsdp", axis=0, tiled=True),
        lax.all_gather(w_down, "fsdp", axis=1, tiled=True),
    )
    cotangent = jnp.concatenate(
        [
            prompt_cot.reshape(prompt_tokens, width_local),
            cont_cot.reshape(cont_tokens, width_local),
        ],
        axis=0,
    ).astype(jnp.float32)
    branch_grad = cotangent * mixing[:, None]
    ffn_grad_wide = widen(branch_grad.astype(jnp.bfloat16))
    grad_down = product(inner_act.T, ffn_grad_wide)
    inner_grad = product(ffn_grad_wide, back_down.T)
    gate_grad = (
        inner_grad * up_pre * sigmoid_gate * (1.0 + gate_pre * (1.0 - sigmoid_gate))
    ).astype(jnp.bfloat16)
    up_grad = (inner_grad * gate_pre * sigmoid_gate).astype(jnp.bfloat16)
    grad_gate = product(normed_ffn.T, gate_grad)
    grad_up = product(normed_ffn.T, up_grad)
    normed_ffn_grad = narrow(product(gate_grad, back_gate.T) + product(up_grad, back_up.T))
    third_stats = row_sums(
        jnp.stack(
            [
                jnp.sum(hidden * gain_two * normed_ffn_grad, axis=1),
                jnp.sum(cotangent * branch_sum, axis=1),
            ]
        )
    )
    logit_grad = third_stats[1] * gates_on * router_gate * (1.0 - router_gate)
    back_ffn = (
        scale_ffn[:, None] * gain_two * normed_ffn_grad
        - hidden * (scale_ffn**3 * third_stats[0] / model_width)[:, None]
    )
    gain_ffn_local = jnp.sum(hidden * scale_ffn[:, None] * normed_ffn_grad, axis=0)
    attn_grad_wide = widen((branch_grad + back_ffn).astype(jnp.bfloat16))
    grad_out = product(attended.T, attn_grad_wide)
    attended_grad = product(attn_grad_wide, back_out.T).astype(jnp.bfloat16)
    prompt_q_grad, prompt_k_grad, prompt_v_grad = attend_backward(
        prompt_query,
        prompt_key_rows,
        prompt_value_rows,
        prompt_allowed,
        prompt_total,
        attended_grad[:prompt_tokens].reshape(group_number, prompt_rows, -1),
    )
    cont_q_grad, cont_k_grad, cont_v_grad = attend_backward(
        cont_query,
        continuation_keys,
        continuation_values,
        cont_allowed,
        cont_total,
        attended_grad[prompt_tokens:].reshape(continuation_count, CONTINUATION_LEN, -1),
    )
    one_hot = (shard_apply[:, None] == jnp.arange(group_number, dtype=jnp.int32)[None, :]).astype(
        jnp.float32
    )
    key_to_prompt = prompt_k_grad + jnp.einsum(
        "cg,csx->gsx", one_hot, cont_k_grad[:, :prompt_length], precision=lax.Precision.HIGHEST
    )
    value_to_prompt = prompt_v_grad + jnp.einsum(
        "cg,csx->gsx", one_hot, cont_v_grad[:, :prompt_length], precision=lax.Precision.HIGHEST
    )
    key_mine, value_mine = (
        lax.psum_scatter(key_to_prompt, "ctx", scatter_dimension=1, tiled=True),
        lax.psum_scatter(value_to_prompt, "ctx", scatter_dimension=1, tiled=True),
    )
    query_grad_all = jnp.concatenate(
        [prompt_q_grad.reshape(prompt_tokens, -1), cont_q_grad.reshape(cont_tokens, -1)], axis=0
    )
    key_grad_all = jnp.concatenate(
        [
            key_mine.reshape(prompt_tokens, key_width),
            cont_k_grad[:, prompt_length:].reshape(cont_tokens, key_width),
        ],
        axis=0,
    )
    value_grad_all = jnp.concatenate(
        [
            value_mine.reshape(prompt_tokens, key_width),
            cont_v_grad[:, prompt_length:].reshape(cont_tokens, key_width),
        ],
        axis=0,
    )
    query_pre = apply_rotation(query_grad_all, token_positions, query_heads, -1.0).astype(
        jnp.bfloat16
    )
    key_pre = apply_rotation(key_grad_all, token_positions, key_heads, -1.0).astype(jnp.bfloat16)
    value_pre = value_grad_all.astype(jnp.bfloat16)
    grad_query = product(normed_attn.T, query_pre)
    grad_key = product(normed_attn.T, key_pre)
    grad_value = product(normed_attn.T, value_pre)
    normed_attn_grad = narrow(
        product(query_pre, back_query.T)
        + product(key_pre, back_key.T)
        + product(value_pre, back_value.T)
    )
    fourth_stats = row_sums(jnp.sum(tokens * gain_one * normed_attn_grad, axis=1)[None, :])
    back_attn = (
        scale_attn[:, None] * gain_one * normed_attn_grad
        - tokens * (scale_attn**3 * fourth_stats[0] / model_width)[:, None]
    )
    gain_attn_local = jnp.sum(tokens * scale_attn[:, None] * normed_attn_grad, axis=0)
    router_local = jnp.sum(tokens * logit_grad[:, None], axis=0)
    token_grad = cotangent + logit_grad[:, None] * router_vec + back_ffn + back_attn
    small_sums = lax.psum((gain_attn_local, gain_ffn_local, router_local), ("fsdp", "ctx"))
    pieces = (
        lax.psum_scatter(grad_query, "fsdp", scatter_dimension=0, tiled=True),
        lax.psum_scatter(grad_key, "fsdp", scatter_dimension=0, tiled=True),
        lax.psum_scatter(grad_value, "fsdp", scatter_dimension=0, tiled=True),
        lax.psum_scatter(grad_out, "fsdp", scatter_dimension=1, tiled=True),
        lax.psum_scatter(grad_gate, "fsdp", scatter_dimension=0, tiled=True),
        lax.psum_scatter(grad_up, "fsdp", scatter_dimension=0, tiled=True),
        lax.psum_scatter(grad_down, "fsdp", scatter_dimension=1, tiled=True),
    )
    summed = lax.psum(
        (pieces[0], pieces[1], pieces[2], pieces[3], pieces[4], pieces[5], pieces[6]), "ctx"
    )
    prompt_out = (
        output[:prompt_tokens].reshape(group_number, prompt_rows, width_local).astype(jnp.bfloat16)
    )
    cont_out = (
        output[prompt_tokens:]
        .reshape(continuation_count, CONTINUATION_LEN, width_local)
        .astype(jnp.bfloat16)
    )
    prompt_grad = token_grad[:prompt_tokens].reshape(group_number, prompt_rows, width_local)
    cont_grad = token_grad[prompt_tokens:].reshape(
        continuation_count, CONTINUATION_LEN, width_local
    )
    return (
        prompt_out,
        cont_out,
        prompt_grad,
        cont_grad,
        small_sums[0],
        small_sums[1],
        small_sums[2],
        summed[0],
        summed[1],
        summed[2],
        summed[3],
        summed[4],
        summed[5],
        summed[6],
    )


def solution(mesh):
    placed = (
        P("fsdp", "ctx", "tp"),
        P(("fsdp", "ctx"), None, "tp"),
        P("fsdp", "ctx"),
        P(("fsdp", "ctx"), None),
        P(("fsdp", "ctx")),
        P(("fsdp", "ctx")),
        P("tp"),
        P("tp"),
        P("tp"),
        P("fsdp", "tp"),
        P("fsdp", "tp"),
        P("fsdp", "tp"),
        P("tp", "fsdp"),
        P("fsdp", "tp"),
        P("fsdp", "tp"),
        P("tp", "fsdp"),
        P("fsdp", "ctx", "tp"),
        P(("fsdp", "ctx"), None, "tp"),
    )
    return jax.shard_map(
        body,
        mesh=mesh,
        in_specs=placed,
        out_specs=(
            P("fsdp", "ctx", "tp"),
            P(("fsdp", "ctx"), None, "tp"),
            P("fsdp", "ctx", "tp"),
            P(("fsdp", "ctx"), None, "tp"),
            P("tp"),
            P("tp"),
            P("tp"),
            P("fsdp", "tp"),
            P("fsdp", "tp"),
            P("fsdp", "tp"),
            P("tp", "fsdp"),
            P("fsdp", "tp"),
            P("fsdp", "tp"),
            P("tp", "fsdp"),
        ),
        check_vma=False,
    )
```

profile of v0, /device:TPU:0, one launch (start us, length us, event | category | flops | bytes accessed | tf_op | source)
XLA Modules:
  0.0 2600.8 jit_solution(11809357465881129413)
XLA Ops:
  11.5 13.7 psum.98
  46.8 43.2 %all-gather.10.cloned.1.call-done = bf16[768,2048]{1,0:T(8,128)(2,1)} async-done(((bf16[768,512]{1,0:T(8,128)(2,1)}), bf16[768,2048]{1,0:T(8,128)(2,1)}) %all-gather.10.cloned.1.call-update) | async-done | bytes 3145744 | tf_op jit(solution)/shard_map/all_gather | solution.py:43
  98.0 25.3 all-gather.12.cloned.1.call-done
  185.1 109.7 %reduce-scatter.12.cloned.1.call-done = f32[768,512]{1,0:T(8,128)} async-done(((f32[768,2048]{1,0:T(8,128)}), f32[768,512]{1,0:T(8,128)}) %reduce-scatter.12.cloned.1.call-update) | async-done | bytes 1572880 | tf_op jit(solution)/shard_map/reduce_scatter | solution.py:47
  311.9 88.8 %all-gather.20.cloned.1.call-done = bf16[2048,2048]{1,0:T(8,128)(2,1)} async-done(((bf16[1024,2048]{1,0:T(8,128)(2,1)}), bf16[2048,2048]{1,0:T(8,128)(2,1)}) %all-gather.20.cloned.1.call-update) | async-done | bytes 8388624 | tf_op jit(solution)/shard_map/all_gather | solution.py:157
  400.7 65.5 %all-gather.16.cloned.1.call-done = bf16[768,2048]{1,0:T(8,128)(2,1)} async-done(((bf16[768,512]{1,0:T(8,128)(2,1)}), bf16[768,2048]{1,0:T(8,128)(2,1)}) %all-gather.16.cloned.1.call-update) | async-done | bytes 3145744 | tf_op jit(solution)/shard_map/all_gather | solution.py:43
  478.0 92.4 %all-gather.18.cloned.1.call-done = bf16[2048,2048]{1,0:T(8,128)(2,1)} async-done(((bf16[1024,2048]{1,0:T(8,128)(2,1)}), bf16[2048,2048]{1,0:T(8,128)(2,1)}) %all-gather.18.cloned.1.call-update) | async-done | bytes 8388624 | tf_op jit(solution)/shard_map/all_gather | solution.py:156
  582.0 53.9 %all-gather.24.cloned.1.call-done = bf16[768,2048]{1,0:T(8,128)(2,1)} async-done(((bf16[768,512]{1,0:T(8,128)(2,1)}), bf16[768,2048]{1,0:T(8,128)(2,1)}) %all-gather.24.cloned.1.call-update) | async-done | bytes 3145744 | tf_op jit(solution)/shard_map/all_gather | solution.py:43
  636.0 104.2 %all-gather.22.cloned.1.call-done = bf16[2048,2048]{1,0:T(8,128)(2,1)} async-done(((bf16[2048,1024]{1,0:T(8,128)(2,1)}), bf16[2048,2048]{1,0:T(8,128)(2,1)}) %all-gather.22.cloned.1.call-update) | async-done | bytes 8388624 | tf_op jit(solution)/shard_map/all_gather | solution.py:158
  740.2 16.7 multiply_convert_fusion
  790.9 99.1 %reduce-scatter.16.cloned.1.call-done = f32[768,512]{1,0:T(8,128)} async-done(((f32[768,2048]{1,0:T(8,128)}), f32[768,512]{1,0:T(8,128)}) %reduce-scatter.16.cloned.1.call-update) | async-done | bytes 1572880 | tf_op jit(solution)/shard_map/reduce_scatter | solution.py:47
  890.0 114.2 %reduce-scatter.14.cloned.1.call-done = f32[768,512]{1,0:T(8,128)} async-done(((f32[768,2048]{1,0:T(8,128)}), f32[768,512]{1,0:T(8,128)}) %reduce-scatter.14.cloned.1.call-update) | async-done | bytes 1572880 | tf_op jit(solution)/shard_map/reduce_scatter | solution.py:47
  1024.5 60.6 %all-gather.26.cloned.1.call-done = bf16[768,2048]{1,0:T(8,128)(2,1)} async-done(((bf16[768,512]{1,0:T(8,128)(2,1)}), bf16[768,2048]{1,0:T(8,128)(2,1)}) %all-gather.26.cloned.1.call-update) | async-done | bytes 3145744 | tf_op jit(solution)/shard_map/all_gather | solution.py:43
  1169.4 37.3 %all-reduce.12 = bf16[2,1024,128]{2,0,1:T(2,128)(2,1)} all-reduce(f32[2,1024,128]{2,0,1:T(2,128)} %convolution_add_fusion.1), channel_id=6, replica_groups=mesh['fsdp'=2,'ctx'=4,'tp'=4] {'ctx'}, use_global_device_ids=true, to_apply=%region_17.19.clone | all-reduce | flops 262144 | bytes 1572864
  1260.6 12.1 fusion.87
  1273.0 12.4 fusion.86
  1287.3 12.2 fusion.88
  1313.0 57.1 %reduce-scatter.20.cloned.1.call-done = f32[1024,512]{1,0:T(8,128)} async-done(((f32[2048,512]{1,0:T(8,128)}), f32[1024,512]{1,0:T(8,128)}) %reduce-scatter.20.cloned.1.call-update) | async-done | bytes 2097168 | tf_op jit(solution)/shard_map/reduce_scatter | solution.py:358
  1370.2 191.4 %reduce-scatter.30.cloned.1.call-done = f32[1024,2048]{1,0:T(8,128)} async-done(((f32[2048,2048]{1,0:T(8,128)}), f32[1024,2048]{1,0:T(8,128)}) %reduce-scatter.30.cloned.1.call-update) | async-done | bytes 8388624 | tf_op jit(solution)/shard_map/reduce_scatter | solution.py:363
  1561.6 191.5 %reduce-scatter.28.cloned.1.call-done = f32[1024,2048]{1,0:T(8,128)} async-done(((f32[2048,2048]{1,0:T(8,128)}), f32[1024,2048]{1,0:T(8,128)}) %reduce-scatter.28.cloned.1.call-update) | async-done | bytes 8388624 | tf_op jit(solution)/shard_map/reduce_scatter | solution.py:362
  1753.1 191.4 %reduce-scatter.32.cloned.1.call-done = f32[2048,1024]{1,0:T(8,128)} async-done(((f32[2048,2048]{1,0:T(8,128)}), f32[2048,1024]{1,0:T(8,128)}) %reduce-scatter.32.cloned.1.call-update) | async-done | bytes 8388624 | tf_op jit(solution)/shard_map/reduce_scatter | solution.py:364
  1948.9 109.3 %reduce-scatter.18.cloned.1.call-done = f32[768,512]{1,0:T(8,128)} async-done(((f32[768,2048]{1,0:T(8,128)}), f32[768,512]{1,0:T(8,128)}) %reduce-scatter.18.cloned.1.call-update) | async-done | bytes 1572880 | tf_op jit(solution)/shard_map/reduce_scatter | solution.py:47
  2076.1 13.0 all-reduce.3
  2089.1 481.0 %all-reduce.11.cloned.1.call-done = (f32[1024,512]{1,0:T(8,128)}, f32[1024,128]{1,0:T(8,128)}, f32[1024,128]{1,0:T(8,128)}, f32[512,1024]{1,0:T(8,128)}, f32[102...) async-done(((f32[1024,512]{1,0:T(8,128)}, f32[1024,128]{1,0:T(8,128)}, f32[1024,128]{1,0:T(8,128)}, f32[512,1024]{1,0:T(8,128)}, f32[1024,2048]{1,0:T(8,128)}, ...) | async-done | bytes 30408720 | tf_op jit(solution)/shard_map/psum | solution.py:366
  (359 shorter events, 388.1 us)
Async XLA Ops:
  7.2 82.8 %all-gather.10.cloned.1.call-start = ((), (), s32[]{:S(2)}) async-start(), calls=%async_computation.11 | async-start | bytes 3932160 | tf_op jit(solution)/shard_map/all_gather | solution.py:43
  25.3 284.3 %copy-start.51 = (f32[768]{0:T(1024)}, f32[768]{0:T(1024)S(1)}, u32[]{:S(2)}) copy-start(f32[768]{0:T(1024)S(1)} %get-tuple-element.24) | copy-start | bytes 9220
  28.1 95.1 %all-gather.12.cloned.1.call-start = ((), (), s32[]{:S(2)}) async-start(), calls=%async_computation.12 | async-start | bytes 3145728 | tf_op jit(solution)/shard_map/all_gather | solution.py:152
  28.9 149.0 %all-gather.14.cloned.1.call-start = ((), (), s32[]{:S(2)}) async-start(), calls=%async_computation.13 | async-start | bytes 3145728 | tf_op jit(solution)/shard_map/all_gather | solution.py:155
  29.6 265.1 %reduce-scatter.12.cloned.1.call-start = ((), (), s32[]{:S(2)}) async-start(), calls=%async_computation.14 | async-start | bytes 7864320 | tf_op jit(solution)/shard_map/reduce_scatter | solution.py:47
  184.4 216.3 %all-gather.20.cloned.1.call-start = ((), (), s32[]{:S(2)}) async-start(), calls=%async_computation.17 | async-start | bytes 12582912 | tf_op jit(solution)/shard_map/all_gather | solution.py:157
  185.0 281.2 %all-gather.16.cloned.1.call-start = ((), (), s32[]{:S(2)}) async-start(), calls=%async_computation.15 | async-start | bytes 3932160 | tf_op jit(solution)/shard_map/all_gather | solution.py:43
  308.8 261.6 %all-gather.18.cloned.1.call-start = ((), (), s32[]{:S(2)}) async-start(), calls=%async_computation.16 | async-start | bytes 12582912 | tf_op jit(solution)/shard_map/all_gather | solution.py:156
  309.5 326.4 %all-gather.24.cloned.1.call-start = ((), (), s32[]{:S(2)}) async-start(), calls=%async_computation.20 | async-start | bytes 3932160 | tf_op jit(solution)/shard_map/all_gather | solution.py:43
  311.1 429.1 %all-gather.22.cloned.1.call-start = ((), (), s32[]{:S(2)}) async-start(), calls=%async_computation.18 | async-start | bytes 12582912 | tf_op jit(solution)/shard_map/all_gather | solution.py:158
  311.8 578.2 %reduce-scatter.16.cloned.1.call-start = ((), (), s32[]{:S(2)}) async-start(), calls=%async_computation.21 | async-start | bytes 7864320 | tf_op jit(solution)/shard_map/reduce_scatter | solution.py:47
  779.1 225.2 %reduce-scatter.14.cloned.1.call-start = ((), (), s32[]{:S(2)}) async-start(), calls=%async_computation.19 | async-start | bytes 7864320 | tf_op jit(solution)/shard_map/reduce_scatter | solution.py:47
  790.9 294.3 %all-gather.26.cloned.1.call-start = ((), (), s32[]{:S(2)}) async-start(), calls=%async_computation.22 | async-start | bytes 3932160 | tf_op jit(solution)/shard_map/all_gather | solution.py:43
  1023.2 194.0 %all-reduce.9.cloned.1.call-start = ((), (), s32[]{:S(2)}) async-start(), calls=%async_computation.31 | async-start | bytes 2097152
  1169.4 139.6 %reduce-scatter.24.cloned.1.call-start = ((), (), s32[]{:S(2)}) async-start(), calls=%async_computation.26 | async-start | bytes 1572864 | tf_op jit(solution)/shard_map/reduce_scatter | solution.py:360
  1213.8 95.3 %reduce-scatter.22.cloned.1.call-start = ((), (), s32[]{:S(2)}) async-start(), calls=%async_computation.25 | async-start | bytes 1572864 | tf_op jit(solution)/shard_map/reduce_scatter | solution.py:359
  1228.0 85.0 %reduce-scatter.26.cloned.1.call-start = ((), (), s32[]{:S(2)}) async-start(), calls=%async_computation.27 | async-start | bytes 6291456 | tf_op jit(solution)/shard_map/reduce_scatter | solution.py:361
  1234.1 136.1 %reduce-scatter.20.cloned.1.call-start = ((), (), s32[]{:S(2)}) async-start(), calls=%async_computation.24 | async-start | bytes 6291456 | tf_op jit(solution)/shard_map/reduce_scatter | solution.py:358
  1258.7 302.9 %reduce-scatter.30.cloned.1.call-start = ((), (), s32[]{:S(2)}) async-start(), calls=%async_computation.29 | async-start | bytes 25165824 | tf_op jit(solution)/shard_map/reduce_scatter | solution.py:363
  1272.7 480.4 %reduce-scatter.28.cloned.1.call-start = ((), (), s32[]{:S(2)}) async-start(), calls=%async_computation.28 | async-start | bytes 25165824 | tf_op jit(solution)/shard_map/reduce_scatter | solution.py:362
  1285.4 659.1 %reduce-scatter.32.cloned.1.call-start = ((), (), s32[]{:S(2)}) async-start(), calls=%async_computation.30 | async-start | bytes 25165824 | tf_op jit(solution)/shard_map/reduce_scatter | solution.py:364
  1299.6 758.6 %reduce-scatter.18.cloned.1.call-start = ((), (), s32[]{:S(2)}) async-start(), calls=%async_computation.23 | async-start | bytes 7864320 | tf_op jit(solution)/shard_map/reduce_scatter | solution.py:47
  1308.9 1261.2 %all-reduce.11.cloned.1.call-start = ((), (), s32[]{:S(2)}) async-start(), calls=%async_computation.32 | async-start | bytes 60817408 | tf_op jit(solution)/shard_map/psum | solution.py:366
  1945.1 126.1 %copy-start.18 = (bf16[2,128,512]{2,1,0:T(8,128)(2,1)S(1)}, bf16[2,128,512]{2,1,0:T(8,128)(2,1)}, u32[]{:S(2)}) copy-start(bf16[2,128,512]{2,1,0:T(8,128)(2,1)} %param.37) | copy-start | bytes 786436
  (74 other events, 1354.4 us)
Sparse Core Ops, SparseCore 0:
  28.3 61.6 all-gather.9
  91.5 31.7 all-gather.11
  124.8 33.0 all-gather.13
  184.5 110.2 reduce-scatter.11
  296.1 104.4 all-gather.19
  402.7 63.4 all-gather.15
  467.7 102.6 all-gather.17
  572.5 63.4 all-gather.23
  637.5 102.6 all-gather.21
  779.2 110.7 reduce-scatter.15
  892.9 111.2 reduce-scatter.13
  1023.3 61.7 all-gather.25
  1169.5 42.5 all-reduce.8
  1214.2 18.5 reduce-scatter.23
  1235.5 20.3 reduce-scatter.21
  1258.6 54.3 reduce-scatter.25
  1315.7 54.3 reduce-scatter.19
  1372.3 189.2 reduce-scatter.29
  1563.9 189.1 reduce-scatter.27
  1755.2 189.1 reduce-scatter.31
  1947.3 110.7 reduce-scatter.17
  2061.4 508.6 all-reduce.10
where the time goes:
time: 2610 us; the launch traced here: 2600 us
  waiting for transfers between devices  2090 us (80%)
  matrix products  229 us (9%)
  blocking collectives  126 us (5%)
  local copies, waits for them, and re-layouts  84.1 us (3%)
  other arithmetic  57.4 us (2%)
    psum x1, waiting for transfers between devices, body(): lax.psum((pieces[0], pieces[1], pieces[2], pieces[3], pieces[4], pieces[5...  481 us
    reduce_scatter x4, waiting for transfers between devices, narrow(): return lax.psum_scatter(partial_sum, 'tp', scatter_dimension=1, tiled=True)  432 us
    all_gather x4, waiting for transfers between devices, widen(): return lax.all_gather(local_part, 'tp', axis=1, tiled=True)  223 us
    reduce_scatter x1, waiting for transfers between devices, body(): lax.psum_scatter(grad_gate, 'fsdp', scatter_dimension=0, tiled=True)  192 us
    reduce_scatter x1, waiting for transfers between devices, body(): lax.psum_scatter(grad_up, 'fsdp', scatter_dimension=0, tiled=True)  191 us
    reduce_scatter x1, waiting for transfers between devices, body(): lax.psum_scatter(grad_down, 'fsdp', scatter_dimension=1, tiled=True)  191 us
    dot_general x21, matrix products, product(): return jnp.dot(left, right, preferred_element_type=jnp.float32)  153 us
    all_gather x1, waiting for transfers between devices, body(): lax.all_gather(w_down, 'fsdp', axis=1, tiled=True)  104 us
  transfers between devices with their start and end apart: 22, of which 18 were waited for; matrix products, arithmetic and copies ran while one was open for 7% of the time, Pallas kernels for 0%

commit v1 on v0

v1 whole, which is shorter than its diff:
```python
import jax
import jax.numpy as jnp
from jax import lax
from jax.sharding import PartitionSpec as P

HEAD_SIZE = 64
CONTINUATION_LEN = 128
EPSILON = 1e-05
ROPE_BASE = 500000.0
BF = jnp.bfloat16
F32 = jnp.float32
EVERY = ("fsdp", "ctx")


def product(left, right):
    return jnp.dot(left, right, preferred_element_type=F32)


def product_nt(left, right):
    return lax.dot_general(left, right, (((1,), (1,)), ((), ())), preferred_element_type=F32)


def product_tn(left, right):
    return lax.dot_general(left, right, (((0,), (0,)), ((), ())), preferred_element_type=F32)


def swap(value, axis, step):
    count = lax.axis_size(axis)
    return lax.ppermute(value, axis, [(i, i ^ step) for i in range(count)])


def pieces_of(value, axis="tp"):
    return [value] + [swap(value, axis, step) for step in range(1, lax.axis_size(axis))]


def all_sum(value, axis="tp"):
    parts = pieces_of(value, axis)
    total = parts[0]
    for part in parts[1:]:
        total = total + part
    return total


def lay_out(parts, width):
    me = lax.axis_index("tp")
    rows = parts[0].shape[0]
    whole = jnp.zeros((rows, width * len(parts)), parts[0].dtype)
    for step, part in enumerate(parts):
        whole = lax.dynamic_update_slice(whole, part, (0, (me ^ step) * width))
    return whole


def scatter_sum(make_block):
    me = lax.axis_index("tp")
    total = make_block(me)
    for step in range(1, lax.axis_size("tp")):
        total = total + swap(make_block(me ^ step).astype(BF), "tp", step).astype(F32)
    return total


def columns(matrix, block, width):
    return lax.dynamic_slice(matrix, (0, block * width), (matrix.shape[0], width))


def rows_of(matrix, block, width):
    return lax.dynamic_slice(matrix, (block * width, 0), (width, matrix.shape[1]))


def rope_tables(positions):
    half = HEAD_SIZE // 2
    frequency = ROPE_BASE ** (-jnp.arange(half, dtype=F32) * 2.0 / HEAD_SIZE)
    angles = positions.astype(F32)[:, None] * frequency[None, :]
    return jnp.cos(angles), jnp.sin(angles)


def rotate(values, tables, direction):
    half = HEAD_SIZE // 2
    cosine = tables[0][:, None, :]
    sine = direction * tables[1][:, None, :]
    shaped = values.reshape(values.shape[0], -1, HEAD_SIZE)
    first, second = shaped[..., :half], shaped[..., half:]
    turned = jnp.concatenate([first * cosine - second * sine, second * cosine + first * sine], -1)
    return turned.reshape(values.shape)


def attend_scores(query_split, key_split, allowed):
    scores = (
        jnp.einsum("gqkrd,gskd->gkrqs", query_split, key_split, preferred_element_type=F32) * 0.125
    )
    return jnp.where(allowed, scores, -1e30)


def attend_forward(query_split, key_split, value_split, allowed):
    scores = attend_scores(query_split, key_split, allowed)
    row_max = jnp.max(scores, axis=-1, keepdims=True)
    exponent = jnp.exp(scores - row_max)
    total = jnp.sum(exponent, axis=-1, keepdims=True)
    prob_low = (exponent / total).astype(BF)
    result = jnp.einsum(
        "gkrqs,gskd->gqkrd", prob_low, value_split, preferred_element_type=F32
    ).astype(BF)
    return result.reshape(result.shape[0] * result.shape[1], -1), row_max + jnp.log(total)


def attend_backward(query_split, key_split, value_split, allowed, log_total, out_grad):
    grad_split = out_grad.reshape(query_split.shape)
    scores = attend_scores(query_split, key_split, allowed)
    prob_full = jnp.exp(scores - log_total)
    prob_low = prob_full.astype(BF)
    value_grad = jnp.einsum("gkrqs,gqkrd->gskd", prob_low, grad_split, preferred_element_type=F32)
    prob_grad = jnp.einsum("gqkrd,gskd->gkrqs", grad_split, value_split, preferred_element_type=F32)
    score_grad = (
        prob_full * (prob_grad - jnp.sum(prob_grad * prob_full, axis=-1, keepdims=True))
    ).astype(BF)
    query_grad = (
        jnp.einsum("gkrqs,gskd->gqkrd", score_grad, key_split, preferred_element_type=F32) * 0.125
    )
    key_grad = (
        jnp.einsum("gkrqs,gqkrd->gskd", score_grad, query_split, preferred_element_type=F32) * 0.125
    )
    batch = query_split.shape[0]
    return (
        query_grad.reshape(batch * query_split.shape[1], -1),
        key_grad.reshape(batch, key_split.shape[1], -1),
        value_grad.reshape(batch, key_split.shape[1], -1),
    )


def body(
    prompt_in,
    cont_in,
    prompt_mask,
    cont_mask,
    cont_prompt,
    cont_start,
    gain_attn,
    gain_ffn,
    router,
    w_query,
    key_projection,
    w_value,
    w_out,
    w_gate,
    w_up,
    w_down,
    prompt_cot,
    cont_cot,
):
    groups, prompt_rows, width = prompt_in.shape
    conts = cont_in.shape[0]
    tp_size = lax.axis_size("tp")
    ctx_size = lax.axis_size("ctx")
    model_width = width * tp_size
    me_tp = lax.axis_index("tp")
    me_ctx = lax.axis_index("ctx")
    query_width = w_query.shape[1]
    key_width = key_projection.shape[1]
    query_heads = query_width // HEAD_SIZE
    key_heads = key_width // HEAD_SIZE
    ratio = query_heads // key_heads
    tokens_in = [prompt_in.reshape(-1, width), cont_in.reshape(-1, width)]
    cots = [prompt_cot.reshape(-1, width), cont_cot.reshape(-1, width)]
    masks = [prompt_mask.reshape(-1).astype(F32), cont_mask.reshape(-1).astype(F32)]
    prompt_place = me_ctx * prompt_rows + jnp.arange(prompt_rows, dtype=jnp.int32)
    cont_place = (
        cont_start[:, None] + jnp.arange(CONTINUATION_LEN, dtype=jnp.int32)[None, :]
    ).reshape(-1)
    tables = [rope_tables(jnp.tile(prompt_place, groups)), rope_tables(cont_place)]
    local_prompt = cont_prompt - lax.axis_index("fsdp") * groups

    def quarter_rows(weight):
        rows = weight.shape[0] // ctx_size
        return lax.dynamic_slice(weight, (me_ctx * rows, 0), (rows, weight.shape[1]))

    def quarter_columns(weight):
        count = weight.shape[1] // ctx_size
        return lax.dynamic_slice(weight, (0, me_ctx * count), (weight.shape[0], count))

    full_qkv = lax.all_gather(
        jnp.concatenate(
            [quarter_rows(w_query), quarter_rows(key_projection), quarter_rows(w_value)], axis=1
        ),
        EVERY,
        axis=0,
        tiled=True,
    )
    full_out = lax.all_gather(quarter_columns(w_out), EVERY, axis=1, tiled=True)
    full_gate = lax.all_gather(quarter_rows(w_gate), EVERY, axis=0, tiled=True)
    full_up = lax.all_gather(quarter_rows(w_up), EVERY, axis=0, tiled=True)
    full_down = lax.all_gather(quarter_columns(w_down), EVERY, axis=1, tiled=True)

    params = [p.astype(F32) for p in pieces_of(jnp.stack([gain_attn, gain_ffn, router]))]
    gains_attn = [p[0] for p in params]
    gains_ffn = [p[1] for p in params]
    routers = [p[2] for p in params]
    x_parts = [pieces_of(t) for t in tokens_in]
    cot_parts = [pieces_of(t) for t in cots]
    streams = range(2)

    scale_attn, gate_router, mixing, xn1 = [], [], [], []
    for i in streams:
        wide = [p.astype(F32) for p in x_parts[i]]
        squares = sum(jnp.sum(p * p, axis=1) for p in wide)
        logits = sum(jnp.sum(p * r, axis=1) for p, r in zip(wide, routers))
        scale = lax.rsqrt(squares / model_width + EPSILON)
        gate = jax.nn.sigmoid(logits)
        scale_attn.append(scale)
        gate_router.append(gate)
        mixing.append(masks[i] * gate)
        xn1.append(
            lay_out([(p * scale[:, None] * g).astype(BF) for p, g in zip(wide, gains_attn)], width)
        )
    qkv = [product(t, full_qkv) for t in xn1]
    query = [rotate(t[:, :query_width], tb, 1.0).astype(BF) for t, tb in zip(qkv, tables)]
    key = [
        rotate(t[:, query_width : query_width + key_width], tb, 1.0).astype(BF)
        for t, tb in zip(qkv, tables)
    ]
    value = [t[:, query_width + key_width :].astype(BF) for t in qkv]

    own_kv = jnp.concatenate([key[0], value[0]], axis=1).reshape(groups, prompt_rows, 2 * key_width)
    prompt_kv = jnp.zeros((groups, prompt_rows * ctx_size, 2 * key_width), BF)
    for step, part in enumerate(pieces_of(own_kv, "ctx")):
        prompt_kv = lax.dynamic_update_slice(prompt_kv, part, (0, (me_ctx ^ step) * prompt_rows, 0))
    length = prompt_rows * ctx_size
    prompt_k, prompt_v = prompt_kv[..., :key_width], prompt_kv[..., key_width:]

    def heads(t, batch):
        return t.reshape(batch, -1, key_heads, HEAD_SIZE)

    all_query = [
        query[0].reshape(groups, prompt_rows, key_heads, ratio, HEAD_SIZE),
        query[1].reshape(conts, CONTINUATION_LEN, key_heads, ratio, HEAD_SIZE),
    ]
    all_key = [
        heads(prompt_k, groups),
        jnp.concatenate(
            [
                heads(jnp.take(prompt_k, local_prompt, axis=0), conts),
                heads(key[1], conts),
            ],
            axis=1,
        ),
    ]
    all_value = [
        heads(prompt_v, groups),
        jnp.concatenate(
            [
                heads(jnp.take(prompt_v, local_prompt, axis=0), conts),
                heads(value[1], conts),
            ],
            axis=1,
        ),
    ]
    allowed = [
        jnp.arange(length, dtype=jnp.int32)[None, :] <= prompt_place[:, None],
        jnp.concatenate(
            [
                jnp.ones((CONTINUATION_LEN, length), dtype=bool),
                jnp.arange(CONTINUATION_LEN)[None, :] <= jnp.arange(CONTINUATION_LEN)[:, None],
            ],
            axis=1,
        ),
    ]
    attended, log_total = [], []
    for i in streams:
        result, total = attend_forward(all_query[i], all_key[i], all_value[i], allowed[i])
        attended.append(result)
        log_total.append(total)

    branch_attn = [
        scatter_sum(lambda b, t=t: product(t, columns(full_out, b, width))) for t in attended
    ]
    a_parts = [pieces_of(a.astype(BF)) for a in branch_attn]
    scale_ffn, xn2, hidden_parts = [], [], []
    for i in streams:
        hid = [x.astype(F32) + a.astype(F32) for x, a in zip(x_parts[i], a_parts[i])]
        scale = lax.rsqrt(sum(jnp.sum(h * h, axis=1) for h in hid) / model_width + EPSILON)
        scale_ffn.append(scale)
        hidden_parts.append(hid)
        xn2.append(
            lay_out([(h * scale[:, None] * g).astype(BF) for h, g in zip(hid, gains_ffn)], width)
        )
    grad_parts = [[c.astype(F32) * mixing[i][:, None] for c in cot_parts[i]] for i in streams]
    ffn_grad = [lay_out([g.astype(BF) for g in grad_parts[i]], width) for i in streams]

    inner, gate_grad, up_grad = [], [], []
    for i in streams:
        g = product(xn2[i], full_gate)
        u = product(xn2[i], full_up)
        s = jax.nn.sigmoid(g)
        inner.append((g * s * u).astype(BF))
        dz = product_nt(ffn_grad[i], full_down)
        gate_grad.append((dz * u * s * (1.0 + g * (1.0 - s))).astype(BF))
        up_grad.append((dz * g * s).astype(BF))

    normed_grad = [
        scatter_sum(
            lambda b, i=i: product_nt(gate_grad[i], rows_of(full_gate, b, width))
            + product_nt(up_grad[i], rows_of(full_up, b, width))
        )
        for i in streams
    ]
    n_parts = [pieces_of(n.astype(BF)) for n in normed_grad]
    back_ffn, dab, gain_ffn_sum = [], [], 0.0
    for i in streams:
        wide = [n.astype(F32) for n in n_parts[i]]
        hid = hidden_parts[i]
        total = sum(jnp.sum(h * g * n, axis=1) for h, g, n in zip(hid, gains_ffn, wide))
        scale = scale_ffn[i]
        factor = (scale**3 * total / model_width)[:, None]
        parts = [
            (d + scale[:, None] * g * n - h * factor).astype(BF)
            for d, g, n, h in zip(grad_parts[i], gains_ffn, wide, hid)
        ]
        dab.append(lay_out(parts, width))
        hid_own = tokens_in[i].astype(F32) + branch_attn[i]
        back_ffn.append(scale[:, None] * gains_ffn[0] * normed_grad[i] - hid_own * factor)
        gain_ffn_sum = gain_ffn_sum + jnp.sum(hid_own * scale[:, None] * normed_grad[i], axis=0)

    branch_ffn = [
        scatter_sum(lambda b, t=t: product(t, columns(full_down, b, width))) for t in inner
    ]
    both = lambda pair: jnp.concatenate(pair, axis=0)

    def reduce_rows(partial_grad):
        part = lax.psum_scatter(partial_grad.astype(BF), EVERY, scatter_dimension=0, tiled=True)
        return lax.all_gather(part, "ctx", axis=0, tiled=True).astype(F32)

    def reduce_columns(partial_grad):
        part = lax.psum_scatter(partial_grad.astype(BF), EVERY, scatter_dimension=1, tiled=True)
        return lax.all_gather(part, "ctx", axis=1, tiled=True).astype(F32)

    grad_down = reduce_columns(product_tn(both(inner), both(ffn_grad)))
    xn2_all = both(xn2)
    grad_gate = reduce_rows(product_tn(xn2_all, both(gate_grad)))
    grad_up = reduce_rows(product_tn(xn2_all, both(up_grad)))

    do = [product_nt(t, full_out).astype(BF) for t in dab]
    grad_out = reduce_columns(product_tn(both(attended), both(dab)))
    back = [
        attend_backward(all_query[i], all_key[i], all_value[i], allowed[i], log_total[i], do[i])
        for i in streams
    ]
    one_hot = (local_prompt[:, None] == jnp.arange(groups, dtype=jnp.int32)[None, :]).astype(F32)
    kv_grad = jnp.concatenate(
        [
            back[0][j]
            + jnp.einsum(
                "cg,csx->gsx",
                one_hot,
                back[1][j][:, :length],
                precision=lax.Precision.HIGHEST,
            )
            for j in (1, 2)
        ],
        axis=2,
    )

    def ctx_block(step):
        return lax.dynamic_slice(
            kv_grad, (0, (me_ctx ^ step) * prompt_rows, 0), (groups, prompt_rows, 2 * key_width)
        )

    kv_mine = ctx_block(0)
    for step in range(1, ctx_size):
        kv_mine = kv_mine + swap(ctx_block(step).astype(BF), "ctx", step).astype(F32)
    dk = [
        kv_mine[..., :key_width].reshape(-1, key_width),
        back[1][1][:, length:].reshape(-1, key_width),
    ]
    dv = [
        kv_mine[..., key_width:].reshape(-1, key_width),
        back[1][2][:, length:].reshape(-1, key_width),
    ]
    dq = [back[0][0], back[1][0]]
    dqkv, total_attn = [], []
    for i in streams:
        dqkv.append(
            jnp.concatenate(
                [
                    rotate(dq[i], tables[i], -1.0).astype(BF),
                    rotate(dk[i], tables[i], -1.0).astype(BF),
                    dv[i].astype(BF),
                ],
                axis=1,
            )
        )
        total_attn.append(
            all_sum(
                jnp.sum(dq[i] * query[i].astype(F32), axis=1)
                + jnp.sum(dk[i] * key[i].astype(F32), axis=1)
                + jnp.sum(dv[i] * value[i].astype(F32), axis=1)
            )
        )
    grad_qkv = reduce_rows(product_tn(both(xn1), both(dqkv)))
    normed_attn_grad = [
        scatter_sum(lambda b, t=t: product_nt(t, rows_of(full_qkv, b, width))) for t in dqkv
    ]

    gain_attn_sum, router_sum = 0.0, 0.0
    outs, token_grads = [], []
    for i in streams:
        x = tokens_in[i].astype(F32)
        dy = cots[i].astype(F32)
        branch = branch_attn[i] + branch_ffn[i]
        outs.append((x + mixing[i][:, None] * branch).astype(BF))
        dl = (1.0 - gate_router[i]) * all_sum(jnp.sum(grad_parts[i][0] * branch, axis=1))
        router_sum = router_sum + jnp.sum(x * dl[:, None], axis=0)
        scale = scale_attn[i]
        n = normed_attn_grad[i]
        gain_attn_sum = gain_attn_sum + jnp.sum(x * scale[:, None] * n, axis=0)
        n1 = (
            scale[:, None] * gains_attn[0] * n
            - x * (scale**2 * total_attn[i] / model_width)[:, None]
        )
        token_grads.append(dy + dl[:, None] * routers[0] + back_ffn[i] + n1)
    small = lax.psum((gain_attn_sum, gain_ffn_sum, router_sum), EVERY)
    return (
        outs[0].reshape(prompt_in.shape),
        outs[1].reshape(cont_in.shape),
        token_grads[0].reshape(prompt_in.shape),
        token_grads[1].reshape(cont_in.shape),
        small[0],
        small[1],
        small[2],
        grad_qkv[:, :query_width],
        grad_qkv[:, query_width : query_width + key_width],
        grad_qkv[:, query_width + key_width :],
        grad_out,
        grad_gate,
        grad_up,
        grad_down,
    )


def solution(mesh):
    placed = (
        P("fsdp", "ctx", "tp"),
        P(("fsdp", "ctx"), None, "tp"),
        P("fsdp", "ctx"),
        P(("fsdp", "ctx"), None),
        P(("fsdp", "ctx")),
        P(("fsdp", "ctx")),
        P("tp"),
        P("tp"),
        P("tp"),
        P("fsdp", "tp"),
        P("fsdp", "tp"),
        P("fsdp", "tp"),
        P("tp", "fsdp"),
        P("fsdp", "tp"),
        P("fsdp", "tp"),
        P("tp", "fsdp"),
        P("fsdp", "ctx", "tp"),
        P(("fsdp", "ctx"), None, "tp"),
    )
    return jax.shard_map(
        body,
        mesh=mesh,
        in_specs=placed,
        out_specs=(
            P("fsdp", "ctx", "tp"),
            P(("fsdp", "ctx"), None, "tp"),
            P("fsdp", "ctx", "tp"),
            P(("fsdp", "ctx"), None, "tp"),
            P("tp"),
            P("tp"),
            P("tp"),
            P("fsdp", "tp"),
            P("fsdp", "tp"),
            P("fsdp", "tp"),
            P("tp", "fsdp"),
            P("fsdp", "tp"),
            P("fsdp", "tp"),
            P("tp", "fsdp"),
        ),
        check_vma=False,
    )
```

time: 2610 us -> 1240 us (0.48)
  waiting for transfers between devices: 2090 us -> 507 us
  starting transfers between devices: 1.36 us -> 200 us
  blocking collectives: 126 us -> 13 us
  other arithmetic: 57.4 us -> 125 us
  local copies, waits for them, and re-layouts: 84.1 us -> 119 us
    reduce_scatter x11 -> x5, waiting for transfers between devices: 1070 us -> 237 us  [the longest x3 161 us: reduce_rows(): lax.psum_scatter(partial_grad.astype(BF), EVERY, scatter_dimension=0, til...]
    all_gather x9 -> x10, waiting for transfers between devices: 534 us -> 20.5 us  [the longest x3 20.4 us: reduce_rows(): return lax.all_gather(part, 'ctx', axis=0, tiled=True).astype(F32)]
    psum x1 -> x0, waiting for transfers between devices: 481 us -> none  [body(): lax.psum((pieces[0], pieces[1], pieces[2], pieces[3], pieces[4], pieces[5...]
    ppermute x0 -> x69, waiting for transfers between devices: none -> 249 us  [swap(): return lax.ppermute(value, axis, [(i, i ^ step) for i in range(count)])]
    ppermute x0 -> x69, starting transfers between devices: none -> 199 us  [swap(): return lax.ppermute(value, axis, [(i, i ^ step) for i in range(count)])]
    psum x5 -> x1, blocking collectives: 59.8 us -> 13 us  [body(): small = lax.psum((gain_attn_sum, gain_ffn_sum, router_sum), EVERY)]
    unnamed x1 -> x0, blocking collectives: 37.3 us -> none
    all_gather x4 -> x0, blocking collectives: 28.8 us -> none  [the longest x1 7.28 us: body(): lax.all_gather(key_rows[:prompt_tokens].reshape(group_number, prompt_rows...]
  transfers between devices with their start and end apart: 22 -> 84, of which waited for: 18 -> 29; matrix products, arithmetic and copies ran while one was open for 7% -> 34% of each run, Pallas kernels for 0% -> 0%
where the time goes in v1:
time: 1240 us; the launch traced here: 1230 us
  waiting for transfers between devices  507 us (41%)
  matrix products  247 us (20%)
  starting transfers between devices  200 us (16%)
  other arithmetic  125 us (10%)
  local copies, waits for them, and re-layouts  119 us (10%)
  between operations  17 us (1%)
  blocking collectives  13 us (1%)
    ppermute x69, waiting for transfers between devices, swap(): return lax.ppermute(value, axis, [(i, i ^ step) for i in range(count)])  249 us
    ppermute x69, starting transfers between devices, swap(): return lax.ppermute(value, axis, [(i, i ^ step) for i in range(count)])  199 us
    reduce_scatter x3, waiting for transfers between devices, reduce_rows(): lax.psum_scatter(partial_grad.astype(BF), EVERY, scatter_dimension=0, til...  161 us
    dot_general x22, matrix products, product(): return jnp.dot(left, right, preferred_element_type=F32)  81 us
    reduce_scatter x2, waiting for transfers between devices, reduce_columns(): lax.psum_scatter(partial_grad.astype(BF), EVERY, scatter_dimension=1, til...  75.3 us
    dot_general x28, matrix products, product_nt(): lax.dot_general(left, right, (((1,), (1,)), ((), ())), preferred_element_...  57.1 us
    dot_general x5, matrix products, product_tn(): lax.dot_general(left, right, (((0,), (0,)), ((), ())), preferred_element_...  42.5 us
  transfers between devices with their start and end apart: 84, of which 29 were waited for; matrix products, arithmetic and copies ran while one was open for 34% of the time, Pallas kernels for 0%

profile of v1, /device:TPU:0, one launch (start us, length us, event | category | flops | bytes accessed | tf_op | source)
XLA Modules:
  0.0 1227.7 jit_solution(8268598804649623330)
XLA Ops:
  40.5 11.1 collective-permute-done.20
  51.6 14.8 %collective-permute-start.18 = (bf16[256,512]{1,0:T(8,128)(2,1)S(1)}, bf16[256,512]{1,0:T(8,128)(2,1)S(1)}, u32[]{:S(2)}, u32[]{:S(2)}) collective-permute-start(bf16[256,512]{1,0:T(8,128)(2,1)S(1)} %bitcast.311), channel_id=1, source_target_pairs={{0,1},{1,0},{2,3},{3,2},{4,5},{5,4},{6,7},{7,6},{8,9},{9,8},{10,11... | collective-permute-start | bytes 786440 | tf_op jit(solution)/shard_map/ppermute | solution.py:29
  73.0 14.0 %collective-permute-done.18 = bf16[256,512]{1,0:T(8,128)(2,1)S(1)} collective-permute-done((bf16[256,512]{1,0:T(8,128)(2,1)S(1)}, bf16[256,512]{1,0:T(8,128)(2,1)S(1)}, u32[]{:S(2)}, u32[]{:S(2)}) %collective-permute-start.18) | collective-permute-done | bytes 262176 | tf_op jit(solution)/shard_map/ppermute | solution.py:29
  94.8 18.5 %collective-permute-done.4 = bf16[512,512]{1,0:T(8,128)(2,1)S(1)} collective-permute-done((bf16[512,512]{1,0:T(8,128)(2,1)S(1)}, bf16[512,512]{1,0:T(8,128)(2,1)S(1)}, u32[]{:S(2)}, u32[]{:S(2)}) %collective-permute-start.4) | collective-permute-done | bytes 524320 | tf_op jit(solution)/shard_map/ppermute | solution.py:29
  113.2 39.1 %collective-permute-start.33 = (bf16[512,512]{1,0:T(8,128)(2,1)}, bf16[512,512]{1,0:T(8,128)(2,1)S(1)}, u32[]{:S(2)}, u32[]{:S(2)}) collective-permute-start(bf16[512,512]{1,0:T(8,128)(2,1)} %bitcast.42), channel_id=1, source_target_pairs={{0,1},{1,0},{2,3},{3,2},{4,5},{5,4},{6,7},{7,6},{8,9},{9,8},{10,11... | collective-permute-start | bytes 1572872 | tf_op jit(solution)/shard_map/ppermute | solution.py:29
  309.9 12.0 collective-permute-done.9
  321.9 26.9 %collective-permute-done.10 = bf16[512,512]{1,0:T(8,128)(2,1)S(1)} collective-permute-done((bf16[512,512]{1,0:T(8,128)(2,1)S(1)}, bf16[512,512]{1,0:T(8,128)(2,1)S(1)}, u32[]{:S(2)}, u32[]{:S(2)}) %collective-permute-start.10) | collective-permute-done | bytes 524320 | tf_op jit(solution)/shard_map/ppermute | solution.py:29
  352.9 22.1 %collective-permute-start.13 = (bf16[512,512]{1,0:T(8,128)(2,1)S(1)}, bf16[512,512]{1,0:T(8,128)(2,1)S(1)}, u32[]{:S(2)}, u32[]{:S(2)}) collective-permute-start(bf16[512,512]{1,0:T(8,128)(2,1)S(1)} %get-tuple-element.51), channel_id=1, source_target_pairs={{0,2},{1,3},{2,0},{3,1},{4,6},{5,7},{6,4},{7,5},{8,10},{9,11},{10,... | collective-permute-start | bytes 1572872 | tf_op jit(solution)/shard_map/ppermute | solution.py:29
  375.0 11.7 collective-permute-start.12
  395.1 19.8 %collective-permute-done.13 = bf16[512,512]{1,0:T(8,128)(2,1)S(1)} collective-permute-done((bf16[512,512]{1,0:T(8,128)(2,1)S(1)}, bf16[512,512]{1,0:T(8,128)(2,1)S(1)}, u32[]{:S(2)}, u32[]{:S(2)}) %collective-permute-start.13) | collective-permute-done | bytes 524320 | tf_op jit(solution)/shard_map/ppermute | solution.py:29
  484.8 11.4 multiply_convert_fusion.1
  534.1 49.9 %collective-permute-done.49 = bf16[256,512]{1,0:T(8,128)(2,1)S(1)} collective-permute-done((bf16[256,512]{1,0:T(8,128)(2,1)S(1)}, bf16[256,512]{1,0:T(8,128)(2,1)S(1)}, u32[]{:S(2)}, u32[]{:S(2)}) %collective-permute-start.49) | collective-permute-done | bytes 262176 | tf_op jit(solution)/shard_map/ppermute | solution.py:29
  595.1 13.1 %collective-permute-start.36 = (bf16[512,512]{1,0:T(8,128)(2,1)}, bf16[512,512]{1,0:T(8,128)(2,1)}, u32[]{:S(2)}, u32[]{:S(2)}) collective-permute-start(bf16[512,512]{1,0:T(8,128)(2,1)} %fusion.121), channel_id=1, source_target_pairs={{0,1},{1,0},{2,3},{3,2},{4,5},{5,4},{6,7},{7,6},{8,9},{9,8},{10,11... | collective-permute-start | bytes 1572872 | tf_op jit(solution)/shard_map/ppermute | solution.py:29
  718.3 11.4 fusion
  734.2 11.7 fusion.2
  791.7 10.9 convolution_convert_fusion
  804.3 11.1 convolution_convert_fusion.1
  816.6 10.9 convolution_convert_fusion.2
  839.2 75.3 %reduce-scatter.14.cloned.1.call-done = bf16[2048,256]{1,0:T(8,128)(2,1)} async-done(((bf16[2048,2048]{1,0:T(8,128)(2,1)}), bf16[2048,256]{1,0:T(8,128)(2,1)}) %reduce-scatter.14.cloned.1.call-update) | async-done | bytes 1048592 | tf_op jit(solution)/shard_map/reduce_scatter | solution.py:331
  914.6 75.5 %reduce-scatter.12.cloned.1.call-done = bf16[256,2048]{1,0:T(8,128)(2,1)} async-done(((bf16[2048,2048]{1,0:T(8,128)(2,1)}), bf16[256,2048]{1,0:T(8,128)(2,1)}) %reduce-scatter.12.cloned.1.call-update) | async-done | bytes 1048592 | tf_op jit(solution)/shard_map/reduce_scatter | solution.py:327
  990.4 75.1 %reduce-scatter.10.cloned.1.call-done = bf16[256,2048]{1,0:T(8,128)(2,1)} async-done(((bf16[2048,2048]{1,0:T(8,128)(2,1)}), bf16[256,2048]{1,0:T(8,128)(2,1)}) %reduce-scatter.10.cloned.1.call-update) | async-done | bytes 1048592 | tf_op jit(solution)/shard_map/reduce_scatter | solution.py:327
  1129.6 26.8 %collective-permute-done.55 = bf16[512,512]{1,0:T(8,128)(2,1)S(1)} collective-permute-done((bf16[512,512]{1,0:T(8,128)(2,1)S(1)}, bf16[512,512]{1,0:T(8,128)(2,1)S(1)}, u32[]{:S(2)}, u32[]{:S(2)}) %collective-permute-start.55) | collective-permute-done | bytes 524320 | tf_op jit(solution)/shard_map/ppermute | solution.py:29
  1160.0 13.0 %all-reduce.1 = (f32[512]{0:T(512)}, f32[512]{0:T(512)}, f32[512]{0:T(512)}) all-reduce(f32[512]{0:T(512)S(1)} %add.839, f32[512]{0:T(512)S(1)} %add.840, f32[512]{0:T(512)S(1)} %add.841), channel_id=1, replica_groups=mesh['fsdp'=2,'ctx'=4,'tp'=4] {'fsdp','ctx'}, use_global_device_ids=true, to_apply=%region_48.50 | all-reduce | flops 1536 | bytes 12288 | tf_op jit(solution)/shard_map/psum | solution.py:418
  1193.6 20.4 %all-gather.25.cloned.1.call-done = bf16[1024,2048]{1,0:T(8,128)(2,1)} async-done(((bf16[256,2048]{1,0:T(8,128)(2,1)}), bf16[1024,2048]{1,0:T(8,128)(2,1)}) %all-gather.25.cloned.1.call-update) | async-done | bytes 4194320 | tf_op jit(solution)/shard_map/all_gather | solution.py:328
  (789 shorter events, 604.2 us)
Async XLA Ops:
  7.2 172.1 %all-gather.11.cloned.1.call-start = ((), (), s32[]{:S(2)}) async-start(), calls=%async_computation.5 | async-start | bytes 3538944 | tf_op jit(solution)/shard_map/all_gather | solution.py:179
  10.1 252.9 %all-gather.13.cloned.1.call-start = ((), (), s32[]{:S(2)}) async-start(), calls=%async_computation.6 | async-start | bytes 2359296 | tf_op jit(solution)/shard_map/all_gather | solution.py:187
  11.9 409.1 %all-gather.19.cloned.1.call-start = ((), (), s32[]{:S(2)}) async-start(), calls=%async_computation.9 | async-start | bytes 9437184 | tf_op jit(solution)/shard_map/all_gather | solution.py:190
  14.4 414.1 %all-gather.17.cloned.1.call-start = ((), (), s32[]{:S(2)}) async-start(), calls=%async_computation.8 | async-start | bytes 9437184 | tf_op jit(solution)/shard_map/all_gather | solution.py:189
  16.8 419.0 %all-gather.15.cloned.1.call-start = ((), (), s32[]{:S(2)}) async-start(), calls=%async_computation.7 | async-start | bytes 9437184 | tf_op jit(solution)/shard_map/all_gather | solution.py:188
  28.8 798.8 %reduce-scatter.8.cloned.1.call-start = ((), (), s32[]{:S(2)}) async-start(), calls=%async_computation.12 | async-start | bytes 2359296 | tf_op jit(solution)/shard_map/reduce_scatter | solution.py:331
  70.6 107.0 %collective-permute-start.35 = (bf16[512,512]{1,0:T(8,128)(2,1)}, bf16[512,512]{1,0:T(8,128)(2,1)S(1)}, u32[]{:S(2)}, u32[]{:S(2)}) collective-permute-start(bf16[512,512]{1,0:T(8,128)(2,1)} %bitcast.42), channel_id=1, source_target_pairs={{0,3},{1,2},{2,1},{3,0},{4,7},{5,6},{6,5},{7,4},{8,11},{9,10},{10,... | collective-permute-start | bytes 1572872 | tf_op jit(solution)/shard_map/ppermute | solution.py:29
  87.0 87.6 %collective-permute-start.34 = (bf16[512,512]{1,0:T(8,128)(2,1)}, bf16[512,512]{1,0:T(8,128)(2,1)S(1)}, u32[]{:S(2)}, u32[]{:S(2)}) collective-permute-start(bf16[512,512]{1,0:T(8,128)(2,1)} %bitcast.42), channel_id=1, source_target_pairs={{0,2},{1,3},{2,0},{3,1},{4,6},{5,7},{6,4},{7,5},{8,10},{9,11},{10,... | collective-permute-start | bytes 1572872 | tf_op jit(solution)/shard_map/ppermute | solution.py:29
  309.9 83.9 %collective-permute-start.25 = (bf16[256,512]{1,0:T(8,128)(2,1)S(1)}, bf16[256,512]{1,0:T(8,128)(2,1)S(1)}, u32[]{:S(2)}, u32[]{:S(2)}) collective-permute-start(bf16[256,512]{1,0:T(8,128)(2,1)S(1)} %get-tuple-element.45), channel_id=1, source_target_pairs={{0,2},{1,3},{2,0},{3,1},{4,6},{5,7},{6,4},{7,5},{8,10},{9,11},{10,... | collective-permute-start | bytes 786440 | tf_op jit(solution)/shard_map/ppermute | solution.py:29
  321.9 72.0 %collective-permute-start.24 = (bf16[256,512]{1,0:T(8,128)(2,1)S(1)}, bf16[256,512]{1,0:T(8,128)(2,1)S(1)}, u32[]{:S(2)}, u32[]{:S(2)}) collective-permute-start(bf16[256,512]{1,0:T(8,128)(2,1)S(1)} %get-tuple-element.45), channel_id=1, source_target_pairs={{0,1},{1,0},{2,3},{3,2},{4,5},{5,4},{6,7},{7,6},{8,9},{9,8},{10,11... | collective-permute-start | bytes 786440 | tf_op jit(solution)/shard_map/ppermute | solution.py:29
  448.5 72.4 %collective-permute-start.27 = (bf16[256,512]{1,0:T(8,128)(2,1)}, bf16[256,512]{1,0:T(8,128)(2,1)S(1)}, u32[]{:S(2)}, u32[]{:S(2)}) collective-permute-start(bf16[256,512]{1,0:T(8,128)(2,1)} %fusion.151), channel_id=1, source_target_pairs={{0,1},{1,0},{2,3},{3,2},{4,5},{5,4},{6,7},{7,6},{8,9},{9,8},{10,11... | collective-permute-start | bytes 786440 | tf_op jit(solution)/shard_map/ppermute | solution.py:29
  451.6 70.8 %collective-permute-start.28 = (bf16[256,512]{1,0:T(8,128)(2,1)}, bf16[256,512]{1,0:T(8,128)(2,1)S(1)}, u32[]{:S(2)}, u32[]{:S(2)}) collective-permute-start(bf16[256,512]{1,0:T(8,128)(2,1)} %fusion.154), channel_id=1, source_target_pairs={{0,2},{1,3},{2,0},{3,1},{4,6},{5,7},{6,4},{7,5},{8,10},{9,11},{10,... | collective-permute-start | bytes 786440 | tf_op jit(solution)/shard_map/ppermute | solution.py:29
  517.0 130.8 %collective-permute-start.15 = (bf16[512,512]{1,0:T(8,128)(2,1)}, bf16[512,512]{1,0:T(8,128)(2,1)}, u32[]{:S(2)}, u32[]{:S(2)}) collective-permute-start(bf16[512,512]{1,0:T(8,128)(2,1)} %fusion.106), channel_id=1, source_target_pairs={{0,1},{1,0},{2,3},{3,2},{4,5},{5,4},{6,7},{7,6},{8,9},{9,8},{10,11... | collective-permute-start | bytes 1572872 | tf_op jit(solution)/shard_map/ppermute | solution.py:29
  517.0 130.8 %collective-permute-start.16 = (bf16[512,512]{1,0:T(8,128)(2,1)}, bf16[512,512]{1,0:T(8,128)(2,1)}, u32[]{:S(2)}, u32[]{:S(2)}) collective-permute-start(bf16[512,512]{1,0:T(8,128)(2,1)} %fusion.109), channel_id=1, source_target_pairs={{0,2},{1,3},{2,0},{3,1},{4,6},{5,7},{6,4},{7,5},{8,10},{9,11},{10,... | collective-permute-start | bytes 1572872 | tf_op jit(solution)/shard_map/ppermute | solution.py:29
  520.9 116.8 %collective-permute-start.38 = (bf16[512,512]{1,0:T(8,128)(2,1)}, bf16[512,512]{1,0:T(8,128)(2,1)}, u32[]{:S(2)}, u32[]{:S(2)}) collective-permute-start(bf16[512,512]{1,0:T(8,128)(2,1)} %fusion.115), channel_id=1, source_target_pairs={{0,3},{1,2},{2,1},{3,0},{4,7},{5,6},{6,5},{7,4},{8,11},{9,10},{10,... | collective-permute-start | bytes 1572872 | tf_op jit(solution)/shard_map/ppermute | solution.py:29
  732.8 106.3 %reduce-scatter.6.cloned.1.call-start = ((), (), s32[]{:S(2)}) async-start(), calls=%async_computation.10 | async-start | bytes 3538944 | tf_op jit(solution)/shard_map/reduce_scatter | solution.py:327
  790.2 124.3 %reduce-scatter.14.cloned.1.call-start = ((), (), s32[]{:S(2)}) async-start(), calls=%async_computation.18 | async-start | bytes 9437184 | tf_op jit(solution)/shard_map/reduce_scatter | solution.py:331
  802.6 187.5 %reduce-scatter.12.cloned.1.call-start = ((), (), s32[]{:S(2)}) async-start(), calls=%async_computation.16 | async-start | bytes 9437184 | tf_op jit(solution)/shard_map/reduce_scatter | solution.py:327
  815.4 250.1 %reduce-scatter.10.cloned.1.call-start = ((), (), s32[]{:S(2)}) async-start(), calls=%async_computation.14 | async-start | bytes 9437184 | tf_op jit(solution)/shard_map/reduce_scatter | solution.py:327
  827.6 345.4 %all-gather.23.cloned.1.call-start = ((), (), s32[]{:S(2)}) async-start(), calls=%async_computation.13 | async-start | bytes 1310720 | tf_op jit(solution)/shard_map/all_gather | solution.py:332
  828.3 347.4 %all-gather.21.cloned.1.call-start = ((), (), s32[]{:S(2)}) async-start(), calls=%async_computation.11 | async-start | bytes 1966080 | tf_op jit(solution)/shard_map/all_gather | solution.py:328
  839.1 340.6 %all-gather.29.cloned.1.call-start = ((), (), s32[]{:S(2)}) async-start(), calls=%async_computation.19 | async-start | bytes 5242880 | tf_op jit(solution)/shard_map/all_gather | solution.py:332
  914.5 271.9 %all-gather.27.cloned.1.call-start = ((), (), s32[]{:S(2)}) async-start(), calls=%async_computation.17 | async-start | bytes 5242880 | tf_op jit(solution)/shard_map/all_gather | solution.py:328
  990.1 223.9 %all-gather.25.cloned.1.call-start = ((), (), s32[]{:S(2)}) async-start(), calls=%async_computation.15 | async-start | bytes 5242880 | tf_op jit(solution)/shard_map/all_gather | solution.py:328
  (233 other events, 7830.1 us)
Sparse Core Ops, SparseCore 0:
  10.5 34.8 all-gather.10
  47.3 28.0 all-gather.12
  77.9 55.8 all-gather.18
  136.1 54.2 all-gather.16
  192.1 61.9 all-gather.14
  732.9 54.0 reduce-scatter.7
  790.4 48.6 reduce-scatter.5
  843.2 71.2 reduce-scatter.13
  918.5 71.5 reduce-scatter.11
  994.0 71.5 reduce-scatter.9
  1067.1 16.8 all-gather.22
  1085.3 19.6 all-gather.20
  1106.6 34.9 all-gather.28
  1143.0 35.0 all-gather.26
  1179.5 34.4 all-gather.24

commit v2 on v1

v2 whole, which is shorter than its diff:
```python
import functools

import jax
import jax.numpy as jnp
from jax import lax
from jax.experimental import pallas as pl
from jax.experimental.pallas import tpu as pltpu
from jax.sharding import PartitionSpec as P

HEAD_SIZE = 64
CONTINUATION_LEN = 128
EPSILON = 1e-05
ROPE_BASE = 500000.0
BF = jnp.bfloat16
F32 = jnp.float32
EVERY = ("fsdp", "ctx")


def product(left, right):
    return jnp.dot(left, right, preferred_element_type=F32)


def product_nt(left, right):
    return lax.dot_general(left, right, (((1,), (1,)), ((), ())), preferred_element_type=F32)


def product_tn(left, right):
    return lax.dot_general(left, right, (((0,), (0,)), ((), ())), preferred_element_type=F32)


def swap(value, axis, step):
    count = lax.axis_size(axis)
    return lax.ppermute(value, axis, [(i, i ^ step) for i in range(count)])


def pieces_of(value, axis="tp"):
    return [value] + [swap(value, axis, step) for step in range(1, lax.axis_size(axis))]


def tie(values, deps):
    return lax.optimization_barrier((values, deps))[0]


def inner_pair():
    me = lax.axis_index("tp")
    return (me == 1) | (me == 2)


def gather_tp(value):
    if lax.axis_size("tp") != 4:
        parts = pieces_of(value)
        return parts, parts[1:]
    second = swap(value, "tp", 2)
    first = swap(value, "tp", 1)
    middle = lax.ppermute(value, "tp", [(1, 2), (2, 1)])
    passed = lax.ppermute(second, "tp", [(2, 3), (1, 0)])
    third = jnp.where(inner_pair(), middle, passed)
    return [value, first, second, third], [first, second, middle]


def all_sum(value, axis="tp"):
    parts = pieces_of(value, axis)
    total = parts[0]
    for part in parts[1:]:
        total = total + part
    return total


def group_sum(value):
    if not paired():
        return lax.psum(value, EVERY)
    for axis, step in (("ctx", 1), ("ctx", 2), ("fsdp", 1)):
        value = value + swap(value, axis, step)
    return value


def blocks_of(make_block):
    me = lax.axis_index("tp")
    blocks = [make_block(me ^ step) for step in range(lax.axis_size("tp"))]
    if len(blocks) != 4:
        return [blocks[0]] + [block.astype(BF) for block in blocks[1:]]
    return [blocks[0], blocks[1].astype(BF), blocks[2], blocks[3].astype(BF)]


def exchange_sum(blocks):
    if len(blocks) != 4:
        sent = [swap(block, "tp", step) for step, block in enumerate(blocks) if step > 0]
    else:
        passed = lax.ppermute(blocks[3], "tp", [(3, 2), (0, 1)])
        middle = lax.ppermute(blocks[3], "tp", [(1, 2), (2, 1)])
        first = swap(blocks[1], "tp", 1)
        relay = (blocks[2] + passed.astype(F32)).astype(BF)
        sent = [middle, first, swap(relay, "tp", 2)]
    total = blocks[0]
    for part in sent:
        total = total + part.astype(F32)
    return total


def columns(matrix, block, width):
    return lax.dynamic_slice(matrix, (0, block * width), (matrix.shape[0], width))


def rows_of(matrix, block, width):
    return lax.dynamic_slice(matrix, (block * width, 0), (width, matrix.shape[1]))


def cut_of(matrix, axis, block, width):
    return rows_of(matrix, block, width) if axis == 0 else columns(matrix, block, width)


def paired():
    return lax.axis_size("fsdp") == 2 and lax.axis_size("ctx") == 4


def gather_weight(weight, axis, after=None):
    me = lax.axis_index("ctx")
    size = weight.shape[axis] // lax.axis_size("ctx")
    quarter = cut_of(weight, axis, me, size)
    if not paired():
        return lax.all_gather(quarter, EVERY, axis=axis, tiled=True), quarter
    if after is not None:
        quarter = tie(quarter, after)
    mine = lax.axis_index("fsdp")
    far = swap(quarter, "fsdp", 1)
    across = swap(far, "ctx", 2)
    found = [(0, far), (2, across), (1, swap(far, "ctx", 1)), (3, swap(across, "ctx", 1))]
    shape = list(weight.shape)
    shape[axis] *= 2
    whole = jnp.zeros(shape, weight.dtype)

    def put(whole, part, start):
        return lax.dynamic_update_slice(whole, part, (start, 0) if axis == 0 else (0, start))

    whole = put(whole, weight, mine * size * 4)
    for step, part in found:
        whole = put(whole, part, ((1 - mine) * 4 + (me ^ step)) * size)
    return whole, far


def gather_weight_offload(weight, axis, after):
    size = weight.shape[axis] // lax.axis_size("ctx")
    quarter = tie(cut_of(weight, axis, lax.axis_index("ctx"), size), after)
    return lax.all_gather(quarter, EVERY, axis=axis, tiled=True)


def gather_out(weight):
    if not paired():
        pieces, done = gather_tp(lax.all_gather(weight, "fsdp", axis=1, tiled=True))
        return jnp.concatenate(pieces, axis=0), done
    me = lax.axis_index("ctx")
    mine = lax.axis_index("fsdp")
    size = weight.shape[1] // lax.axis_size("ctx")
    pieces, done = gather_tp(columns(weight, me, size))
    own = jnp.concatenate(pieces, axis=0)
    far = swap(own, "fsdp", 1)
    found = [(mine, 0, own), (1 - mine, 0, far)]
    found += [(mine, 2, swap(own, "ctx", 2)), (1 - mine, 2, swap(far, "ctx", 2))]
    found += [(f, step ^ 1, swap(part, "ctx", 1)) for f, step, part in found]
    whole = jnp.zeros((own.shape[0], size * 8), weight.dtype)
    for f, step, part in found:
        whole = lax.dynamic_update_slice(whole, part, (0, (f * 4 + (me ^ step)) * size))
    return whole, done


def grad_start(left, right, axis):
    if not paired():
        whole = product_tn(left, right).astype(BF)
        return whole, whole, whole
    mine = lax.axis_index("fsdp")
    core = lax.axis_index("ctx") % 2
    split, other = (left, right) if axis == 0 else (right, left)
    half = lambda m, i: columns(m, i, m.shape[1] // 2)
    split_far, split_own = half(split, 1 - mine), half(split, mine)
    other_far, other_own = half(other, 1 - core), half(other, core)
    dot = lambda s, t: product_tn(s, t) if axis == 0 else product_tn(t, s)
    first = swap(dot(split_far, other_far).astype(BF), "ctx", 1)
    second = swap(dot(split_own, other_far).astype(BF), "ctx", 1)
    far = (dot(split_far, other_own) + first.astype(F32)).astype(BF)
    kept = dot(split_own, other_own) + second.astype(F32)
    return swap(far, "fsdp", 1), kept, far


def grad_middle(arrived, kept, far, axis):
    if not paired():
        return lax.psum_scatter(kept, EVERY, scatter_dimension=axis, tiled=True)
    side = lax.axis_index("ctx") // 2
    size = kept.shape[axis] // 2
    half = lambda i: cut_of(kept, axis, i, size) + cut_of(arrived, axis, i, size).astype(F32)
    sent = swap(half(1 - side).astype(BF), "ctx", 2)
    return (half(side) + sent.astype(F32)).astype(BF)


def grad_end(piece, axis):
    if not paired():
        return lax.all_gather(piece, "ctx", axis=axis, tiled=True).astype(F32)
    side = lax.axis_index("ctx") // 2
    core = lax.axis_index("ctx") % 2
    across = swap(piece, "ctx", 2)
    own = in_order(piece, across, side, axis)
    return in_order(own, swap(own, "ctx", 1), core, 1 - axis).astype(F32)


def in_order(mine, theirs, index, axis):
    low = index == 0
    return jnp.concatenate(
        [jnp.where(low, mine, theirs), jnp.where(low, theirs, mine)], axis=axis
    )


LOG2E = 1.4426950408889634
SCORE_SCALE = 0.125
LANES = 128


def lane_index(shape):
    return lax.broadcasted_iota(jnp.int32, shape, len(shape) - 1)


def turn(tile, cosine, sine):
    low = lane_index(tile.shape) % HEAD_SIZE < HEAD_SIZE // 2
    other = jnp.where(
        low,
        pltpu.roll(tile, LANES - HEAD_SIZE // 2, 1),
        pltpu.roll(tile, HEAD_SIZE // 2, 1),
    )
    return tile * cosine + other * sine


def doubled(tile, head):
    wide = tile.astype(F32)
    low = lane_index(tile.shape) < HEAD_SIZE
    other = pltpu.roll(wide, HEAD_SIZE, 1)
    return jnp.where(low == (head == 0), wide, other).astype(tile.dtype)


def half_of(tile, j):
    low = lane_index(tile.shape) < HEAD_SIZE
    keep = low if j == 0 else jnp.logical_not(low)
    return jnp.where(keep, tile, jnp.zeros_like(tile))


def dot_nt(left, right):
    return lax.dot_general(left, right, (((1,), (1,)), ((), ())), preferred_element_type=F32)


def dot_nn(left, right):
    return lax.dot_general(left, right, (((1,), (0,)), ((), ())), preferred_element_type=F32)


def params_of(*semantics, limit=56 << 20):
    return pltpu.CompilerParams(dimension_semantics=semantics, vmem_limit_bytes=limit)


def entry_kernel(count, model_width, query_width, order, *refs):
    parts = refs[:count]
    gain, router, weight, mask, cosine, sine = refs[count : count + 6]
    xn_ref, query_ref, kv_ref, scale_ref, gate_ref, mix_ref = refs[count + 6 :]
    width = parts[0].shape[1]
    wide = [p[...].astype(F32) for p in parts]
    squares = sum(jnp.sum(w * w, axis=1, keepdims=True) for w in wide)
    logits = sum(
        jnp.sum(w * router[r : r + 1, :], axis=1, keepdims=True) for r, w in enumerate(wide)
    )
    scale = lax.rsqrt(squares / model_width + EPSILON)
    gate = jax.nn.sigmoid(logits)
    scale_ref[...] = scale
    gate_ref[...] = gate
    mix_ref[...] = mask[...] * gate
    total = None
    for r, w in enumerate(wide):
        normed = (w * scale * gain[r : r + 1, :]).astype(BF)
        place = pl.ds(pl.multiple_of(order[r] * width, width), width)
        xn_ref[:, place] = normed
        term = dot_nn(normed, weight[place, :])
        total = term if total is None else total + term
    for t in range(query_width // LANES):
        cut = slice(t * LANES, (t + 1) * LANES)
        query_ref[:, cut] = turn(total[:, cut], cosine[...], sine[...]).astype(BF)
    key_width = kv_ref.shape[1] // 2
    key = total[:, query_width : query_width + key_width]
    kv_ref[:, :key_width] = turn(key, cosine[...], sine[...]).astype(BF)
    kv_ref[:, key_width:] = total[:, query_width + key_width :].astype(BF)


def entry(parts, gains, routers, weight, mask, tables, order, query_width):
    rows, width = parts[0].shape
    count = len(parts)
    block = min(rows, 256)
    total_width = weight.shape[1]
    kv_width = total_width - query_width
    whole = lambda a: pl.BlockSpec(a.shape, lambda i, o: (0, 0))
    row = lambda w: pl.BlockSpec((block, w), lambda i, o: (i, 0))
    outs = [(width * count, BF), (query_width, BF), (kv_width, BF), (1, F32), (1, F32), (1, F32)]
    return pl.pallas_call(
        functools.partial(entry_kernel, count, width * count, query_width),
        out_shape=[jax.ShapeDtypeStruct((rows, w), d) for w, d in outs],
        grid_spec=pltpu.PrefetchScalarGridSpec(
            num_scalar_prefetch=1,
            grid=(rows // block,),
            in_specs=[row(width)] * count
            + [whole(gains), whole(routers), whole(weight), row(1), row(LANES), row(LANES)],
            out_specs=[row(w) for w, d in outs],
        ),
        compiler_params=params_of("arbitrary"),
        cost_estimate=pl.CostEstimate(
            flops=2 * rows * width * count * total_width,
            bytes_accessed=rows * width * count * 4 + weight.size * 2,
            transcendentals=rows,
        ),
        name="entry",
    )(order, *parts, gains, routers, weight, mask, *tables)


def softmax_columns(keys, biases, queries, scores):
    top = None
    for i, (key, bias) in enumerate(zip(keys, biases)):
        s = dot_nt(key, queries) * (SCORE_SCALE * LOG2E)
        if bias is not None:
            s = s + bias
        scores[i][...] = s
        part = jnp.max(s, axis=0, keepdims=True)
        top = part if top is None else jnp.maximum(top, part)
    total = 0.0
    for ref in scores:
        e = jnp.exp2(ref[...] - top)
        ref[...] = e
        total = total + jnp.sum(e, axis=0, keepdims=True)
    share = 1.0 / total
    return [(ref[...] * share).astype(BF) for ref in scores], top + jnp.log2(total)


def causal_bias(keys, rows, start):
    key = lax.broadcasted_iota(jnp.int32, (keys, rows), 0)
    row = lax.broadcasted_iota(jnp.int32, (keys, rows), 1)
    return jnp.where(key <= row + start, 0.0, -1e30)


def prompt_forward_kernel(start, q_ref, kv_ref, o_ref, lse_ref, vt_ref, bias_ref, s_ref):
    tile = pl.program_id(1)
    rows = q_ref.shape[1]
    head = tile // (pl.num_programs(1) // 2)

    @pl.when((pl.program_id(0) == 0) & (tile == 0))
    def _():
        bias_ref[...] = causal_bias(bias_ref.shape[0], rows, start[0])

    @pl.when(tile == 0)
    def _():
        vt_ref[...] = kv_ref[0, :, LANES:].astype(F32).T.astype(BF)

    key = doubled(kv_ref[0, :, :LANES], head)
    value_t = vt_ref[pl.ds(pl.multiple_of(head * HEAD_SIZE, HEAD_SIZE), HEAD_SIZE), :]
    query = q_ref[0]
    outs = []
    for j in range(2):
        probs, lse = softmax_columns([key], [bias_ref[...]], half_of(query, j), [s_ref])
        lse_ref[0, 0, j : j + 1, :] = lse
        outs.append(dot_nn(value_t, probs[0]))
    o_ref[0] = jnp.concatenate(outs, axis=0).T.astype(BF)


def prompt_forward(query, kv, start):
    groups, rows, query_width = query.shape
    length = kv.shape[1]
    tiles = query_width // LANES
    return pl.pallas_call(
        prompt_forward_kernel,
        out_shape=[
            jax.ShapeDtypeStruct(query.shape, BF),
            jax.ShapeDtypeStruct((groups, tiles, 2, rows), F32),
        ],
        grid_spec=pltpu.PrefetchScalarGridSpec(
            num_scalar_prefetch=1,
            grid=(groups, tiles),
            in_specs=[
                pl.BlockSpec((1, rows, LANES), lambda g, t, s: (g, 0, t)),
                pl.BlockSpec((1, length, 2 * LANES), lambda g, t, s: (g, 0, 0)),
            ],
            out_specs=[
                pl.BlockSpec((1, rows, LANES), lambda g, t, s: (g, 0, t)),
                pl.BlockSpec((1, 1, 2, rows), lambda g, t, s: (g, t, 0, 0)),
            ],
            scratch_shapes=[
                pltpu.VMEM((LANES, length), BF),
                pltpu.VMEM((length, rows), F32),
                pltpu.VMEM((length, rows), F32),
            ],
        ),
        compiler_params=params_of("arbitrary", "arbitrary"),
        cost_estimate=pl.CostEstimate(
            flops=8 * groups * tiles * rows * length * LANES,
            bytes_accessed=query.size * 4 + kv.size * 2,
            transcendentals=groups * tiles * 2 * rows * length,
        ),
        name="prompt_forward",
    )(start, query, kv)


def cont_forward_kernel(which, q_ref, kv_ref, own_ref, o_ref, lse_ref, vt_ref, wt_ref, s_ref, t_ref):
    tile = pl.program_id(1)
    rows = q_ref.shape[1]
    head = tile // (pl.num_programs(1) // 2)

    @pl.when(tile == 0)
    def _():
        vt_ref[...] = kv_ref[0, :, LANES:].astype(F32).T.astype(BF)
        wt_ref[...] = own_ref[0, :, LANES:].astype(F32).T.astype(BF)

    place = pl.ds(pl.multiple_of(head * HEAD_SIZE, HEAD_SIZE), HEAD_SIZE)
    keys = [doubled(kv_ref[0, :, :LANES], head), doubled(own_ref[0, :, :LANES], head)]
    query = q_ref[0]
    both = jnp.concatenate([half_of(query, 0), half_of(query, 1)], axis=0)
    bias = causal_bias(rows, rows, 0)
    probs, lse = softmax_columns(
        keys, [None, jnp.concatenate([bias, bias], axis=1)], both, [s_ref, t_ref]
    )
    out = dot_nn(vt_ref[place, :], probs[0]) + dot_nn(wt_ref[place, :], probs[1])
    lse_ref[0, 0] = lse
    o_ref[0] = jnp.concatenate([out[:, :rows], out[:, rows:]], axis=0).T.astype(BF)


def cont_forward(query, kv, own, which):
    conts, rows, query_width = query.shape
    length = kv.shape[1]
    tiles = query_width // LANES
    return pl.pallas_call(
        cont_forward_kernel,
        out_shape=[
            jax.ShapeDtypeStruct(query.shape, BF),
            jax.ShapeDtypeStruct((conts, tiles, 1, 2 * rows), F32),
        ],
        grid_spec=pltpu.PrefetchScalarGridSpec(
            num_scalar_prefetch=1,
            grid=(conts, tiles),
            in_specs=[
                pl.BlockSpec((1, rows, LANES), lambda g, t, w: (g, 0, t)),
                pl.BlockSpec((1, length, 2 * LANES), lambda g, t, w: (w[g], 0, 0)),
                pl.BlockSpec((1, rows, 2 * LANES), lambda g, t, w: (g, 0, 0)),
            ],
            out_specs=[
                pl.BlockSpec((1, rows, LANES), lambda g, t, w: (g, 0, t)),
                pl.BlockSpec((1, 1, 1, 2 * rows), lambda g, t, w: (g, t, 0, 0)),
            ],
            scratch_shapes=[
                pltpu.VMEM((LANES, length), BF),
                pltpu.VMEM((LANES, rows), BF),
                pltpu.VMEM((length, 2 * rows), F32),
                pltpu.VMEM((rows, 2 * rows), F32),
            ],
        ),
        compiler_params=params_of("arbitrary", "arbitrary"),
        cost_estimate=pl.CostEstimate(
            flops=8 * conts * tiles * rows * (length + rows) * LANES,
            bytes_accessed=query.size * 4 + conts * length * LANES * 4,
            transcendentals=conts * tiles * 2 * rows * (length + rows),
        ),
        name="cont_forward",
    )(which, query, kv, own)


def backward_columns(key, value, key_t, bias, query, grad, lse, delta, chunk):
    dks, dvs, dq = [], [], None
    for c in range(key.shape[0] // chunk):
        cut = slice(c * chunk, (c + 1) * chunk)
        s = dot_nt(key[cut], query) * (SCORE_SCALE * LOG2E)
        if bias is not None:
            s = s + bias[cut]
        p = jnp.exp2(s - lse)
        dp = dot_nt(value[cut], grad)
        ds = (p * (dp - delta)).astype(BF)
        dvs.append(dot_nn(p.astype(BF), grad))
        dks.append(dot_nn(ds, query))
        term = dot_nn(key_t[:, cut], ds)
        dq = term if dq is None else dq + term
    return dks, dvs, dq


def folded(parts, head):
    whole = jnp.concatenate(parts, axis=0)
    low = lane_index(whole.shape) < HEAD_SIZE
    return jnp.where(low == (head == 0), whole + pltpu.roll(whole, HEAD_SIZE, 1), 0.0)


def add_into(ref, value, first):
    @pl.when(first)
    def _():
        ref[0] = value

    @pl.when(jnp.logical_not(first))
    def _():
        ref[0] = ref[0] + value


def prompt_backward_kernel(
    start, q_ref, kv_ref, o_ref, g_ref, lse_ref, dq_ref, dk_ref, dv_ref, kt_ref, bias_ref
):
    tile = pl.program_id(1)
    rows = q_ref.shape[1]
    head = tile // (pl.num_programs(1) // 2)

    @pl.when((pl.program_id(0) == 0) & (tile == 0))
    def _():
        bias_ref[...] = causal_bias(bias_ref.shape[0], rows, start[0])

    @pl.when(tile == 0)
    def _():
        kt_ref[...] = kv_ref[0, :, :LANES].astype(F32).T.astype(BF)

    key = doubled(kv_ref[0, :, :LANES], head)
    value = doubled(kv_ref[0, :, LANES:], head)
    key_t = kt_ref[pl.ds(pl.multiple_of(head * HEAD_SIZE, HEAD_SIZE), HEAD_SIZE), :]
    query, grad = q_ref[0], g_ref[0]
    mixed = (grad.astype(F32) * o_ref[0].astype(F32)).T
    dks, dvs, dqs = None, None, []
    for j in range(2):
        delta = jnp.sum(mixed[j * HEAD_SIZE : (j + 1) * HEAD_SIZE], axis=0, keepdims=True)
        dk, dv, dq = backward_columns(
            key,
            value,
            key_t,
            bias_ref,
            half_of(query, j),
            half_of(grad, j),
            lse_ref[0, 0, j : j + 1, :],
            delta,
            256,
        )
        dks = dk if dks is None else [a + b for a, b in zip(dks, dk)]
        dvs = dv if dvs is None else [a + b for a, b in zip(dvs, dv)]
        dqs.append(dq)
    dq_ref[0] = jnp.concatenate(dqs, axis=0).T * SCORE_SCALE
    add_into(dk_ref, folded(dks, head) * SCORE_SCALE, tile == 0)
    add_into(dv_ref, folded(dvs, head), tile == 0)


def prompt_backward(query, kv, out, grad, lse, start):
    groups, rows, query_width = query.shape
    length = kv.shape[1]
    tiles = query_width // LANES
    q_spec = pl.BlockSpec((1, rows, LANES), lambda g, t, s: (g, 0, t))
    k_spec = pl.BlockSpec((1, length, LANES), lambda g, t, s: (g, 0, 0))
    return pl.pallas_call(
        prompt_backward_kernel,
        out_shape=[
            jax.ShapeDtypeStruct(query.shape, F32),
            jax.ShapeDtypeStruct((groups, length, LANES), F32),
            jax.ShapeDtypeStruct((groups, length, LANES), F32),
        ],
        grid_spec=pltpu.PrefetchScalarGridSpec(
            num_scalar_prefetch=1,
            grid=(groups, tiles),
            in_specs=[
                q_spec,
                pl.BlockSpec((1, length, 2 * LANES), lambda g, t, s: (g, 0, 0)),
                q_spec,
                q_spec,
                pl.BlockSpec((1, 1, 2, rows), lambda g, t, s: (g, t, 0, 0)),
            ],
            out_specs=[q_spec, k_spec, k_spec],
            scratch_shapes=[pltpu.VMEM((LANES, length), BF), pltpu.VMEM((length, rows), F32)],
        ),
        compiler_params=params_of("arbitrary", "arbitrary"),
        cost_estimate=pl.CostEstimate(
            flops=20 * groups * tiles * rows * length * LANES,
            bytes_accessed=query.size * 10 + kv.size * 6,
            transcendentals=groups * tiles * 2 * rows * length,
        ),
        name="prompt_backward",
    )(start, query, kv, out, grad, lse)


def cont_backward_kernel(
    which,
    q_ref,
    kv_ref,
    own_ref,
    o_ref,
    g_ref,
    lse_ref,
    dq_ref,
    dk_ref,
    dv_ref,
    ek_ref,
    ev_ref,
    kt_ref,
    ot_ref,
):
    tile = pl.program_id(1)
    rows = q_ref.shape[1]
    head = tile // (pl.num_programs(1) // 2)

    @pl.when(tile == 0)
    def _():
        kt_ref[...] = kv_ref[0, :, :LANES].astype(F32).T.astype(BF)
        ot_ref[...] = own_ref[0, :, :LANES].astype(F32).T.astype(BF)

    place = pl.ds(pl.multiple_of(head * HEAD_SIZE, HEAD_SIZE), HEAD_SIZE)
    query, grad = q_ref[0], g_ref[0]
    mixed = (grad.astype(F32) * o_ref[0].astype(F32)).T
    delta = jnp.concatenate(
        [
            jnp.sum(mixed[j * HEAD_SIZE : (j + 1) * HEAD_SIZE], axis=0, keepdims=True)
            for j in range(2)
        ],
        axis=1,
    )
    queries = jnp.concatenate([half_of(query, 0), half_of(query, 1)], axis=0)
    grads = jnp.concatenate([half_of(grad, 0), half_of(grad, 1)], axis=0)
    bias = causal_bias(rows, rows, 0)
    lse = lse_ref[0, 0]
    dk, dv, dq = backward_columns(
        doubled(kv_ref[0, :, :LANES], head),
        doubled(kv_ref[0, :, LANES:], head),
        kt_ref[place, :],
        None,
        queries,
        grads,
        lse,
        delta,
        256,
    )
    ek, ev, eq = backward_columns(
        doubled(own_ref[0, :, :LANES], head),
        doubled(own_ref[0, :, LANES:], head),
        ot_ref[place, :],
        jnp.concatenate([bias, bias], axis=1),
        queries,
        grads,
        lse,
        delta,
        rows,
    )
    dq = dq + eq
    dq_ref[0] = jnp.concatenate([dq[:, :rows], dq[:, rows:]], axis=0).T * SCORE_SCALE
    add_into(dk_ref, folded(dk, head) * SCORE_SCALE, tile == 0)
    add_into(dv_ref, folded(dv, head), tile == 0)
    add_into(ek_ref, folded(ek, head) * SCORE_SCALE, tile == 0)
    add_into(ev_ref, folded(ev, head), tile == 0)


def cont_backward(query, kv, own, out, grad, lse, which):
    conts, rows, query_width = query.shape
    length = kv.shape[1]
    tiles = query_width // LANES
    q_spec = pl.BlockSpec((1, rows, LANES), lambda g, t, w: (g, 0, t))
    k_spec = pl.BlockSpec((1, length, LANES), lambda g, t, w: (g, 0, 0))
    e_spec = pl.BlockSpec((1, rows, LANES), lambda g, t, w: (g, 0, 0))
    return pl.pallas_call(
        cont_backward_kernel,
        out_shape=[jax.ShapeDtypeStruct(query.shape, F32)]
        + [jax.ShapeDtypeStruct((conts, length, LANES), F32)] * 2
        + [jax.ShapeDtypeStruct((conts, rows, LANES), F32)] * 2,
        grid_spec=pltpu.PrefetchScalarGridSpec(
            num_scalar_prefetch=1,
            grid=(conts, tiles),
            in_specs=[
                q_spec,
                pl.BlockSpec((1, length, 2 * LANES), lambda g, t, w: (w[g], 0, 0)),
                pl.BlockSpec((1, rows, 2 * LANES), lambda g, t, w: (g, 0, 0)),
                q_spec,
                q_spec,
                pl.BlockSpec((1, 1, 1, 2 * rows), lambda g, t, w: (g, t, 0, 0)),
            ],
            out_specs=[q_spec, k_spec, k_spec, e_spec, e_spec],
            scratch_shapes=[pltpu.VMEM((LANES, length), BF), pltpu.VMEM((LANES, rows), BF)],
        ),
        compiler_params=params_of("arbitrary", "arbitrary"),
        cost_estimate=pl.CostEstimate(
            flops=20 * conts * tiles * rows * (length + rows) * LANES,
            bytes_accessed=query.size * 10 + conts * length * LANES * 12,
            transcendentals=conts * tiles * 2 * rows * (length + rows),
        ),
        name="cont_backward",
    )(which, query, kv, own, out, grad, lse)


def finish_kernel(count, dq_ref, dkv_ref, *refs):
    others = refs[:count]
    q_ref, kv_ref, cosine, sine, out_ref, total_ref = refs[count:]
    query_width = dq_ref.shape[1]
    key_width = dkv_ref.shape[1] // 2
    dkv = dkv_ref[...]
    for other in others:
        dkv = dkv + other[...].astype(F32)
    dq = dq_ref[...]
    total_ref[...] = jnp.sum(dq * q_ref[...].astype(F32), axis=1, keepdims=True) + jnp.sum(
        dkv * kv_ref[...].astype(F32), axis=1, keepdims=True
    )
    back = -sine[...]
    for t in range(query_width // LANES):
        cut = slice(t * LANES, (t + 1) * LANES)
        out_ref[:, cut] = turn(dq[:, cut], cosine[...], back).astype(BF)
    out_ref[:, query_width : query_width + key_width] = turn(
        dkv[:, :key_width], cosine[...], back
    ).astype(BF)
    out_ref[:, query_width + key_width :] = dkv[:, key_width:].astype(BF)


def finish(dq, dkv, others, query, kv, tables):
    rows, query_width = dq.shape
    kv_width = dkv.shape[1]
    block = min(rows, 256)
    row = lambda w: pl.BlockSpec((block, w), lambda i: (i, 0))
    return pl.pallas_call(
        functools.partial(finish_kernel, len(others)),
        out_shape=[
            jax.ShapeDtypeStruct((rows, query_width + kv_width), BF),
            jax.ShapeDtypeStruct((rows, 1), F32),
        ],
        grid=(rows // block,),
        in_specs=[row(query_width)]
        + [row(kv_width)] * (1 + len(others))
        + [row(query_width), row(kv_width), row(LANES), row(LANES)],
        out_specs=[row(query_width + kv_width), row(1)],
        compiler_params=params_of("arbitrary"),
        cost_estimate=pl.CostEstimate(
            flops=20 * dq.size, bytes_accessed=dq.size * 12, transcendentals=0
        ),
        name="finish",
    )(dq, dkv, *others, query, kv, *tables)


def rope_tables(positions):
    lane = jnp.arange(LANES)
    half = HEAD_SIZE // 2
    frequency = ROPE_BASE ** (-(lane % half).astype(F32) * 2.0 / HEAD_SIZE)
    angles = positions.astype(F32)[:, None] * frequency[None, :]
    sign = jnp.where(lane % HEAD_SIZE < half, -1.0, 1.0)
    return jnp.cos(angles), jnp.sin(angles) * sign[None, :]


def second_norm_kernel(count, model_width, order, *refs):
    x, o = refs[:count], refs[count : 2 * count]
    gain, weight, out_ref, hidden_ref, scale_ref = refs[2 * count :]
    width, head_width = x[0].shape[1], o[0].shape[1]
    total = None
    for r, part in enumerate(o):
        term = dot_nn(part[...], weight[r * head_width : (r + 1) * head_width, :])
        total = term if total is None else total + term
    hidden_ref[...] = total
    places = [pl.ds(pl.multiple_of(order[r] * width, width), width) for r in range(count)]
    squares = 0.0
    for place, part in zip(places, x):
        h = hidden_ref[:, place] + part[...].astype(F32)
        hidden_ref[:, place] = h
        squares = squares + jnp.sum(h * h, axis=1, keepdims=True)
    scale = lax.rsqrt(squares / model_width + EPSILON)
    scale_ref[...] = scale
    for r, place in enumerate(places):
        out_ref[:, place] = (hidden_ref[:, place] * scale * gain[r : r + 1, :]).astype(BF)


def spread_kernel(count, order, *refs):
    parts = refs[:count]
    mix, out_ref = refs[count:]
    width = parts[0].shape[1]
    for r, part in enumerate(parts):
        place = pl.ds(pl.multiple_of(order[r] * width, width), width)
        out_ref[:, place] = (part[...].astype(F32) * mix[...]).astype(BF)


def third_norm_kernel(count, model_width, order, *refs):
    cot, n = refs[:count], refs[count : 2 * count]
    gain, scale_ref, mix, hidden_ref, out_ref, factor_ref = refs[2 * count :]
    width = cot[0].shape[1]
    places = [pl.ds(pl.multiple_of(order[r] * width, width), width) for r in range(count)]
    scale = scale_ref[...]
    total = 0.0
    for r, place in enumerate(places):
        total = total + jnp.sum(
            hidden_ref[:, place] * gain[r : r + 1, :] * n[r][...].astype(F32),
            axis=1,
            keepdims=True,
        )
    factor = scale * scale * scale * total / model_width
    factor_ref[...] = factor
    for r, place in enumerate(places):
        value = (
            cot[r][...].astype(F32) * mix[...]
            + scale * gain[r : r + 1, :] * n[r][...].astype(F32)
            - hidden_ref[:, place] * factor
        )
        out_ref[:, place] = value.astype(BF)


def placed_call(kernel, name, order, part_sets, wholes, columns_in, outs, flops=0):
    parts = [p for group in part_sets for p in group]
    rows, width = parts[0].shape
    block = min(rows, 256)
    row = lambda w: pl.BlockSpec((block, w), lambda i, o: (i, 0))
    return pl.pallas_call(
        kernel,
        out_shape=[jax.ShapeDtypeStruct((rows, w), d) for w, d in outs],
        grid_spec=pltpu.PrefetchScalarGridSpec(
            num_scalar_prefetch=1,
            grid=(rows // block,),
            in_specs=[row(p.shape[1]) for p in parts]
            + [pl.BlockSpec(w.shape, lambda i, o: (0, 0)) for w in wholes]
            + [row(c.shape[1]) for c in columns_in],
            out_specs=[row(w) for w, d in outs],
        ),
        compiler_params=params_of("arbitrary"),
        cost_estimate=pl.CostEstimate(
            flops=8 * len(parts) * rows * width + flops,
            bytes_accessed=2 * len(parts) * rows * width,
            transcendentals=rows,
        ),
        name=name,
    )(order, *parts, *wholes, *columns_in)


def second_norm(x, o, gains, weight, order):
    count, width = len(x), x[0].shape[1]
    return placed_call(
        functools.partial(second_norm_kernel, count, count * width),
        "second_norm",
        order,
        [x, o],
        [gains, weight],
        [],
        [(count * width, BF), (count * width, F32), (1, F32)],
        x[0].shape[0] * weight.size * 2,
    )


def spread(parts, mix, order):
    count, width = len(parts), parts[0].shape[1]
    return placed_call(
        functools.partial(spread_kernel, count),
        "spread",
        order,
        [parts],
        [],
        [mix],
        [(count * width, BF)],
    )[0]


def third_norm(hidden, cot, n, gains, scale, mix, order):
    count, width = len(cot), cot[0].shape[1]
    return placed_call(
        functools.partial(third_norm_kernel, count, count * width),
        "third_norm",
        order,
        [cot, n],
        [gains],
        [scale, mix, hidden],
        [(count * width, BF), (1, F32)],
    )


def body(
    prompt_in,
    cont_in,
    prompt_mask,
    cont_mask,
    cont_prompt,
    cont_start,
    gain_attn,
    gain_ffn,
    router,
    w_query,
    key_projection,
    w_value,
    w_out,
    w_gate,
    w_up,
    w_down,
    prompt_cot,
    cont_cot,
):
    groups, prompt_rows, width = prompt_in.shape
    conts = cont_in.shape[0]
    tp_size = lax.axis_size("tp")
    ctx_size = lax.axis_size("ctx")
    model_width = width * tp_size
    me_tp = lax.axis_index("tp")
    me_ctx = lax.axis_index("ctx")
    query_width = w_query.shape[1]
    key_width = key_projection.shape[1]
    kv_width = 2 * key_width
    streams = range(2)
    tokens_in = [prompt_in.reshape(-1, width), cont_in.reshape(-1, width)]
    cots = [prompt_cot.reshape(-1, width), cont_cot.reshape(-1, width)]
    masks = [prompt_mask.reshape(-1, 1).astype(F32), cont_mask.reshape(-1, 1).astype(F32)]
    prompt_place = me_ctx * prompt_rows + jnp.arange(prompt_rows, dtype=jnp.int32)
    cont_place = (
        cont_start[:, None] + jnp.arange(CONTINUATION_LEN, dtype=jnp.int32)[None, :]
    ).reshape(-1)
    tables = [rope_tables(jnp.tile(prompt_place, groups)), rope_tables(cont_place)]
    local_prompt = jnp.clip(cont_prompt - lax.axis_index("fsdp") * groups, 0, groups - 1)
    start = (me_ctx * prompt_rows).astype(jnp.int32)[None]
    order = jnp.stack([me_tp ^ step for step in range(tp_size)]).astype(jnp.int32)

    full_qkv, qkv_far = gather_weight(
        jnp.concatenate([w_query, key_projection, w_value], axis=1), 0
    )
    params = [p.astype(F32) for p in pieces_of(jnp.stack([gain_attn, gain_ffn, router]))]
    gains_attn = jnp.stack([p[0] for p in params])
    gains_ffn = jnp.stack([p[1] for p in params])
    routers = jnp.stack([p[2] for p in params])
    full_out, sent_out = gather_out(w_out)
    x_prompt, sent_prompt = gather_tp(tie(tokens_in[0], sent_out))
    x_cont, sent_cont = gather_tp(tie(tokens_in[1], sent_prompt))
    x_parts = [x_prompt, x_cont]
    full_gate, gate_far = gather_weight(w_gate, 0, qkv_far)
    full_up, up_far = gather_weight(w_up, 0, gate_far)
    full_down = gather_weight_offload(w_down, 1, sent_prompt)

    def enter(i):
        return entry(
            x_parts[i], gains_attn, routers, full_qkv, masks[i], tables[i], order, query_width
        )

    xn1, query, kv, scale_attn, gate_router, mixing = zip(enter(0), enter(1))
    own_kv = kv[0].reshape(groups, prompt_rows, kv_width)
    prompt_kv = jnp.zeros((groups, prompt_rows * ctx_size, kv_width), BF)
    for step, part in enumerate(pieces_of(own_kv, "ctx")):
        prompt_kv = lax.dynamic_update_slice(prompt_kv, part, (0, (me_ctx ^ step) * prompt_rows, 0))
    queries = [
        query[0].reshape(groups, prompt_rows, query_width),
        query[1].reshape(conts, CONTINUATION_LEN, query_width),
    ]
    cont_kv = kv[1].reshape(conts, CONTINUATION_LEN, kv_width)
    prompt_o, prompt_lse = prompt_forward(queries[0], prompt_kv, start)
    cont_o, cont_lse = cont_forward(queries[1], prompt_kv, cont_kv, local_prompt)
    attended = [prompt_o.reshape(-1, query_width), cont_o.reshape(-1, query_width)]
    o_prompt, sent_prompt = gather_tp(attended[0])
    o_cont, sent_cont = gather_tp(tie(attended[1], sent_prompt))
    cot_cont, sent_cont = gather_tp(tie(cots[1], sent_cont))
    cot_prompt, sent_prompt = gather_tp(tie(cots[0], sent_cont))
    o_parts, cot_parts = [o_prompt, o_cont], [cot_prompt, cot_cont]

    xn2, hidden, scale_ffn = zip(
        *[second_norm(x_parts[i], o_parts[i], gains_ffn, full_out, order) for i in streams]
    )

    inner, gate_grad, up_grad = [None, None], [None, None], [None, None]
    ffn_grad, blocks = [None, None], [None, None]
    for i in (1, 0):
        g = product(xn2[i], full_gate)
        u = product(xn2[i], full_up)
        s = jax.nn.sigmoid(g)
        inner[i] = (g * s * u).astype(BF)
        ffn_grad[i] = spread(cot_parts[i], mixing[i], order)
        dz = product_nt(ffn_grad[i], full_down)
        gate_grad[i] = (dz * u * s * (1.0 + g * (1.0 - s))).astype(BF)
        up_grad[i] = (dz * g * s).astype(BF)
        blocks[i] = blocks_of(
            lambda b, i=i: product_nt(gate_grad[i], rows_of(full_gate, b, width))
            + product_nt(up_grad[i], rows_of(full_up, b, width))
        )

    both = lambda pair: jnp.concatenate(pair, axis=0)
    normed_grad = [None, exchange_sum(blocks[1])]
    blocks[0], normed_grad[1] = lax.optimization_barrier((blocks[0], normed_grad[1]))
    normed_grad[0] = exchange_sum(blocks[0])
    n_cont, sent_cont = gather_tp(normed_grad[1].astype(BF))
    xn2_all, ffn_grad_all, inner_all, gate_all, up_all = tie(
        (both(xn2), both(ffn_grad), both(inner), both(gate_grad), both(up_grad)), blocks[0]
    )
    started = [
        grad_start(xn2_all, gate_all, 0),
        grad_start(xn2_all, up_all, 0),
        grad_start(inner_all, ffn_grad_all, 1),
    ]
    late = tie(normed_grad[0].astype(BF), (sent_cont, [s[2] for s in started]))
    n_prompt, sent_prompt = gather_tp(late)
    n_parts = [n_prompt, n_cont]
    inner_late = tie(inner, normed_grad[0])
    ffn_blocks = [
        blocks_of(lambda b, t=t: product(t, columns(full_down, b, width))) for t in inner_late
    ]

    def third(i):
        return third_norm(
            hidden[i], cot_parts[i], n_parts[i], gains_ffn, scale_ffn[i], mixing[i], order
        )

    middle = [grad_middle(*started[i], axis) for i, axis in enumerate((0, 0, 1))]
    dab_cont, factor_cont = third(1)
    dab_cont = tie(dab_cont, started[0][0])
    do_cont = product_nt(dab_cont, full_out[:query_width]).astype(BF)
    dq_cont, dk_cont, dv_cont, dk_own, dv_own = cont_backward(
        queries[1],
        prompt_kv,
        cont_kv,
        cont_o,
        do_cont.reshape(queries[1].shape),
        cont_lse,
        local_prompt,
    )
    dab_prompt, factor_prompt = third(0)
    dab_prompt = tie(dab_prompt, (middle[0], started[1][0]))
    do_prompt = product_nt(dab_prompt, full_out[:query_width]).astype(BF)
    dab, factor = [dab_prompt, dab_cont], [factor_prompt, factor_cont]
    ffn_blocks, do_prompt = lax.optimization_barrier((ffn_blocks, do_prompt))
    branch_ffn = [None, exchange_sum(ffn_blocks[1])]
    ffn_blocks[0] = tie(ffn_blocks[0], branch_ffn[1])
    branch_ffn[0] = exchange_sum(ffn_blocks[0])
    dq_prompt, dk_prompt, dv_prompt = prompt_backward(
        queries[0], prompt_kv, prompt_o, do_prompt.reshape(queries[0].shape), prompt_lse, start
    )
    dq_prompt = tie(dq_prompt, branch_ffn[1])
    started_out = grad_start(both(attended), both(dab), 1)
    chosen = (local_prompt[:, None] == jnp.arange(groups, dtype=jnp.int32)[None, :]).astype(F32)

    def kv_block(step):
        place = (me_ctx ^ step) * prompt_rows

        def piece(whole):
            return lax.dynamic_slice(
                whole, (0, place, 0), (whole.shape[0], prompt_rows, whole.shape[2])
            )

        def total(prompts, extra):
            extra = piece(extra)
            sums = [
                sum(chosen[c, g] * extra[c] for c in range(conts)) for g in range(groups)
            ]
            return piece(prompts) + jnp.stack(sums)

        return jnp.concatenate(
            [total(dk_prompt, dk_cont), total(dv_prompt, dv_cont)], axis=2
        ).reshape(-1, kv_width)

    sent = [swap(kv_block(step).astype(BF), "ctx", step) for step in range(1, ctx_size)]
    dkv_own = jnp.concatenate([dk_own, dv_own], axis=2).reshape(-1, kv_width)
    finished_cont = finish(
        dq_cont.reshape(-1, query_width), dkv_own, [], query[1], kv[1], tables[1]
    )
    finished = [
        finish(dq_prompt.reshape(-1, query_width), kv_block(0), sent, query[0], kv[0], tables[0]),
        finished_cont,
    ]
    dqkv = [f[0] for f in finished]
    attn_blocks = [
        blocks_of(lambda b, t=t: product_nt(t, rows_of(full_qkv, b, width))) for t in dqkv
    ]
    attn_blocks = tie(attn_blocks, (middle[1], branch_ffn[0], started[2][0]))
    normed_attn_grad = [None, exchange_sum(attn_blocks[1])]
    attn_blocks[0] = tie(attn_blocks[0], normed_attn_grad[1])
    normed_attn_grad[0] = exchange_sum(attn_blocks[0])
    sizes = [t.shape[0] for t in dqkv]
    joined = lambda pair: jnp.concatenate([p.reshape(-1, LANES) for p in pair], axis=0)
    parted = lambda t: [
        p.reshape(-1, 1) for p in jnp.split(t, [sizes[0] // LANES], axis=0)
    ]
    total_attn = parted(all_sum(joined([f[1] for f in finished])))
    qkv_left, qkv_right = tie((both(xn1), both(dqkv)), attn_blocks)
    started_qkv = grad_start(qkv_left, qkv_right, 0)
    middle.append(grad_middle(*started_out, 1))
    middle.append(grad_middle(*started_qkv, 0))
    grad_gate, grad_up, grad_down, grad_out, grad_qkv = [
        grad_end(middle[i], axis) for i, axis in enumerate((0, 0, 1, 1, 0))
    ]

    gain_attn_sum, gain_ffn_sum, router_sum = 0.0, 0.0, 0.0
    outs, token_grads = [], []
    hidden_own = [columns(h, me_tp, width) for h in hidden]
    branch = [
        hidden_own[i] - tokens_in[i].astype(F32) + branch_ffn[i] for i in streams
    ]
    sums = parted(
        all_sum(
            joined(
                [
                    jnp.sum(cots[i].astype(F32) * mixing[i] * branch[i], axis=1, keepdims=True)
                    for i in streams
                ]
            )
        )
    )
    for i in streams:
        x = tokens_in[i].astype(F32)
        dy = cots[i].astype(F32)
        outs.append((x + mixing[i] * branch[i]).astype(BF))
        dl = (1.0 - gate_router[i]) * sums[i]
        router_sum = router_sum + jnp.sum(x * dl, axis=0)
        gain_ffn_sum = gain_ffn_sum + jnp.sum(
            hidden_own[i] * scale_ffn[i] * normed_grad[i], axis=0
        )
        back_ffn = scale_ffn[i] * gains_ffn[0:1] * normed_grad[i] - hidden_own[i] * factor[i]
        scale = scale_attn[i]
        n = normed_attn_grad[i]
        gain_attn_sum = gain_attn_sum + jnp.sum(x * scale * n, axis=0)
        n1 = scale * gains_attn[0:1] * n - x * (scale * scale * total_attn[i] / model_width)
        token_grads.append(dy + dl * routers[0:1] + back_ffn + n1)
    early = group_sum(jnp.stack([gain_ffn_sum, router_sum]))
    small = [group_sum(gain_attn_sum), early[0], early[1]]
    return (
        outs[0].reshape(prompt_in.shape),
        outs[1].reshape(cont_in.shape),
        token_grads[0].reshape(prompt_in.shape),
        token_grads[1].reshape(cont_in.shape),
        small[0],
        small[1],
        small[2],
        grad_qkv[:, :query_width],
        grad_qkv[:, query_width : query_width + key_width],
        grad_qkv[:, query_width + key_width :],
        grad_out,
        grad_gate,
        grad_up,
        grad_down,
    )


def solution(mesh):
    placed = (
        P("fsdp", "ctx", "tp"),
        P(("fsdp", "ctx"), None, "tp"),
        P("fsdp", "ctx"),
        P(("fsdp", "ctx"), None),
        P(("fsdp", "ctx")),
        P(("fsdp", "ctx")),
        P("tp"),
        P("tp"),
        P("tp"),
        P("fsdp", "tp"),
        P("fsdp", "tp"),
        P("fsdp", "tp"),
        P("tp", "fsdp"),
        P("fsdp", "tp"),
        P("fsdp", "tp"),
        P("tp", "fsdp"),
        P("fsdp", "ctx", "tp"),
        P(("fsdp", "ctx"), None, "tp"),
    )
    return jax.shard_map(
        body,
        mesh=mesh,
        in_specs=placed,
        out_specs=(
            P("fsdp", "ctx", "tp"),
            P(("fsdp", "ctx"), None, "tp"),
            P("fsdp", "ctx", "tp"),
            P(("fsdp", "ctx"), None, "tp"),
            P("tp"),
            P("tp"),
            P("tp"),
            P("fsdp", "tp"),
            P("fsdp", "tp"),
            P("fsdp", "tp"),
            P("tp", "fsdp"),
            P("fsdp", "tp"),
            P("fsdp", "tp"),
            P("tp", "fsdp"),
        ),
        check_vma=False,
    )
```

time: 1240 us -> 992 us (0.80)
  waiting for transfers between devices: 507 us -> 283 us
  Pallas kernels: 0 us -> 128 us
  matrix products: 247 us -> 194 us
  local copies, waits for them, and re-layouts: 119 us -> 68.9 us
  starting transfers between devices: 200 us -> 157 us
  blocking collectives: 13 us -> 0 us
    reduce_scatter x5 -> x0, waiting for transfers between devices: 237 us -> none  [the longest x3 161 us: reduce_rows(): lax.psum_scatter(partial_grad.astype(BF), EVERY, scatter_dimension=0, til...]
    pallas_call x0 -> x14, Pallas kernels: none -> 128 us  [the longest x6 39.4 us: placed_call(): pl.pallas_call(kernel, out_shape=[jax.ShapeDtypeStruct((rows, w), d) for...]
    ppermute x69 -> x100, starting transfers between devices: 199 us -> 117 us  [swap(): return lax.ppermute(value, axis, [(i, i ^ step) for i in range(count)])]
    dot_general x14 -> x0, matrix products: 66.3 us -> none  [the longest x2 18.4 us: attend_backward(): jnp.einsum('gqkrd,gskd->gkrqs', grad_split, value_split, preferred_elemen...]
    ppermute x0 -> x30, waiting for transfers between devices: none -> 58.3 us  [the longest x9 48.5 us: gather_tp(): passed = lax.ppermute(second, 'tp', [(2, 3), (1, 0)])]
    ppermute x0 -> x30, starting transfers between devices: none -> 39.3 us  [the longest x6 13.7 us: exchange_sum(): passed = lax.ppermute(blocks[3], 'tp', [(3, 2), (0, 1)])]
    dynamic_update_slice x0 -> x22, local copies, waits for them, and re-layouts: none -> 29.2 us  [the longest x15 19.5 us: put(): lax.dynamic_update_slice(whole, part, (start, 0) if axis == 0 else (0, st...]
    dot_general x22 -> x12, matrix products: 81 us -> 54.7 us  [product(): return jnp.dot(left, right, preferred_element_type=F32)]
  transfers between devices with their start and end apart: 84 -> 131, of which waited for: 29 -> 37; matrix products, arithmetic and copies ran while one was open for 34% -> 35% of each run, Pallas kernels for 0% -> 13%
where the time goes in v2:
time: 992 us; the launch traced here: 980 us
  waiting for transfers between devices  283 us (29%)
  matrix products  194 us (20%)
  starting transfers between devices  157 us (16%)
  other arithmetic  133 us (13%)
  Pallas kernels  128 us (13%)
  local copies, waits for them, and re-layouts  68.9 us (7%)
  between operations  16.6 us (2%)
    ppermute x100, waiting for transfers between devices, swap(): return lax.ppermute(value, axis, [(i, i ^ step) for i in range(count)])  225 us
    ppermute x100, starting transfers between devices, swap(): return lax.ppermute(value, axis, [(i, i ^ step) for i in range(count)])  117 us
    dot_general x28, matrix products, product_nt(): lax.dot_general(left, right, (((1,), (1,)), ((), ())), preferred_element_...  80.8 us
    dot_general x20, matrix products, product_tn(): lax.dot_general(left, right, (((0,), (0,)), ((), ())), preferred_element_...  58.4 us
    dot_general x12, matrix products, product(): return jnp.dot(left, right, preferred_element_type=F32)  54.7 us
    ppermute x9, waiting for transfers between devices, gather_tp(): passed = lax.ppermute(second, 'tp', [(2, 3), (1, 0)])  48.5 us
    pallas_call x6, Pallas kernels, placed_call(): pl.pallas_call(kernel, out_shape=[jax.ShapeDtypeStruct((rows, w), d) for...  39.4 us
    pallas_call x1, Pallas kernels, prompt_backward(): pl.pallas_call(prompt_backward_kernel, out_shape=[jax.ShapeDtypeStruct(qu...  21.6 us
  transfers between devices with their start and end apart: 131, of which 37 were waited for; matrix products, arithmetic and copies ran while one was open for 35% of the time, Pallas kernels for 13%

profile of v2, /device:TPU:0, one launch (start us, length us, event | category | flops | bytes accessed | tf_op | source)
XLA Modules:
  0.0 980.5 jit_solution(5133765807886712188)
XLA Ops:
  39.5 13.8 %collective-permute-done.3.refs_1_ = bf16[512,512]{1,0:T(8,128)(2,1)} collective-permute-done((bf16[512,512]{1,0:T(8,128)(2,1)}, bf16[512,512]{1,0:T(8,128)(2,1)}, u32[]{:S(2)}, u32[]{:S(2)}) %collective-permute-start.3) | collective-permute-done | bytes 524320 | tf_op jit(solution)/shard_map/ppermute | solution.py:33
  90.7 7.6 collective-permute-done.11
  100.1 12.0 %collective-permute-done.6 = bf16[512,512]{1,0:T(8,128)(2,1)S(1)} collective-permute-done((bf16[512,512]{1,0:T(8,128)(2,1)}, bf16[512,512]{1,0:T(8,128)(2,1)S(1)}, u32[]{:S(2)}, u32[]{:S(2)}) %collective-permute-start.6) | collective-permute-done | bytes 524320 | tf_op jit(solution)/shard_map/ppermute | solution.py:56
  133.7 8.2 collective-permute-done.38.refs_2_
  144.9 17.7 %prompt_forward.1 = (bf16[2,256,512]{2,1,0:T(8,128)(2,1)}, f32[2,4,2,256]{3,2,1,0:T(2,128)}) custom-call(s32[1]{0:T(128)} %bitcast.5.start, bf16[2,256,512]{2,1,0:T(8,128)(2,1)} %bitcast.149, bf16[2,1024,256]{2,1,0:T(8,128)(2,1)} %copy-done.83), custom_call_target="tpu_custom_call" | custom-call | flops 2147483648 | bytes 2097152 | tf_op jit(solution)/shard_map/prompt_forward/pallas_call | solution.py:367
  176.3 11.4 %cont_forward.1 = (bf16[2,128,512]{2,1,0:T(8,128)(2,1)}, f32[2,4,1,256]{3,2,1,0:T(1,128)}) custom-call(s32[2]{0:T(128)} %subtract_clamp_fusion.which, bf16[2,128,512]{2,1,0:T(8,128)(2,1)} %bitcast.166, bf16[2,1024,256]{2,1,0:T(8,128)(2,1)} %copy-done.83, bf16[2,128,256]{2,1,0:T(8,128)(2,1)} %bitcast.168), custom_call_target="tpu_custom_call" | custom-call | flops 1207959552 | bytes 1572864 | tf_op jit(solution)/shard_map/cont_forward/pallas_call | solution.py:427
  192.7 10.0 %collective-permute-start.41 = (bf16[256,512]{1,0:T(8,128)(2,1)}, bf16[256,512]{1,0:T(8,128)(2,1)S(1)}, u32[]{:S(2)}, u32[]{:S(2)}) collective-permute-start(bf16[256,512]{1,0:T(8,128)(2,1)} %bitcast.138), channel_id=1, source_target_pairs={{0,1},{1,0},{2,3},{3,2},{4,5},{5,4},{6,7},{7,6},{8,9},{9,8},{10,11... | collective-permute-start | bytes 786440 | tf_op jit(solution)/shard_map/ppermute | solution.py:33
  214.0 8.3 collective-permute-done.42.refs_6_
  271.1 17.1 %collective-permute-done.52 = bf16[256,512]{1,0:T(8,128)(2,1)S(1)} collective-permute-done((bf16[256,512]{1,0:T(8,128)(2,1)S(1)}, bf16[256,512]{1,0:T(8,128)(2,1)S(1)}, u32[]{:S(2)}, u32[]{:S(2)}) %collective-permute-start.52) | collective-permute-done | bytes 262176 | tf_op jit(solution)/shard_map/ppermute | solution.py:56
  299.5 9.3 collective-permute-done.51
  318.6 12.2 %second_norm.2 = (bf16[512,2048]{1,0:T(8,128)(2,1)}, f32[512,2048]{1,0:T(8,128)}, f32[512,1]{1,0:T(8,128)}) custom-call(s32[4]{0:T(128)} %pad_add_fusion.order, bf16[512,512]{1,0:T(8,128)(2,1)} %bitcast.refs_0_, bf16[512,512]{1,0:T(8,128)(2,1)} %collective-permute-done.3.refs_1_, bf16[512,512]{1,0:T(8,128)(2,1)} %collective-permute-done.4.refs_2_, ...), custom_call_target="tpu_custom_call" | custom-call | flops 4311744512 | bytes 4194304 | tf_op jit(solution)/shard_map/second_norm/pallas_call | solution.py:792
  332.5 9.1 second_norm.3
  356.1 9.6 fusion.310
  365.7 9.6 fusion.312
  375.3 11.5 %multiply_convert_fusion.1 = (bf16[512,2048]{1,0:T(8,128)(2,1)S(1)}, bf16[512,2048]{1,0:T(8,128)(2,1)S(1)}, bf16[512,2048]{1,0:T(8,128)(2,1)S(1)}) fusion(f32[512,2048]{1,0:T(8,128)} %fusion.312, f32[512,2048]{1,0:T(8,128)} %fusion.310, bf16[512,2048]{1,0:T(8,128)(2,1)S(1)} %copy-done.52, bf16[2048,2048]{1,0:T(8,128)(2,1)} %constant_dynamic-update-slice_fusion.5), kind=kOutput, calls=%fused_computation.10 | convolution fusion | flops 4311744512 | bytes 25165824 | tf_op jit(solution)/shard_map/dot_general | solution.py:20
  449.2 8.4 collective-permute-done.56
  560.6 16.8 %collective-permute-done.68.refs_6_ = bf16[512,512]{1,0:T(8,128)(2,1)S(1)} collective-permute-done((bf16[512,512]{1,0:T(8,128)(2,1)S(1)}, bf16[512,512]{1,0:T(8,128)(2,1)S(1)}, u32[]{:S(2)}, u32[]{:S(2)}) %collective-permute-start.68) | collective-permute-done | bytes 524320 | tf_op jit(solution)/shard_map/ppermute | solution.py:33
  618.2 19.1 %cont_backward.1 = (f32[2,128,512]{2,1,0:T(8,128)}, f32[2,1024,128]{2,1,0:T(8,128)}, f32[2,1024,128]{2,1,0:T(8,128)}, f32[2,128,128]{2,1,0:T(8,128)}, f32[2,128,128]{2,1,0:T(8,128)}) custom-call(s32[2]{0:T(128)} %subtract_clamp_fusion.which, bf16[2,128,512]{2,1,0:T(8,128)(2,1)} %bitcast.167, bf16[2,1024,256]{2,1,0:T(8,128)(2,1)} %copy-done.83, ...), custom_call_target="tpu_custom_call" | custom-call | flops 3019898880 | bytes 4456448 | tf_op jit(solution)/shard_map/cont_backward/pallas_call | solution.py:649
  647.7 32.3 %collective-permute-done.92 = bf16[1024,1024]{1,0:T(8,128)(2,1)} collective-permute-done((bf16[1024,1024]{1,0:T(8,128)(2,1)}, bf16[1024,1024]{1,0:T(8,128)(2,1)}, u32[]{:S(2)}, u32[]{:S(2)}) %collective-permute-start.92) | collective-permute-done | bytes 2097184 | tf_op jit(solution)/shard_map/ppermute | solution.py:33
  708.8 21.6 %prompt_backward.1 = (f32[2,256,512]{2,1,0:T(8,128)}, f32[2,1024,128]{2,1,0:T(8,128)}, f32[2,1024,128]{2,1,0:T(8,128)}) custom-call(s32[1]{0:T(128)} %bitcast.5.start, bf16[2,256,512]{2,1,0:T(8,128)(2,1)} %bitcast.150, bf16[2,1024,256]{2,1,0:T(8,128)(2,1)} %copy-done.83, bf16[2,256,512]{2,1,0:T(8,128)(2,1)} %get-tuple-element.107.o_ref, ...), custom_call_target="tpu_custom_call" | custom-call | flops 5368709120 | bytes 5767168 | tf_op jit(solution)/shard_map/prompt_backward/pallas_call | solution.py:543
  748.4 9.0 collective-permute-done.78
  815.7 20.1 %collective-permute-done.128 = bf16[1024,512]{1,0:T(8,128)(2,1)} collective-permute-done((bf16[1024,512]{1,0:T(8,128)(2,1)S(1)}, bf16[1024,512]{1,0:T(8,128)(2,1)}, u32[]{:S(2)}, u32[]{:S(2)}) %collective-permute-start.128) | collective-permute-done | bytes 1048608 | tf_op jit(solution)/shard_map/ppermute | solution.py:33
  851.1 9.2 collective-permute-done.94
  901.5 20.7 %collective-permute-done.100 = bf16[512,512]{1,0:T(8,128)(2,1)S(1)} collective-permute-done((bf16[512,512]{1,0:T(8,128)(2,1)}, bf16[512,512]{1,0:T(8,128)(2,1)S(1)}, u32[]{:S(2)}, u32[]{:S(2)}) %collective-permute-start.100) | collective-permute-done | bytes 524320 | tf_op jit(solution)/shard_map/ppermute | solution.py:33
  (771 shorter events, 639.3 us)
Async XLA Ops:
  7.2 358.5 %all-gather.2.cloned.1.call-start = ((), (), s32[]{:S(2)}) async-start(), calls=%async_computation | async-start | bytes 9437184 | tf_op jit(solution)/shard_map/all_gather | solution.py:144
  16.9 67.2 %collective-permute-start.9 = (bf16[3,512]{1,0:T(4,128)(2,1)S(1)}, bf16[3,512]{1,0:T(4,128)(2,1)S(1)}, u32[]{:S(2)}, u32[]{:S(2)}) collective-permute-start(bf16[3,512]{1,0:T(4,128)(2,1)S(1)} %pad_maximum_fusion.21), channel_id=1, source_target_pairs={{0,3},{1,2},{2,1},{3,0},{4,7},{5,6},{6,5},{7,4},{8,11},{9,10},{10,... | collective-permute-start | bytes 9224 | tf_op jit(solution)/shard_map/ppermute | solution.py:33
  17.0 67.1 %collective-permute-start.8 = (bf16[3,512]{1,0:T(4,128)(2,1)S(1)}, bf16[3,512]{1,0:T(4,128)(2,1)S(1)}, u32[]{:S(2)}, u32[]{:S(2)}) collective-permute-start(bf16[3,512]{1,0:T(4,128)(2,1)S(1)} %pad_maximum_fusion.21), channel_id=1, source_target_pairs={{0,2},{1,3},{2,0},{3,1},{4,6},{5,7},{6,4},{7,5},{8,10},{9,11},{10,... | collective-permute-start | bytes 9224 | tf_op jit(solution)/shard_map/ppermute | solution.py:33
  87.7 87.0 %collective-permute-start.29 = (bf16[256,2048]{1,0:T(8,128)(2,1)}, bf16[256,2048]{1,0:T(8,128)(2,1)}, u32[]{:S(2)}, u32[]{:S(2)}) collective-permute-start(bf16[256,2048]{1,0:T(8,128)(2,1)} %constant_dynamic-slice_fusion.2), channel_id=1, source_target_pairs={{0,16},{16,0},{1,17},{17,1},{2,18},{18,2},{3,19},{19,3},{4,20},{20... | collective-permute-start | bytes 3145736 | tf_op jit(solution)/shard_map/ppermute | solution.py:33
  129.8 77.1 %collective-permute-start.22 = (bf16[2048,256]{1,0:T(8,128)(2,1)}, bf16[2048,256]{1,0:T(8,128)(2,1)}, u32[]{:S(2)}, u32[]{:S(2)}) collective-permute-start(bf16[2048,256]{1,0:T(8,128)(2,1)} %get-tuple-element.257), channel_id=1, source_target_pairs={{0,16},{16,0},{1,17},{17,1},{2,18},{18,2},{3,19},{19,3},{4,20},{20... | collective-permute-start | bytes 3145736 | tf_op jit(solution)/shard_map/ppermute | solution.py:33
  174.7 53.5 %collective-permute-start.23 = (bf16[2048,256]{1,0:T(8,128)(2,1)}, bf16[2048,256]{1,0:T(8,128)(2,1)}, u32[]{:S(2)}, u32[]{:S(2)}) collective-permute-start(bf16[2048,256]{1,0:T(8,128)(2,1)} %get-tuple-element.257), channel_id=1, source_target_pairs={{0,8},{4,12},{8,0},{12,4},{1,9},{5,13},{9,1},{13,5},{2,10},{6,14},... | collective-permute-start | bytes 3145736 | tf_op jit(solution)/shard_map/ppermute | solution.py:33
  187.7 44.5 %collective-permute-start.33 = (bf16[256,2048]{1,0:T(8,128)(2,1)}, bf16[256,2048]{1,0:T(8,128)(2,1)}, u32[]{:S(2)}, u32[]{:S(2)}) collective-permute-start(bf16[256,2048]{1,0:T(8,128)(2,1)} %constant_dynamic-slice_fusion.1), channel_id=1, source_target_pairs={{0,16},{16,0},{1,17},{17,1},{2,18},{18,2},{3,19},{19,3},{4,20},{20... | collective-permute-start | bytes 3145736 | tf_op jit(solution)/shard_map/ppermute | solution.py:33
  297.9 48.7 %collective-permute-start.36 = (bf16[256,2048]{1,0:T(8,128)(2,1)}, bf16[256,2048]{1,0:T(8,128)(2,1)}, u32[]{:S(2)}, u32[]{:S(2)}) collective-permute-start(bf16[256,2048]{1,0:T(8,128)(2,1)} %collective-permute-done.34), channel_id=1, source_target_pairs={{0,4},{4,0},{8,12},{12,8},{1,5},{5,1},{9,13},{13,9},{2,6},{6,2},{1... | collective-permute-start | bytes 3145736 | tf_op jit(solution)/shard_map/ppermute | solution.py:33
  461.3 52.4 %collective-permute-start.57 = (bf16[512,512]{1,0:T(8,128)(2,1)}, bf16[512,512]{1,0:T(8,128)(2,1)}, u32[]{:S(2)}, u32[]{:S(2)}) collective-permute-start(bf16[512,512]{1,0:T(8,128)(2,1)} %fusion.140), channel_id=1, source_target_pairs={{1,2},{2,1},{5,6},{6,5},{9,10},{10,9},{13,14},{14,13},{17,18},{18,... | collective-permute-start | bytes 1572872 | tf_op jit(solution)/shard_map/ppermute | solution.py:90
  464.1 49.6 %collective-permute-start.58 = (bf16[512,512]{1,0:T(8,128)(2,1)}, bf16[512,512]{1,0:T(8,128)(2,1)}, u32[]{:S(2)}, u32[]{:S(2)}) collective-permute-start(bf16[512,512]{1,0:T(8,128)(2,1)} %fusion.143), channel_id=1, source_target_pairs={{0,1},{1,0},{2,3},{3,2},{4,5},{5,4},{6,7},{7,6},{8,9},{9,8},{10,11... | collective-permute-start | bytes 1572872 | tf_op jit(solution)/shard_map/ppermute | solution.py:33
  514.2 40.4 %collective-permute-start.90 = (bf16[1024,1024]{1,0:T(8,128)(2,1)}, bf16[1024,1024]{1,0:T(8,128)(2,1)S(1)}, u32[]{:S(2)}, u32[]{:S(2)}) collective-permute-start(bf16[1024,1024]{1,0:T(8,128)(2,1)} %convolution_convert_fusion.1), channel_id=1, source_target_pairs={{0,4},{4,0},{8,12},{12,8},{1,5},{5,1},{9,13},{13,9},{2,6},{6,2},{1... | collective-permute-start | bytes 6291464 | tf_op jit(solution)/shard_map/ppermute | solution.py:33
  541.8 69.8 %collective-permute-start.72 = (bf16[1024,1024]{1,0:T(8,128)(2,1)}, bf16[1024,1024]{1,0:T(8,128)(2,1)}, u32[]{:S(2)}, u32[]{:S(2)}) collective-permute-start(bf16[1024,1024]{1,0:T(8,128)(2,1)} %add_convert_fusion.2), channel_id=1, source_target_pairs={{0,16},{16,0},{1,17},{17,1},{2,18},{18,2},{3,19},{19,3},{4,20},{20... | collective-permute-start | bytes 6291464 | tf_op jit(solution)/shard_map/ppermute | solution.py:33
  554.6 88.0 %collective-permute-start.74 = (bf16[1024,1024]{1,0:T(8,128)(2,1)}, bf16[1024,1024]{1,0:T(8,128)(2,1)}, u32[]{:S(2)}, u32[]{:S(2)}) collective-permute-start(bf16[1024,1024]{1,0:T(8,128)(2,1)} %add_convert_fusion.1), channel_id=1, source_target_pairs={{0,16},{16,0},{1,17},{17,1},{2,18},{18,2},{3,19},{19,3},{4,20},{20... | collective-permute-start | bytes 6291464 | tf_op jit(solution)/shard_map/ppermute | solution.py:33
  559.9 120.1 %collective-permute-start.92 = (bf16[1024,1024]{1,0:T(8,128)(2,1)}, bf16[1024,1024]{1,0:T(8,128)(2,1)}, u32[]{:S(2)}, u32[]{:S(2)}) collective-permute-start(bf16[1024,1024]{1,0:T(8,128)(2,1)} %add_convert_fusion), channel_id=1, source_target_pairs={{0,16},{16,0},{1,17},{17,1},{2,18},{18,2},{3,19},{19,3},{4,20},{20... | collective-permute-start | bytes 6291464 | tf_op jit(solution)/shard_map/ppermute | solution.py:33
  614.8 79.0 %collective-permute-start.73 = (bf16[512,1024]{1,0:T(8,128)(2,1)}, bf16[512,1024]{1,0:T(8,128)(2,1)}, u32[]{:S(2)}, u32[]{:S(2)}) collective-permute-start(bf16[512,1024]{1,0:T(8,128)(2,1)} %add_convert_fusion.8), channel_id=1, source_target_pairs={{0,8},{4,12},{8,0},{12,4},{1,9},{5,13},{9,1},{13,5},{2,10},{6,14},... | collective-permute-start | bytes 3145736 | tf_op jit(solution)/shard_map/ppermute | solution.py:33
  646.1 91.5 %collective-permute-start.91 = (bf16[512,1024]{1,0:T(8,128)(2,1)}, bf16[512,1024]{1,0:T(8,128)(2,1)}, u32[]{:S(2)}, u32[]{:S(2)}) collective-permute-start(bf16[512,1024]{1,0:T(8,128)(2,1)} %add_convert_fusion.6), channel_id=1, source_target_pairs={{0,8},{4,12},{8,0},{12,4},{1,9},{5,13},{9,1},{13,5},{2,10},{6,14},... | collective-permute-start | bytes 3145736 | tf_op jit(solution)/shard_map/ppermute | solution.py:33
  681.6 60.6 %collective-permute-start.127 = (bf16[1024,512]{1,0:T(8,128)(2,1)S(1)}, bf16[1024,512]{1,0:T(8,128)(2,1)}, u32[]{:S(2)}, u32[]{:S(2)}) collective-permute-start(bf16[1024,512]{1,0:T(8,128)(2,1)S(1)} %add_convert_fusion.4), channel_id=1, source_target_pairs={{0,8},{4,12},{8,0},{12,4},{1,9},{5,13},{9,1},{13,5},{2,10},{6,14},... | collective-permute-start | bytes 3145736 | tf_op jit(solution)/shard_map/ppermute | solution.py:33
  705.8 41.7 %collective-permute-start.75 = (bf16[256,512]{1,0:T(8,128)(2,1)}, bf16[256,512]{1,0:T(8,128)(2,1)}, u32[]{:S(2)}, u32[]{:S(2)}) collective-permute-start(bf16[256,512]{1,0:T(8,128)(2,1)} %fusion.185), channel_id=1, source_target_pairs={{1,2},{2,1},{5,6},{6,5},{9,10},{10,9},{13,14},{14,13},{17,18},{18,... | collective-permute-start | bytes 786440 | tf_op jit(solution)/shard_map/ppermute | solution.py:90
  707.3 96.2 %collective-permute-start.122 = (bf16[512,1024]{1,0:T(8,128)(2,1)}, bf16[512,1024]{1,0:T(8,128)(2,1)}, u32[]{:S(2)}, u32[]{:S(2)}) collective-permute-start(bf16[512,1024]{1,0:T(8,128)(2,1)} %add_convert_fusion.7), channel_id=1, source_target_pairs={{0,8},{4,12},{8,0},{12,4},{1,9},{5,13},{9,1},{13,5},{2,10},{6,14},... | collective-permute-start | bytes 3145736 | tf_op jit(solution)/shard_map/ppermute | solution.py:33
  787.8 48.0 %collective-permute-start.128 = (bf16[1024,512]{1,0:T(8,128)(2,1)S(1)}, bf16[1024,512]{1,0:T(8,128)(2,1)}, u32[]{:S(2)}, u32[]{:S(2)}) collective-permute-start(bf16[1024,512]{1,0:T(8,128)(2,1)S(1)} %copy-done.34), channel_id=1, source_target_pairs={{0,8},{4,12},{8,0},{12,4},{1,9},{5,13},{9,1},{13,5},{2,10},{6,14},... | collective-permute-start | bytes 3145736 | tf_op jit(solution)/shard_map/ppermute | solution.py:33
  794.5 43.2 %collective-permute-start.79 = (bf16[512,512]{1,0:T(8,128)(2,1)}, bf16[512,512]{1,0:T(8,128)(2,1)S(1)}, u32[]{:S(2)}, u32[]{:S(2)}) collective-permute-start(bf16[512,512]{1,0:T(8,128)(2,1)} %fusion.125), channel_id=1, source_target_pairs={{1,2},{2,1},{5,6},{6,5},{9,10},{10,9},{13,14},{14,13},{17,18},{18,... | collective-permute-start | bytes 1572872 | tf_op jit(solution)/shard_map/ppermute | solution.py:90
  835.8 51.2 %collective-permute-start.123 = (bf16[1024,1024]{1,0:T(8,128)(2,1)S(1)}, bf16[1024,1024]{1,0:T(8,128)(2,1)S(1)}, u32[]{:S(2)}, u32[]{:S(2)}) collective-permute-start(bf16[1024,1024]{1,0:T(8,128)(2,1)S(1)} %pad_maximum_fusion.6), channel_id=1, source_target_pairs={{0,4},{4,0},{8,12},{12,8},{1,5},{5,1},{9,13},{13,9},{2,6},{6,2},{1... | collective-permute-start | bytes 6291464 | tf_op jit(solution)/shard_map/ppermute | solution.py:33
  837.2 58.1 %collective-permute-start.125 = (bf16[1024,1024]{1,0:T(8,128)(2,1)S(1)}, bf16[1024,1024]{1,0:T(8,128)(2,1)S(1)}, u32[]{:S(2)}, u32[]{:S(2)}) collective-permute-start(bf16[1024,1024]{1,0:T(8,128)(2,1)S(1)} %pad_maximum_fusion.7), channel_id=1, source_target_pairs={{0,4},{4,0},{8,12},{12,8},{1,5},{5,1},{9,13},{13,9},{2,6},{6,2},{1... | collective-permute-start | bytes 6291464 | tf_op jit(solution)/shard_map/ppermute | solution.py:33
  878.6 50.2 %collective-permute-start.129 = (bf16[1024,1024]{1,0:T(8,128)(2,1)S(1)}, bf16[1024,1024]{1,0:T(8,128)(2,1)S(1)}, u32[]{:S(2)}, u32[]{:S(2)}) collective-permute-start(bf16[1024,1024]{1,0:T(8,128)(2,1)S(1)} %pad_maximum_fusion.8), channel_id=1, source_target_pairs={{0,4},{4,0},{8,12},{12,8},{1,5},{5,1},{9,13},{13,9},{2,6},{6,2},{1... | collective-permute-start | bytes 6291464 | tf_op jit(solution)/shard_map/ppermute | solution.py:33
  (247 other events, 4172.8 us)
Sparse Core Ops, SparseCore 0:
  61.2 76.2 all-gather.1

commit v3 on v2

--- a/solution.py
+++ b/solution.py
@@ -46,16 +46,17 @@
     return (me == 1) | (me == 2)
 
 
-def gather_tp(value):
+def gather_tp(value, before=None):
     if lax.axis_size("tp") != 4:
         parts = pieces_of(value)
         return parts, parts[1:]
     second = swap(value, "tp", 2)
     first = swap(value, "tp", 1)
     middle = lax.ppermute(value, "tp", [(1, 2), (2, 1)])
-    passed = lax.ppermute(second, "tp", [(2, 3), (1, 0)])
+    ready = tie(second, first if before is None else (first, before))
+    passed = lax.ppermute(ready, "tp", [(2, 3), (1, 0)])
     third = jnp.where(inner_pair(), middle, passed)
-    return [value, first, second, third], [first, second, middle]
+    return [value, first, second, third], [first, second, middle, passed]
 
 
 def all_sum(value, axis="tp"):
@@ -82,19 +83,30 @@
     return [blocks[0], blocks[1].astype(BF), blocks[2], blocks[3].astype(BF)]
 
 
-def exchange_sum(blocks):
+def exchange_direct(blocks):
+    sent = [swap(block.astype(BF), "tp", step) for step, block in enumerate(blocks) if step > 0]
+    total = blocks[0]
+    for part in sent:
+        total = total + part.astype(F32)
+    return total, sent
+
+
+def exchange_sum(blocks, after=()):
     if len(blocks) != 4:
         sent = [swap(block, "tp", step) for step, block in enumerate(blocks) if step > 0]
+        early, phase = sent[0], sent
     else:
         passed = lax.ppermute(blocks[3], "tp", [(3, 2), (0, 1)])
         middle = lax.ppermute(blocks[3], "tp", [(1, 2), (2, 1)])
         first = swap(blocks[1], "tp", 1)
-        relay = (blocks[2] + passed.astype(F32)).astype(BF)
-        sent = [middle, first, swap(relay, "tp", 2)]
+        phase = [passed, middle, first]
+        passed, middle, first = tie(phase, after)
+        early = (blocks[2] + passed.astype(F32)).astype(BF)
+        sent = [middle, first, swap(early, "tp", 2)]
     total = blocks[0]
     for part in sent:
         total = total + part.astype(F32)
-    return total
+    return total, early, phase
 
 
 def columns(matrix, block, width):
@@ -116,51 +128,71 @@
 def gather_weight(weight, axis, after=None):
     me = lax.axis_index("ctx")
     size = weight.shape[axis] // lax.axis_size("ctx")
-    quarter = cut_of(weight, axis, me, size)
     if not paired():
-        return lax.all_gather(quarter, EVERY, axis=axis, tiled=True), quarter
+        quarter = cut_of(weight, axis, me, size)
+        return [quarter] * 2, lambda after: lax.all_gather(quarter, EVERY, axis=axis, tiled=True)
     if after is not None:
-        quarter = tie(quarter, after)
+        weight = tie(weight, after)
     mine = lax.axis_index("fsdp")
-    far = swap(quarter, "fsdp", 1)
+    far = swap(cut_of(weight, axis, me, size), "fsdp", 1)
     across = swap(far, "ctx", 2)
     found = [(0, far), (2, across), (1, swap(far, "ctx", 1)), (3, swap(across, "ctx", 1))]
     shape = list(weight.shape)
     shape[axis] *= 2
-    whole = jnp.zeros(shape, weight.dtype)
-
-    def put(whole, part, start):
-        return lax.dynamic_update_slice(whole, part, (start, 0) if axis == 0 else (0, start))
-
-    whole = put(whole, weight, mine * size * 4)
-    for step, part in found:
-        whole = put(whole, part, ((1 - mine) * 4 + (me ^ step)) * size)
-    return whole, far
-
-
-def gather_weight_offload(weight, axis, after):
-    size = weight.shape[axis] // lax.axis_size("ctx")
-    quarter = tie(cut_of(weight, axis, lax.axis_index("ctx"), size), after)
-    return lax.all_gather(quarter, EVERY, axis=axis, tiled=True)
-
-
-def gather_out(weight):
+    at = lambda start: (start, 0) if axis == 0 else (0, start)
+
+    def whole(after):
+        own = weight if after is None else tie(weight, after)
+        result = lax.dynamic_update_slice(
+            jnp.zeros(shape, weight.dtype), own, at(mine * size * 4)
+        )
+        for step, part in found:
+            result = lax.dynamic_update_slice(
+                result, part, at(((1 - mine) * 4 + (me ^ step)) * size)
+            )
+        return result
+
+    return [far, across], whole
+
+
+def gather_out(weight, after):
     if not paired():
         pieces, done = gather_tp(lax.all_gather(weight, "fsdp", axis=1, tiled=True))
-        return jnp.concatenate(pieces, axis=0), done
+        return done, pieces, lambda after: jnp.concatenate(pieces, axis=0)
     me = lax.axis_index("ctx")
     mine = lax.axis_index("fsdp")
     size = weight.shape[1] // lax.axis_size("ctx")
-    pieces, done = gather_tp(columns(weight, me, size))
+    pieces, done = gather_tp(tie(columns(weight, me, size), after))
     own = jnp.concatenate(pieces, axis=0)
     far = swap(own, "fsdp", 1)
-    found = [(mine, 0, own), (1 - mine, 0, far)]
-    found += [(mine, 2, swap(own, "ctx", 2)), (1 - mine, 2, swap(far, "ctx", 2))]
+    across = swap(own, "ctx", 2)
+    far_across = swap(across, "fsdp", 1)
+    found = [(mine, 0, own), (1 - mine, 0, far), (mine, 2, across), (1 - mine, 2, far_across)]
     found += [(f, step ^ 1, swap(part, "ctx", 1)) for f, step, part in found]
-    whole = jnp.zeros((own.shape[0], size * 8), weight.dtype)
-    for f, step, part in found:
-        whole = lax.dynamic_update_slice(whole, part, (0, (f * 4 + (me ^ step)) * size))
-    return whole, done
+
+    def whole(after):
+        result = jnp.zeros((own.shape[0], size * 8), weight.dtype)
+        for f, step, part in found:
+            result = lax.dynamic_update_slice(result, part, (0, (f * 4 + (me ^ step)) * size))
+        return result
+
+    return done, [far, across, far_across], whole
+
+
+def scatter_grad(part, axis):
+    return lax.psum_scatter(part, EVERY, scatter_dimension=axis, tiled=True)
+
+
+def spread_grad(piece, across, axis):
+    if not paired():
+        return lax.all_gather(piece, "ctx", axis=axis, tiled=True).astype(F32)
+    low_side = lax.axis_index("ctx") // 2 == 0
+    low_core = lax.axis_index("ctx") % 2 == 0
+    pair = [jnp.where(low_side, piece, across), jnp.where(low_side, across, piece)]
+    parts = []
+    for mine, theirs in zip(pair, [swap(p, "ctx", 1) for p in pair]):
+        parts += [jnp.where(low_core, mine, theirs), jnp.where(low_core, theirs, mine)]
+    return jnp.concatenate(parts, axis=axis).astype(F32)
 
 
 def grad_start(left, right, axis):
@@ -175,8 +207,9 @@
     other_far, other_own = half(other, 1 - core), half(other, core)
     dot = lambda s, t: product_tn(s, t) if axis == 0 else product_tn(t, s)
     first = swap(dot(split_far, other_far).astype(BF), "ctx", 1)
+    far = (dot(split_far, other_own) + first.astype(F32)).astype(BF)
+    split_own = tie(split_own, far)
     second = swap(dot(split_own, other_far).astype(BF), "ctx", 1)
-    far = (dot(split_far, other_own) + first.astype(F32)).astype(BF)
     kept = dot(split_own, other_own) + second.astype(F32)
     return swap(far, "fsdp", 1), kept, far
 
@@ -893,20 +926,22 @@
     start = (me_ctx * prompt_rows).astype(jnp.int32)[None]
     order = jnp.stack([me_tp ^ step for step in range(tp_size)]).astype(jnp.int32)
 
-    full_qkv, qkv_far = gather_weight(
+    qkv_moves, lay_qkv = gather_weight(
         jnp.concatenate([w_query, key_projection, w_value], axis=1), 0
     )
-    params = [p.astype(F32) for p in pieces_of(jnp.stack([gain_attn, gain_ffn, router]))]
+    x_prompt, sent_prompt = gather_tp(tokens_in[0], qkv_moves[0])
+    full_qkv = lay_qkv(None)
+    small_params = tie(jnp.stack([gain_attn, gain_ffn, router]), x_prompt[2])
+    params = [p.astype(F32) for p in pieces_of(small_params)]
     gains_attn = jnp.stack([p[0] for p in params])
     gains_ffn = jnp.stack([p[1] for p in params])
     routers = jnp.stack([p[2] for p in params])
-    full_out, sent_out = gather_out(w_out)
-    x_prompt, sent_prompt = gather_tp(tie(tokens_in[0], sent_out))
-    x_cont, sent_cont = gather_tp(tie(tokens_in[1], sent_prompt))
-    x_parts = [x_prompt, x_cont]
-    full_gate, gate_far = gather_weight(w_gate, 0, qkv_far)
-    full_up, up_far = gather_weight(w_up, 0, gate_far)
-    full_down = gather_weight_offload(w_down, 1, sent_prompt)
+    gate_moves, lay_gate = gather_weight(w_gate, 0, qkv_moves[0])
+    up_moves, lay_up = gather_weight(w_up, 0, gate_moves[0])
+    down_moves, lay_down = gather_weight(w_down, 1, up_moves[0])
+    sent_out, out_moves, lay_out = gather_out(w_out, sent_prompt)
+    x_cont, sent_cont = gather_tp(tie(tokens_in[1], sent_out))
+    x_parts = [x_prompt, tie(x_cont, out_moves[1])]
 
     def enter(i):
         return entry(
@@ -918,6 +953,11 @@
     prompt_kv = jnp.zeros((groups, prompt_rows * ctx_size, kv_width), BF)
     for step, part in enumerate(pieces_of(own_kv, "ctx")):
         prompt_kv = lax.dynamic_update_slice(prompt_kv, part, (0, (me_ctx ^ step) * prompt_rows, 0))
+    query = [tie(query[0], (sent_out, up_moves[0])), tie(query[1], (gate_moves[1], down_moves[0]))]
+    full_out = lay_out(xn1[0])
+    full_gate = lay_gate(xn1[0])
+    full_up = lay_up(xn1[1])
+    full_down = lay_down(xn1[1])
     queries = [
         query[0].reshape(groups, prompt_rows, query_width),
         query[1].reshape(conts, CONTINUATION_LEN, query_width),
@@ -927,23 +967,38 @@
     cont_o, cont_lse = cont_forward(queries[1], prompt_kv, cont_kv, local_prompt)
     attended = [prompt_o.reshape(-1, query_width), cont_o.reshape(-1, query_width)]
     o_prompt, sent_prompt = gather_tp(attended[0])
-    o_cont, sent_cont = gather_tp(tie(attended[1], sent_prompt))
+    o_cont, sent_cont = gather_tp(
+        tie(attended[1], (sent_prompt, out_moves, up_moves[1]))
+    )
+
+    def second(i, o):
+        return second_norm(x_parts[i], o, gains_ffn, full_out, order)
+
+    xn2_prompt, hidden_prompt, scale_prompt = second(0, o_prompt)
     cot_cont, sent_cont = gather_tp(tie(cots[1], sent_cont))
-    cot_prompt, sent_prompt = gather_tp(tie(cots[0], sent_cont))
-    o_parts, cot_parts = [o_prompt, o_cont], [cot_prompt, cot_cont]
-
-    xn2, hidden, scale_ffn = zip(
-        *[second_norm(x_parts[i], o_parts[i], gains_ffn, full_out, order) for i in streams]
-    )
+    xn2_cont, hidden_cont, scale_cont = second(1, o_cont)
+    xn2, hidden, scale_ffn = (
+        [xn2_prompt, xn2_cont],
+        [hidden_prompt, hidden_cont],
+        [scale_prompt, scale_cont],
+    )
+
+    def forward(i):
+        g = product(xn2[i], full_gate)
+        u = product(xn2[i], full_up)
+        s = jax.nn.sigmoid(g)
+        return g, u, s, (g * s * u).astype(BF)
+
+    ahead = [forward(0), forward(1)]
+    cot_prompt, sent_prompt = gather_tp(tie(cots[0], (sent_cont, ahead[0][3], xn2_cont, down_moves[1])))
+    cot_parts = [cot_prompt, cot_cont]
 
     inner, gate_grad, up_grad = [None, None], [None, None], [None, None]
     ffn_grad, blocks = [None, None], [None, None]
     for i in (1, 0):
-        g = product(xn2[i], full_gate)
-        u = product(xn2[i], full_up)
-        s = jax.nn.sigmoid(g)
-        inner[i] = (g * s * u).astype(BF)
-        ffn_grad[i] = spread(cot_parts[i], mixing[i], order)
+        g, u, s, inner[i] = ahead[i]
+        mix = mixing[i] if i == 1 else tie(mixing[i], blocks[1])
+        ffn_grad[i] = spread(cot_parts[i], mix, order)
         dz = product_nt(ffn_grad[i], full_down)
         gate_grad[i] = (dz * u * s * (1.0 + g * (1.0 - s))).astype(BF)
         up_grad[i] = (dz * g * s).astype(BF)
@@ -951,24 +1006,27 @@
             lambda b, i=i: product_nt(gate_grad[i], rows_of(full_gate, b, width))
             + product_nt(up_grad[i], rows_of(full_up, b, width))
         )
+        if i == 1:
+            cont_sum, sent_cont = exchange_direct(blocks[1])
 
     both = lambda pair: jnp.concatenate(pair, axis=0)
-    normed_grad = [None, exchange_sum(blocks[1])]
-    blocks[0], normed_grad[1] = lax.optimization_barrier((blocks[0], normed_grad[1]))
-    normed_grad[0] = exchange_sum(blocks[0])
-    n_cont, sent_cont = gather_tp(normed_grad[1].astype(BF))
-    xn2_all, ffn_grad_all, inner_all, gate_all, up_all = tie(
-        (both(xn2), both(ffn_grad), both(inner), both(gate_grad), both(up_grad)), blocks[0]
-    )
-    started = [
-        grad_start(xn2_all, gate_all, 0),
-        grad_start(xn2_all, up_all, 0),
-        grad_start(inner_all, ffn_grad_all, 1),
+    normed_grad = [None, cont_sum]
+    blocks[0] = tie(blocks[0], cont_sum)
+    normed_grad[0], sent_prompt = exchange_direct(blocks[0])
+    n_cont = pieces_of(normed_grad[1].astype(BF))
+    xn2_all, gate_all, up_all, inner_all, ffn_grad_all = tie(
+        (both(xn2), both(gate_grad), both(up_grad), both(inner), both(ffn_grad)), blocks[0]
+    )
+    parts = [
+        product_tn(xn2_all, gate_all).astype(BF),
+        product_tn(xn2_all, up_all).astype(BF),
+        product_tn(inner_all, ffn_grad_all).astype(BF),
     ]
-    late = tie(normed_grad[0].astype(BF), (sent_cont, [s[2] for s in started]))
-    n_prompt, sent_prompt = gather_tp(late)
+    pieces = [scatter_grad(part, axis) for part, axis in zip(parts, (0, 0, 1))]
+    late = tie(normed_grad[0].astype(BF), (n_cont, parts))
+    n_prompt = pieces_of(late)
     n_parts = [n_prompt, n_cont]
-    inner_late = tie(inner, normed_grad[0])
+    inner_late = tie(inner, parts)
     ffn_blocks = [
         blocks_of(lambda b, t=t: product(t, columns(full_down, b, width))) for t in inner_late
     ]
@@ -978,9 +1036,7 @@
             hidden[i], cot_parts[i], n_parts[i], gains_ffn, scale_ffn[i], mixing[i], order
         )
 
-    middle = [grad_middle(*started[i], axis) for i, axis in enumerate((0, 0, 1))]
     dab_cont, factor_cont = third(1)
-    dab_cont = tie(dab_cont, started[0][0])
     do_cont = product_nt(dab_cont, full_out[:query_width]).astype(BF)
     dq_cont, dk_cont, dv_cont, dk_own, dv_own = cont_backward(
         queries[1],
@@ -992,18 +1048,18 @@
         local_prompt,
     )
     dab_prompt, factor_prompt = third(0)
-    dab_prompt = tie(dab_prompt, (middle[0], started[1][0]))
     do_prompt = product_nt(dab_prompt, full_out[:query_width]).astype(BF)
     dab, factor = [dab_prompt, dab_cont], [factor_prompt, factor_cont]
-    ffn_blocks, do_prompt = lax.optimization_barrier((ffn_blocks, do_prompt))
-    branch_ffn = [None, exchange_sum(ffn_blocks[1])]
-    ffn_blocks[0] = tie(ffn_blocks[0], branch_ffn[1])
-    branch_ffn[0] = exchange_sum(ffn_blocks[0])
+    ffn_blocks = tie(ffn_blocks, n_prompt)
+    branch_ffn = [None, None]
+    branch_ffn[1], sent_cont = exchange_direct(ffn_blocks[1])
+    branch_ffn[0], sent_prompt = exchange_direct(ffn_blocks[0])
+    across = [swap(p, "ctx", 2) if paired() else p for p in pieces]
     dq_prompt, dk_prompt, dv_prompt = prompt_backward(
         queries[0], prompt_kv, prompt_o, do_prompt.reshape(queries[0].shape), prompt_lse, start
     )
     dq_prompt = tie(dq_prompt, branch_ffn[1])
-    started_out = grad_start(both(attended), both(dab), 1)
+    started_out = grad_start(both(attended), tie(both(dab), dq_prompt), 1)
     chosen = (local_prompt[:, None] == jnp.arange(groups, dtype=jnp.int32)[None, :]).astype(F32)
 
     def kv_block(step):
@@ -1038,22 +1094,22 @@
     attn_blocks = [
         blocks_of(lambda b, t=t: product_nt(t, rows_of(full_qkv, b, width))) for t in dqkv
     ]
-    attn_blocks = tie(attn_blocks, (middle[1], branch_ffn[0], started[2][0]))
-    normed_attn_grad = [None, exchange_sum(attn_blocks[1])]
-    attn_blocks[0] = tie(attn_blocks[0], normed_attn_grad[1])
-    normed_attn_grad[0] = exchange_sum(attn_blocks[0])
+    qkv_left, qkv_right = tie((both(xn1), both(dqkv)), attn_blocks)
+    started_qkv = grad_start(qkv_left, qkv_right, 0)
+    normed_attn_grad = [None, None]
+    normed_attn_grad[1], relay_cont, _ = exchange_sum(
+        tie(attn_blocks[1], sent_prompt), across[0]
+    )
     sizes = [t.shape[0] for t in dqkv]
     joined = lambda pair: jnp.concatenate([p.reshape(-1, LANES) for p in pair], axis=0)
     parted = lambda t: [
         p.reshape(-1, 1) for p in jnp.split(t, [sizes[0] // LANES], axis=0)
     ]
     total_attn = parted(all_sum(joined([f[1] for f in finished])))
-    qkv_left, qkv_right = tie((both(xn1), both(dqkv)), attn_blocks)
-    started_qkv = grad_start(qkv_left, qkv_right, 0)
-    middle.append(grad_middle(*started_out, 1))
-    middle.append(grad_middle(*started_qkv, 0))
-    grad_gate, grad_up, grad_down, grad_out, grad_qkv = [
-        grad_end(middle[i], axis) for i, axis in enumerate((0, 0, 1, 1, 0))
+    grad_out = grad_end(grad_middle(*started_out, 1), 1)
+    grad_qkv = grad_end(grad_middle(*started_qkv, 0), 0)
+    grad_gate, grad_up, grad_down = [
+        spread_grad(piece, far, axis) for piece, far, axis in zip(pieces, across, (0, 0, 1))
     ]
 
     gain_attn_sum, gain_ffn_sum, router_sum = 0.0, 0.0, 0.0
@@ -1072,6 +1128,10 @@
             )
         )
     )
+    normed_attn_grad[0] = exchange_sum(
+        tie(attn_blocks[0], (relay_cont, branch_ffn[0])),
+        (sums, total_attn, across[1]),
+    )[0]
     for i in streams:
         x = tokens_in[i].astype(F32)
         dy = cots[i].astype(F32)
@@ -1087,8 +1147,7 @@
         gain_attn_sum = gain_attn_sum + jnp.sum(x * scale * n, axis=0)
         n1 = scale * gains_attn[0:1] * n - x * (scale * scale * total_attn[i] / model_width)
         token_grads.append(dy + dl * routers[0:1] + back_ffn + n1)
-    early = group_sum(jnp.stack([gain_ffn_sum, router_sum]))
-    small = [group_sum(gain_attn_sum), early[0], early[1]]
+    small = group_sum(jnp.stack([gain_attn_sum, gain_ffn_sum, router_sum]))
     return (
         outs[0].reshape(prompt_in.shape),
         outs[1].reshape(cont_in.shape),

time: 992 us -> 913 us (0.920)
  waiting for transfers between devices: 283 us -> 245 us
  other arithmetic: 133 us -> 108 us
  matrix products: 194 us -> 179 us
    ppermute x9 -> x7, waiting for transfers between devices: 48.5 us -> 20.5 us  [gather_tp(): passed = lax.ppermute(ready, 'tp', [(2, 3), (1, 0)])]
    dot_general x20 -> x11, matrix products: 58.4 us -> 42.3 us  [product_tn(): lax.dot_general(left, right, (((0,), (0,)), ((), ())), preferred_element_...]
    convert_element_type x5 -> x2, other arithmetic: 16.7 us -> 1.78 us  [grad_end(): return in_order(own, swap(own, 'ctx', 1), core, 1 - axis).astype(F32)]
    select_n x0 -> x9, other arithmetic: none -> 13.7 us  [the longest x3 7.15 us: spread_grad(): jnp.where(low_side, piece, across)]
    convert_element_type x7, other arithmetic: 7.66 us -> 19.9 us  [the longest x3 11.8 us: spread_grad(): return jnp.concatenate(parts, axis=axis).astype(F32)]
    dynamic_update_slice x22 -> x27, local copies, waits for them, and re-layouts: 29.2 us -> 33.7 us  [the longest x16 19.4 us: whole(): lax.dynamic_update_slice(result, part, at(((1 - mine) * 4 + (me ^ step))...]
    ppermute x100 -> x98, starting transfers between devices: 117 us -> 119 us  [swap(): return lax.ppermute(value, axis, [(i, i ^ step) for i in range(count)])]
    ppermute x100 -> x98, waiting for transfers between devices: 225 us -> 225 us  [swap(): return lax.ppermute(value, axis, [(i, i ^ step) for i in range(count)])]
  transfers between devices with their start and end apart: 131 -> 119, of which waited for: 37 -> 38; matrix products, arithmetic and copies ran while one was open for 35% -> 37% of each run, Pallas kernels for 13% -> 14%
where the time goes in v3:
time: 913 us; the launch traced here: 904 us
  waiting for transfers between devices  245 us (27%)
  matrix products  179 us (20%)
  starting transfers between devices  150 us (16%)
  Pallas kernels  129 us (14%)
  other arithmetic  108 us (12%)
  local copies, waits for them, and re-layouts  76.4 us (8%)
  between operations  16.3 us (2%)
    ppermute x98, waiting for transfers between devices, swap(): return lax.ppermute(value, axis, [(i, i ^ step) for i in range(count)])  225 us
    ppermute x98, starting transfers between devices, swap(): return lax.ppermute(value, axis, [(i, i ^ step) for i in range(count)])  119 us
    dot_general x28, matrix products, product_nt(): lax.dot_general(left, right, (((1,), (1,)), ((), ())), preferred_element_...  76.8 us
    dot_general x12, matrix products, product(): return jnp.dot(left, right, preferred_element_type=F32)  59.5 us
    dot_general x11, matrix products, product_tn(): lax.dot_general(left, right, (((0,), (0,)), ((), ())), preferred_element_...  42.3 us
    pallas_call x6, Pallas kernels, placed_call(): pl.pallas_call(kernel, out_shape=[jax.ShapeDtypeStruct((rows, w), d) for...  40.6 us
    pallas_call x1, Pallas kernels, prompt_backward(): pl.pallas_call(prompt_backward_kernel, out_shape=[jax.ShapeDtypeStruct(qu...  21.6 us
    ppermute x7, waiting for transfers between devices, gather_tp(): passed = lax.ppermute(ready, 'tp', [(2, 3), (1, 0)])  20.5 us
  transfers between devices with their start and end apart: 119, of which 38 were waited for; matrix products, arithmetic and copies ran while one was open for 37% of the time, Pallas kernels for 14%

profile of v3, /device:TPU:0, one launch (start us, length us, event | category | flops | bytes accessed | tf_op | source)
XLA Modules:
  0.0 903.9 jit_solution(6395456124923793483)
XLA Ops:
  57.1 14.1 %collective-permute-done.4 = bf16[512,512]{1,0:T(8,128)(2,1)S(1)} collective-permute-done((bf16[512,512]{1,0:T(8,128)(2,1)}, bf16[512,512]{1,0:T(8,128)(2,1)S(1)}, u32[]{:S(2)}, u32[]{:S(2)}) %collective-permute-start.4) | collective-permute-done | bytes 524320 | tf_op jit(solution)/shard_map/ppermute | solution.py:57
  131.4 17.6 %prompt_forward.1 = (bf16[2,256,512]{2,1,0:T(8,128)(2,1)}, f32[2,4,2,256]{3,2,1,0:T(2,128)}) custom-call(s32[1]{0:T(128)} %bitcast.5.start, bf16[2,256,512]{2,1,0:T(8,128)(2,1)} %bitcast.178, bf16[2,1024,256]{2,1,0:T(8,128)(2,1)} %copy-done.70), custom_call_target="tpu_custom_call" | custom-call | flops 2147483648 | bytes 2097152 | tf_op jit(solution)/shard_map/prompt_forward/pallas_call | solution.py:400
  191.5 11.4 %cont_forward.1 = (bf16[2,128,512]{2,1,0:T(8,128)(2,1)}, f32[2,4,1,256]{3,2,1,0:T(1,128)}) custom-call(s32[2]{0:T(128)} %subtract_clamp_fusion.which, bf16[2,128,512]{2,1,0:T(8,128)(2,1)} %bitcast.187, bf16[2,1024,256]{2,1,0:T(8,128)(2,1)} %copy-done.70, bf16[2,128,256]{2,1,0:T(8,128)(2,1)} %bitcast.189), custom_call_target="tpu_custom_call" | custom-call | flops 1207959552 | bytes 1572864 | tf_op jit(solution)/shard_map/cont_forward/pallas_call | solution.py:460
  210.8 7.7 collective-permute-done.42.refs_5_
  243.5 11.8 %collective-permute-done.47.refs_2_ = bf16[256,512]{1,0:T(8,128)(2,1)S(1)} collective-permute-done((bf16[256,512]{1,0:T(8,128)(2,1)S(1)}, bf16[256,512]{1,0:T(8,128)(2,1)S(1)}, u32[]{:S(2)}, u32[]{:S(2)}) %collective-permute-start.47) | collective-permute-done | bytes 262176 | tf_op jit(solution)/shard_map/ppermute | solution.py:33
  263.1 12.2 %second_norm.2 = (bf16[512,2048]{1,0:T(8,128)(2,1)}, f32[512,2048]{1,0:T(8,128)}, f32[512,1]{1,0:T(8,128)}) custom-call(s32[4]{0:T(128)} %pad_add_fusion.order, bf16[512,512]{1,0:T(8,128)(2,1)} %bitcast.142, bf16[512,512]{1,0:T(8,128)(2,1)} %collective-permute-done.refs_1_, bf16[512,512]{1,0:T(8,128)(2,1)} %collective-permute-done.1.refs_2_, ...), custom_call_target="tpu_custom_call" | custom-call | flops 4311744512 | bytes 4194304 | tf_op jit(solution)/shard_map/second_norm/pallas_call | solution.py:825
  275.4 7.7 fusion.227
  285.1 10.1 %multiply_convert_fusion.2 = (bf16[512,2048]{1,0:T(8,128)(2,1)S(1)}, f32[512,2048]{1,0:T(8,128)}) fusion(f32[512,2048]{1,0:T(8,128)S(1)} %fusion.227, bf16[512,2048]{1,0:T(8,128)(2,1)S(1)} %copy-done.45, bf16[2048,2048]{1,0:T(8,128)(2,1)} %constant_dynamic-update-slice_fusion.5), kind=kOutput, calls=%fused_computation.8 | convolution fusion | flops 4301258752 | bytes 20971520 | tf_op jit(solution)/shard_map/dot_general | solution.py:20
  295.1 9.0 %second_norm.3 = (bf16[256,2048]{1,0:T(8,128)(2,1)}, f32[256,2048]{1,0:T(8,128)}, f32[256,1]{1,0:T(8,128)}) custom-call(s32[4]{0:T(128)} %pad_add_fusion.order, bf16[256,512]{1,0:T(8,128)(2,1)} %bitcast.134, bf16[256,512]{1,0:T(8,128)(2,1)} %copy-done.64, bf16[256,512]{1,0:T(8,128)(2,1)} %copy-done.65, bf16[256,512]{1,0:T(8,128)(2,1)} %broadcast_select_fusion.31.refs_3_, ...), custom_call_target="tpu_custom_call" | custom-call | flops 2155872256 | bytes 2097152 | tf_op jit(solution)/shard_map/second_norm/pallas_call | solution.py:825
  321.3 16.7 %collective-permute-done.51.refs_1_ = bf16[512,512]{1,0:T(8,128)(2,1)S(1)} collective-permute-done((bf16[512,512]{1,0:T(8,128)(2,1)S(1)}, bf16[512,512]{1,0:T(8,128)(2,1)S(1)}, u32[]{:S(2)}, u32[]{:S(2)}) %collective-permute-start.51) | collective-permute-done | bytes 524320 | tf_op jit(solution)/shard_map/ppermute | solution.py:33
  384.1 11.9 %multiply_convert_fusion.1 = (bf16[512,2048]{1,0:T(8,128)(2,1)S(1)}, bf16[512,2048]{1,0:T(8,128)(2,1)S(1)}) fusion(f32[512,2048]{1,0:T(8,128)} %copy-done.131, f32[512,2048]{1,0:T(8,128)} %get-tuple-element.324, bf16[512,2048]{1,0:T(8,128)(2,1)} %spread.3, bf16[2048,2048]{1,0:T(8,128)(2,1)} %constant_dynamic-update-slice_fusion), kind=kOutput, calls=%fused_computation.7 | convolution fusion | flops 4308598784 | bytes 23068672 | tf_op jit(solution)/shard_map/dot_general | solution.py:24
  425.0 9.0 convolution_convert_fusion.2
  434.1 11.7 %convolution_convert_fusion.1 = bf16[2048,2048]{1,0:T(8,128)(2,1)} fusion(bf16[768,2048]{1,0:T(8,128)(2,1)} %copy-done.35, bf16[768,2048]{1,0:T(8,128)(2,1)} %pad_maximum_fusion.2), kind=kOutput, calls=%fused_computation.1 | convolution fusion | flops 6446645248 | bytes 14680064 | tf_op jit(solution)/shard_map/dot_general | solution.py:28
  459.9 9.5 %convolution_convert_fusion = bf16[2048,2048]{1,0:T(8,128)(2,1)} fusion(bf16[768,2048]{1,0:T(8,128)(2,1)S(1)} %copy-done.33, bf16[768,2048]{1,0:T(8,128)(2,1)S(1)} %copy-done.34), kind=kOutput, calls=%fused_computation | convolution fusion | flops 6446645248 | bytes 14680064 | tf_op jit(solution)/shard_map/dot_general | solution.py:28
  497.2 19.0 %collective-permute-done.64.refs_6_ = bf16[256,512]{1,0:T(8,128)(2,1)} collective-permute-done((bf16[256,512]{1,0:T(8,128)(2,1)S(1)}, bf16[256,512]{1,0:T(8,128)(2,1)}, u32[]{:S(2)}, u32[]{:S(2)}) %collective-permute-start.64) | collective-permute-done | bytes 262176 | tf_op jit(solution)/shard_map/ppermute | solution.py:33
  526.0 19.3 %cont_backward.1 = (f32[2,128,512]{2,1,0:T(8,128)}, f32[2,1024,128]{2,1,0:T(8,128)}, f32[2,1024,128]{2,1,0:T(8,128)}, f32[2,128,128]{2,1,0:T(8,128)}, f32[2,128,128]{2,1,0:T(8,128)}) custom-call(s32[2]{0:T(128)} %subtract_clamp_fusion.which, bf16[2,128,512]{2,1,0:T(8,128)(2,1)} %bitcast.188, bf16[2,1024,256]{2,1,0:T(8,128)(2,1)} %copy-done.70, ...), custom_call_target="tpu_custom_call" | custom-call | flops 3019898880 | bytes 4456448 | tf_op jit(solution)/shard_map/cont_backward/pallas_call | solution.py:682
  574.0 14.1 %collective-permute-done.66.refs_5_ = bf16[512,512]{1,0:T(8,128)(2,1)S(1)} collective-permute-done((bf16[512,512]{1,0:T(8,128)(2,1)S(1)}, bf16[512,512]{1,0:T(8,128)(2,1)S(1)}, u32[]{:S(2)}, u32[]{:S(2)}) %collective-permute-start.66) | collective-permute-done | bytes 524320 | tf_op jit(solution)/shard_map/ppermute | solution.py:33
  588.0 16.7 %collective-permute-done.67.refs_6_ = bf16[512,512]{1,0:T(8,128)(2,1)S(1)} collective-permute-done((bf16[512,512]{1,0:T(8,128)(2,1)S(1)}, bf16[512,512]{1,0:T(8,128)(2,1)S(1)}, u32[]{:S(2)}, u32[]{:S(2)}) %collective-permute-start.67) | collective-permute-done | bytes 524320 | tf_op jit(solution)/shard_map/ppermute | solution.py:33
  605.3 16.9 %collective-permute-start.73 = (bf16[256,512]{1,0:T(8,128)(2,1)}, bf16[256,512]{1,0:T(8,128)(2,1)}, u32[]{:S(2)}, u32[]{:S(2)}) collective-permute-start(bf16[256,512]{1,0:T(8,128)(2,1)} %fusion.8), channel_id=1, source_target_pairs={{0,2},{1,3},{2,0},{3,1},{4,6},{5,7},{6,4},{7,5},{8,10},{9,11},{10,... | collective-permute-start | bytes 786440 | tf_op jit(solution)/shard_map/ppermute | solution.py:33
  633.3 21.6 %prompt_backward.1 = (f32[2,256,512]{2,1,0:T(8,128)}, f32[2,1024,128]{2,1,0:T(8,128)}, f32[2,1024,128]{2,1,0:T(8,128)}) custom-call(s32[1]{0:T(128)} %bitcast.5.start, bf16[2,256,512]{2,1,0:T(8,128)(2,1)} %bitcast.179, bf16[2,1024,256]{2,1,0:T(8,128)(2,1)} %copy-done.70, bf16[2,256,512]{2,1,0:T(8,128)(2,1)} %get-tuple-element.128.o_ref, ...), custom_call_target="tpu_custom_call" | custom-call | flops 5368709120 | bytes 5767168 | tf_op jit(solution)/shard_map/prompt_backward/pallas_call | solution.py:576
  718.1 8.8 collective-permute-done.99
  776.3 12.0 %collective-permute-done.84 = bf16[256,2048]{1,0:T(8,128)(2,1)} collective-permute-done((bf16[256,2048]{1,0:T(8,128)(2,1)}, bf16[256,2048]{1,0:T(8,128)(2,1)}, u32[]{:S(2)}, u32[]{:S(2)}) %collective-permute-start.84) | collective-permute-done | bytes 1048608 | tf_op jit(solution)/shard_map/ppermute | solution.py:33
  815.8 16.7 %collective-permute-done.113 = bf16[2048,256]{1,0:T(8,128)(2,1)S(1)} collective-permute-done((bf16[2048,256]{1,0:T(8,128)(2,1)}, bf16[2048,256]{1,0:T(8,128)(2,1)S(1)}, u32[]{:S(2)}, u32[]{:S(2)}) %collective-permute-start.113) | collective-permute-done | bytes 1048608 | tf_op jit(solution)/shard_map/ppermute | solution.py:33
  849.7 22.0 %collective-permute-done.92 = bf16[512,512]{1,0:T(8,128)(2,1)} collective-permute-done((bf16[512,512]{1,0:T(8,128)(2,1)}, bf16[512,512]{1,0:T(8,128)(2,1)}, u32[]{:S(2)}, u32[]{:S(2)}) %collective-permute-start.92) | collective-permute-done | bytes 524320 | tf_op jit(solution)/shard_map/ppermute | solution.py:33
  (724 shorter events, 560.3 us)
Async XLA Ops:
  7.3 754.7 %reduce-scatter.4.cloned.1.call-start = ((), (), s32[]{:S(2)}) async-start(), calls=%async_computation.3 | async-start | bytes 9437184 | tf_op jit(solution)/shard_map/reduce_scatter | solution.py:183
  29.7 61.8 %collective-permute-start.15 = (bf16[256,2048]{1,0:T(8,128)(2,1)S(1)}, bf16[256,2048]{1,0:T(8,128)(2,1)S(1)}, u32[]{:S(2)}, u32[]{:S(2)}) collective-permute-start(bf16[256,2048]{1,0:T(8,128)(2,1)S(1)} %constant_dynamic-slice_fusion.4), channel_id=1, source_target_pairs={{0,16},{16,0},{1,17},{17,1},{2,18},{18,2},{3,19},{19,3},{4,20},{20... | collective-permute-start | bytes 3145736 | tf_op jit(solution)/shard_map/ppermute | solution.py:33
  98.1 55.0 %collective-permute-start.31 = (bf16[256,2048]{1,0:T(8,128)(2,1)S(1)}, bf16[256,2048]{1,0:T(8,128)(2,1)}, u32[]{:S(2)}, u32[]{:S(2)}) collective-permute-start(bf16[256,2048]{1,0:T(8,128)(2,1)S(1)} %collective-permute-done.15), channel_id=1, source_target_pairs={{0,8},{4,12},{8,0},{12,4},{1,9},{5,13},{9,1},{13,5},{2,10},{6,14},... | collective-permute-start | bytes 3145736 | tf_op jit(solution)/shard_map/ppermute | solution.py:33
  99.8 56.4 %collective-permute-start.32 = (bf16[256,2048]{1,0:T(8,128)(2,1)S(1)}, bf16[256,2048]{1,0:T(8,128)(2,1)}, u32[]{:S(2)}, u32[]{:S(2)}) collective-permute-start(bf16[256,2048]{1,0:T(8,128)(2,1)S(1)} %collective-permute-done.15), channel_id=1, source_target_pairs={{0,4},{4,0},{8,12},{12,8},{1,5},{5,1},{9,13},{13,9},{2,6},{6,2},{1... | collective-permute-start | bytes 3145736 | tf_op jit(solution)/shard_map/ppermute | solution.py:33
  126.9 47.0 %collective-permute-start.24 = (bf16[2048,256]{1,0:T(8,128)(2,1)}, bf16[2048,256]{1,0:T(8,128)(2,1)}, u32[]{:S(2)}, u32[]{:S(2)}) collective-permute-start(bf16[2048,256]{1,0:T(8,128)(2,1)} %get-tuple-element.295), channel_id=1, source_target_pairs={{0,16},{16,0},{1,17},{17,1},{2,18},{18,2},{3,19},{19,3},{4,20},{20... | collective-permute-start | bytes 3145736 | tf_op jit(solution)/shard_map/ppermute | solution.py:33
  255.3 56.3 %collective-permute-start.48 = (bf16[256,512]{1,0:T(8,128)(2,1)S(1)}, bf16[256,512]{1,0:T(8,128)(2,1)S(1)}, u32[]{:S(2)}, u32[]{:S(2)}) collective-permute-start(bf16[256,512]{1,0:T(8,128)(2,1)S(1)} %bitcast.152), channel_id=1, source_target_pairs={{1,2},{2,1},{5,6},{6,5},{9,10},{10,9},{13,14},{14,13},{17,18},{18,... | collective-permute-start | bytes 786440 | tf_op jit(solution)/shard_map/ppermute | solution.py:55
  256.0 55.7 %collective-permute-start.49 = (bf16[256,512]{1,0:T(8,128)(2,1)S(1)}, bf16[256,512]{1,0:T(8,128)(2,1)S(1)}, u32[]{:S(2)}, u32[]{:S(2)}) collective-permute-start(bf16[256,512]{1,0:T(8,128)(2,1)S(1)} %collective-permute-done.47.refs_2_), channel_id=1, source_target_pairs={{2,3},{1,0},{6,7},{5,4},{10,11},{9,8},{14,15},{13,12},{18,19},{17,... | collective-permute-start | bytes 786440 | tf_op jit(solution)/shard_map/ppermute | solution.py:57
  259.9 83.9 %collective-permute-start.56 = (bf16[2048,256]{1,0:T(8,128)(2,1)}, bf16[2048,256]{1,0:T(8,128)(2,1)S(1)}, u32[]{:S(2)}, u32[]{:S(2)}) collective-permute-start(bf16[2048,256]{1,0:T(8,128)(2,1)} %collective-permute-done.50), channel_id=1, source_target_pairs={{0,4},{4,0},{8,12},{12,8},{1,5},{5,1},{9,13},{13,9},{2,6},{6,2},{1... | collective-permute-start | bytes 3145736 | tf_op jit(solution)/shard_map/ppermute | solution.py:33
  315.6 64.0 %collective-permute-start.53 = (bf16[512,512]{1,0:T(8,128)(2,1)S(1)}, bf16[512,512]{1,0:T(8,128)(2,1)}, u32[]{:S(2)}, u32[]{:S(2)}) collective-permute-start(bf16[512,512]{1,0:T(8,128)(2,1)S(1)} %bitcast.147), channel_id=1, source_target_pairs={{1,2},{2,1},{5,6},{6,5},{9,10},{10,9},{13,14},{14,13},{17,18},{18,... | collective-permute-start | bytes 1572872 | tf_op jit(solution)/shard_map/ppermute | solution.py:55
  372.4 49.9 %collective-permute-start.59 = (bf16[256,512]{1,0:T(8,128)(2,1)}, bf16[256,512]{1,0:T(8,128)(2,1)S(1)}, u32[]{:S(2)}, u32[]{:S(2)}) collective-permute-start(bf16[256,512]{1,0:T(8,128)(2,1)} %fusion.103), channel_id=1, source_target_pairs={{0,3},{1,2},{2,1},{3,0},{4,7},{5,6},{6,5},{7,4},{8,11},{9,10},{10,... | collective-permute-start | bytes 786440 | tf_op jit(solution)/shard_map/ppermute | solution.py:33
  374.1 48.2 %collective-permute-start.58 = (bf16[256,512]{1,0:T(8,128)(2,1)}, bf16[256,512]{1,0:T(8,128)(2,1)}, u32[]{:S(2)}, u32[]{:S(2)}) collective-permute-start(bf16[256,512]{1,0:T(8,128)(2,1)} %fusion.97), channel_id=1, source_target_pairs={{0,2},{1,3},{2,0},{3,1},{4,6},{5,7},{6,4},{7,5},{8,10},{9,11},{10,... | collective-permute-start | bytes 786440 | tf_op jit(solution)/shard_map/ppermute | solution.py:33
  434.0 340.2 %reduce-scatter.6.cloned.1.call-start = ((), (), s32[]{:S(2)}) async-start(), calls=%async_computation.4 | async-start | bytes 9437184 | tf_op jit(solution)/shard_map/reduce_scatter | solution.py:183
  445.8 329.9 %reduce-scatter.8.cloned.1.call-start = ((), (), s32[]{:S(2)}) async-start(), calls=%async_computation.5 | async-start | bytes 9437184 | tf_op jit(solution)/shard_map/reduce_scatter | solution.py:183
  451.5 106.9 %collective-permute-start.62 = (bf16[512,512]{1,0:T(8,128)(2,1)}, bf16[512,512]{1,0:T(8,128)(2,1)}, u32[]{:S(2)}, u32[]{:S(2)}) collective-permute-start(bf16[512,512]{1,0:T(8,128)(2,1)} %fusion.85), channel_id=1, source_target_pairs={{0,3},{1,2},{2,1},{3,0},{4,7},{5,6},{6,5},{7,4},{8,11},{9,10},{10,... | collective-permute-start | bytes 1572872 | tf_op jit(solution)/shard_map/ppermute | solution.py:33
  453.4 105.1 %collective-permute-start.61 = (bf16[512,512]{1,0:T(8,128)(2,1)}, bf16[512,512]{1,0:T(8,128)(2,1)}, u32[]{:S(2)}, u32[]{:S(2)}) collective-permute-start(bf16[512,512]{1,0:T(8,128)(2,1)} %fusion.67), channel_id=1, source_target_pairs={{0,2},{1,3},{2,0},{3,1},{4,6},{5,7},{6,4},{7,5},{8,10},{9,11},{10,... | collective-permute-start | bytes 1572872 | tf_op jit(solution)/shard_map/ppermute | solution.py:33
  455.9 60.2 %collective-permute-start.64 = (bf16[256,512]{1,0:T(8,128)(2,1)S(1)}, bf16[256,512]{1,0:T(8,128)(2,1)}, u32[]{:S(2)}, u32[]{:S(2)}) collective-permute-start(bf16[256,512]{1,0:T(8,128)(2,1)S(1)} %get-tuple-element.234.refs_4_), channel_id=1, source_target_pairs={{0,2},{1,3},{2,0},{3,1},{4,6},{5,7},{6,4},{7,5},{8,10},{9,11},{10,... | collective-permute-start | bytes 786440 | tf_op jit(solution)/shard_map/ppermute | solution.py:33
  458.0 58.2 %collective-permute-start.65 = (bf16[256,512]{1,0:T(8,128)(2,1)S(1)}, bf16[256,512]{1,0:T(8,128)(2,1)}, u32[]{:S(2)}, u32[]{:S(2)}) collective-permute-start(bf16[256,512]{1,0:T(8,128)(2,1)S(1)} %get-tuple-element.234.refs_4_), channel_id=1, source_target_pairs={{0,3},{1,2},{2,1},{3,0},{4,7},{5,6},{6,5},{7,4},{8,11},{9,10},{10,... | collective-permute-start | bytes 786440 | tf_op jit(solution)/shard_map/ppermute | solution.py:33
  497.2 61.3 %collective-permute-start.60 = (bf16[512,512]{1,0:T(8,128)(2,1)S(1)}, bf16[512,512]{1,0:T(8,128)(2,1)S(1)}, u32[]{:S(2)}, u32[]{:S(2)}) collective-permute-start(bf16[512,512]{1,0:T(8,128)(2,1)S(1)} %copy-done.126), channel_id=1, source_target_pairs={{0,1},{1,0},{2,3},{3,2},{4,5},{5,4},{6,7},{7,6},{8,9},{9,8},{10,11... | collective-permute-start | bytes 1572872 | tf_op jit(solution)/shard_map/ppermute | solution.py:33
  604.8 55.2 %collective-permute-start.74 = (bf16[256,512]{1,0:T(8,128)(2,1)}, bf16[256,512]{1,0:T(8,128)(2,1)}, u32[]{:S(2)}, u32[]{:S(2)}) collective-permute-start(bf16[256,512]{1,0:T(8,128)(2,1)} %fusion.115), channel_id=1, source_target_pairs={{0,3},{1,2},{2,1},{3,0},{4,7},{5,6},{6,5},{7,4},{8,11},{9,10},{10,... | collective-permute-start | bytes 786440 | tf_op jit(solution)/shard_map/ppermute | solution.py:33
  605.3 56.0 %collective-permute-start.73 = (bf16[256,512]{1,0:T(8,128)(2,1)}, bf16[256,512]{1,0:T(8,128)(2,1)}, u32[]{:S(2)}, u32[]{:S(2)}) collective-permute-start(bf16[256,512]{1,0:T(8,128)(2,1)} %fusion.8), channel_id=1, source_target_pairs={{0,2},{1,3},{2,0},{3,1},{4,6},{5,7},{6,4},{7,5},{8,10},{9,11},{10,... | collective-permute-start | bytes 786440 | tf_op jit(solution)/shard_map/ppermute | solution.py:33
  700.3 50.7 %collective-permute-start.69 = (bf16[512,512]{1,0:T(8,128)(2,1)}, bf16[512,512]{1,0:T(8,128)(2,1)}, u32[]{:S(2)}, u32[]{:S(2)}) collective-permute-start(bf16[512,512]{1,0:T(8,128)(2,1)} %fusion.73), channel_id=1, source_target_pairs={{0,1},{1,0},{2,3},{3,2},{4,5},{5,4},{6,7},{7,6},{8,9},{9,8},{10,11... | collective-permute-start | bytes 1572872 | tf_op jit(solution)/shard_map/ppermute | solution.py:33
  775.7 56.8 %collective-permute-start.113 = (bf16[2048,256]{1,0:T(8,128)(2,1)}, bf16[2048,256]{1,0:T(8,128)(2,1)S(1)}, u32[]{:S(2)}, u32[]{:S(2)}) collective-permute-start(bf16[2048,256]{1,0:T(8,128)(2,1)} %reduce-scatter.8.cloned.1.call-done), channel_id=1, source_target_pairs={{0,8},{4,12},{8,0},{12,4},{1,9},{5,13},{9,1},{13,5},{2,10},{6,14},... | collective-permute-start | bytes 3145736 | tf_op jit(solution)/shard_map/ppermute | solution.py:33
  790.6 51.5 %collective-permute-start.85 = (bf16[512,512]{1,0:T(8,128)(2,1)}, bf16[512,512]{1,0:T(8,128)(2,1)}, u32[]{:S(2)}, u32[]{:S(2)}) collective-permute-start(bf16[512,512]{1,0:T(8,128)(2,1)} %convolution_convert_fusion.5), channel_id=1, source_target_pairs={{3,2},{0,1},{7,6},{4,5},{11,10},{8,9},{15,14},{12,13},{19,18},{16,... | collective-permute-start | bytes 1572872 | tf_op jit(solution)/shard_map/ppermute | solution.py:99
  795.3 47.1 %collective-permute-start.86 = (bf16[512,512]{1,0:T(8,128)(2,1)}, bf16[512,512]{1,0:T(8,128)(2,1)}, u32[]{:S(2)}, u32[]{:S(2)}) collective-permute-start(bf16[512,512]{1,0:T(8,128)(2,1)} %convolution_convert_fusion.5), channel_id=1, source_target_pairs={{1,2},{2,1},{5,6},{6,5},{9,10},{10,9},{13,14},{14,13},{17,18},{18,... | collective-permute-start | bytes 1572872 | tf_op jit(solution)/shard_map/ppermute | solution.py:100
  (231 other events, 3935.2 us)
Sparse Core Ops, SparseCore 0:
  434.1 71.1 reduce-scatter.3
  509.4 71.5 reduce-scatter.5
  584.4 71.2 reduce-scatter.7

commit v4 on v3

--- a/solution.py
+++ b/solution.py
@@ -70,9 +70,8 @@
 def group_sum(value):
     if not paired():
         return lax.psum(value, EVERY)
-    for axis, step in (("ctx", 1), ("ctx", 2), ("fsdp", 1)):
-        value = value + swap(value, axis, step)
-    return value
+    value = all_sum(value, "ctx")
+    return value + swap(value, "fsdp", 1)
 
 
 def blocks_of(make_block):
@@ -990,7 +989,7 @@
         return g, u, s, (g * s * u).astype(BF)
 
     ahead = [forward(0), forward(1)]
-    cot_prompt, sent_prompt = gather_tp(tie(cots[0], (sent_cont, ahead[0][3], xn2_cont, down_moves[1])))
+    cot_prompt, sent_prompt = gather_tp(tie(cots[0], (sent_cont, xn2_prompt, down_moves[1])))
     cot_parts = [cot_prompt, cot_cont]
 
     inner, gate_grad, up_grad = [None, None], [None, None], [None, None]

time: 913 us -> 912 us (level)
    ppermute x98 -> x99, starting transfers between devices: 119 us -> 121 us  [swap(): return lax.ppermute(value, axis, [(i, i ^ step) for i in range(count)])]
    ppermute x98 -> x99, waiting for transfers between devices: 225 us -> 225 us  [swap(): return lax.ppermute(value, axis, [(i, i ^ step) for i in range(count)])]
  transfers between devices with their start and end apart: 119 -> 120, of which waited for: 38 -> 37; matrix products, arithmetic and copies ran while one was open for 37% -> 37% of each run, Pallas kernels for 14% -> 14%
where the time goes in v4:
time: 912 us; the launch traced here: 903 us
  waiting for transfers between devices  245 us (27%)
  matrix products  178 us (20%)
  starting transfers between devices  151 us (17%)
  Pallas kernels  129 us (14%)
  other arithmetic  108 us (12%)
  local copies, waits for them, and re-layouts  74.2 us (8%)
  between operations  16.3 us (2%)
    ppermute x99, waiting for transfers between devices, swap(): return lax.ppermute(value, axis, [(i, i ^ step) for i in range(count)])  225 us
    ppermute x99, starting transfers between devices, swap(): return lax.ppermute(value, axis, [(i, i ^ step) for i in range(count)])  121 us
    dot_general x28, matrix products, product_nt(): lax.dot_general(left, right, (((1,), (1,)), ((), ())), preferred_element_...  72.4 us
    dot_general x12, matrix products, product(): return jnp.dot(left, right, preferred_element_type=F32)  63.5 us
    dot_general x11, matrix products, product_tn(): lax.dot_general(left, right, (((0,), (0,)), ((), ())), preferred_element_...  42.4 us
    pallas_call x6, Pallas kernels, placed_call(): pl.pallas_call(kernel, out_shape=[jax.ShapeDtypeStruct((rows, w), d) for...  40.7 us
    pallas_call x1, Pallas kernels, prompt_backward(): pl.pallas_call(prompt_backward_kernel, out_shape=[jax.ShapeDtypeStruct(qu...  21.6 us
    ppermute x7, waiting for transfers between devices, gather_tp(): passed = lax.ppermute(ready, 'tp', [(2, 3), (1, 0)])  20.4 us
  transfers between devices with their start and end apart: 120, of which 37 were waited for; matrix products, arithmetic and copies ran while one was open for 37% of the time, Pallas kernels for 14%

profile of v4, /device:TPU:0, one launch (start us, length us, event | category | flops | bytes accessed | tf_op | source)
XLA Modules:
  0.0 903.1 jit_solution(577329975867755012)
XLA Ops:
  57.1 14.1 %collective-permute-done.4 = bf16[512,512]{1,0:T(8,128)(2,1)S(1)} collective-permute-done((bf16[512,512]{1,0:T(8,128)(2,1)}, bf16[512,512]{1,0:T(8,128)(2,1)S(1)}, u32[]{:S(2)}, u32[]{:S(2)}) %collective-permute-start.4) | collective-permute-done | bytes 524320 | tf_op jit(solution)/shard_map/ppermute | solution.py:57
  131.3 17.6 %prompt_forward.1 = (bf16[2,256,512]{2,1,0:T(8,128)(2,1)}, f32[2,4,2,256]{3,2,1,0:T(2,128)}) custom-call(s32[1]{0:T(128)} %bitcast.5.start, bf16[2,256,512]{2,1,0:T(8,128)(2,1)} %bitcast.178, bf16[2,1024,256]{2,1,0:T(8,128)(2,1)} %copy-done.69), custom_call_target="tpu_custom_call" | custom-call | flops 2147483648 | bytes 2097152 | tf_op jit(solution)/shard_map/prompt_forward/pallas_call | solution.py:399
  191.8 11.4 %cont_forward.1 = (bf16[2,128,512]{2,1,0:T(8,128)(2,1)}, f32[2,4,1,256]{3,2,1,0:T(1,128)}) custom-call(s32[2]{0:T(128)} %subtract_clamp_fusion.which, bf16[2,128,512]{2,1,0:T(8,128)(2,1)} %bitcast.187, bf16[2,1024,256]{2,1,0:T(8,128)(2,1)} %copy-done.69, bf16[2,128,256]{2,1,0:T(8,128)(2,1)} %bitcast.189), custom_call_target="tpu_custom_call" | custom-call | flops 1207959552 | bytes 1572864 | tf_op jit(solution)/shard_map/cont_forward/pallas_call | solution.py:459
  211.0 7.8 collective-permute-done.42.refs_5_
  243.8 11.8 %collective-permute-done.47.refs_2_ = bf16[256,512]{1,0:T(8,128)(2,1)S(1)} collective-permute-done((bf16[256,512]{1,0:T(8,128)(2,1)S(1)}, bf16[256,512]{1,0:T(8,128)(2,1)S(1)}, u32[]{:S(2)}, u32[]{:S(2)}) %collective-permute-start.47) | collective-permute-done | bytes 262176 | tf_op jit(solution)/shard_map/ppermute | solution.py:33
  263.3 12.2 %second_norm.2 = (bf16[512,2048]{1,0:T(8,128)(2,1)}, f32[512,2048]{1,0:T(8,128)}, f32[512,1]{1,0:T(8,128)}) custom-call(s32[4]{0:T(128)} %pad_add_fusion.order, bf16[512,512]{1,0:T(8,128)(2,1)} %bitcast.142, bf16[512,512]{1,0:T(8,128)(2,1)} %collective-permute-done.refs_1_, bf16[512,512]{1,0:T(8,128)(2,1)} %collective-permute-done.1.refs_2_, ...), custom_call_target="tpu_custom_call" | custom-call | flops 4311744512 | bytes 4194304 | tf_op jit(solution)/shard_map/second_norm/pallas_call | solution.py:824
  275.5 10.5 %fusion.226 = f32[512,2048]{1,0:T(8,128)} fusion(bf16[512,2048]{1,0:T(8,128)(2,1)} %get-tuple-element.131, bf16[2048,2048]{1,0:T(8,128)(2,1)} %constant_dynamic-update-slice_fusion.10), kind=kOutput, calls=%fused_computation.380 | convolution fusion | flops 4294967296 | bytes 14680064 | tf_op jit(solution)/shard_map/dot_general | solution.py:20
  286.0 9.0 second_norm.3
  312.4 16.5 %collective-permute-done.51.refs_1_ = bf16[512,512]{1,0:T(8,128)(2,1)S(1)} collective-permute-done((bf16[512,512]{1,0:T(8,128)(2,1)S(1)}, bf16[512,512]{1,0:T(8,128)(2,1)S(1)}, u32[]{:S(2)}, u32[]{:S(2)}) %collective-permute-start.51) | collective-permute-done | bytes 524320 | tf_op jit(solution)/shard_map/ppermute | solution.py:33
  373.4 7.6 fusion.229
  381.1 10.2 %multiply_convert_fusion.2 = (bf16[512,2048]{1,0:T(8,128)(2,1)S(1)}, bf16[512,2048]{1,0:T(8,128)(2,1)S(1)}, bf16[512,2048]{1,0:T(8,128)(2,1)S(1)}) fusion(f32[512,2048]{1,0:T(8,128)} %fusion.226, f32[512,2048]{1,0:T(8,128)S(1)} %fusion.229, bf16[512,2048]{1,0:T(8,128)(2,1)S(1)} %copy-done.44, bf16[2048,2048]{1,0:T(8,128)(2,1)} %constant_dynamic-update-slice_fusion.5), kind=kOutput, calls=%fused_computation.8 | convolution fusion | flops 4311744512 | bytes 25165824 | tf_op jit(solution)/shard_map/dot_general | solution.py:20
  423.7 9.2 %convolution_convert_fusion.2 = bf16[2048,2048]{1,0:T(8,128)(2,1)} fusion(bf16[768,2048]{1,0:T(8,128)(2,1)S(1)} %pad_maximum_fusion, bf16[768,2048]{1,0:T(8,128)(2,1)S(1)} %pad_maximum_fusion.1), kind=kOutput, calls=%fused_computation.2 | convolution fusion | flops 6446645248 | bytes 14680064 | tf_op jit(solution)/shard_map/dot_general | solution.py:28
  432.9 11.6 %convolution_convert_fusion.1 = bf16[2048,2048]{1,0:T(8,128)(2,1)} fusion(bf16[768,2048]{1,0:T(8,128)(2,1)} %copy-done.35, bf16[768,2048]{1,0:T(8,128)(2,1)} %pad_maximum_fusion.2), kind=kOutput, calls=%fused_computation.1 | convolution fusion | flops 6446645248 | bytes 14680064 | tf_op jit(solution)/shard_map/dot_general | solution.py:28
  458.8 9.4 %convolution_convert_fusion = bf16[2048,2048]{1,0:T(8,128)(2,1)} fusion(bf16[768,2048]{1,0:T(8,128)(2,1)S(1)} %copy-done.34, bf16[768,2048]{1,0:T(8,128)(2,1)S(1)} %copy-done.33), kind=kOutput, calls=%fused_computation | convolution fusion | flops 6446645248 | bytes 14680064 | tf_op jit(solution)/shard_map/dot_general | solution.py:28
  496.0 18.9 %collective-permute-done.64.refs_6_ = bf16[256,512]{1,0:T(8,128)(2,1)} collective-permute-done((bf16[256,512]{1,0:T(8,128)(2,1)S(1)}, bf16[256,512]{1,0:T(8,128)(2,1)}, u32[]{:S(2)}, u32[]{:S(2)}) %collective-permute-start.64) | collective-permute-done | bytes 262176 | tf_op jit(solution)/shard_map/ppermute | solution.py:33
  524.9 19.3 %cont_backward.1 = (f32[2,128,512]{2,1,0:T(8,128)}, f32[2,1024,128]{2,1,0:T(8,128)}, f32[2,1024,128]{2,1,0:T(8,128)}, f32[2,128,128]{2,1,0:T(8,128)}, f32[2,128,128]{2,1,0:T(8,128)}) custom-call(s32[2]{0:T(128)} %subtract_clamp_fusion.which, bf16[2,128,512]{2,1,0:T(8,128)(2,1)} %bitcast.188, bf16[2,1024,256]{2,1,0:T(8,128)(2,1)} %copy-done.69, ...), custom_call_target="tpu_custom_call" | custom-call | flops 3019898880 | bytes 4456448 | tf_op jit(solution)/shard_map/cont_backward/pallas_call | solution.py:681
  572.6 14.3 %collective-permute-done.66.refs_5_ = bf16[512,512]{1,0:T(8,128)(2,1)S(1)} collective-permute-done((bf16[512,512]{1,0:T(8,128)(2,1)S(1)}, bf16[512,512]{1,0:T(8,128)(2,1)S(1)}, u32[]{:S(2)}, u32[]{:S(2)}) %collective-permute-start.66) | collective-permute-done | bytes 524320 | tf_op jit(solution)/shard_map/ppermute | solution.py:33
  586.9 16.4 %collective-permute-done.67.refs_6_ = bf16[512,512]{1,0:T(8,128)(2,1)S(1)} collective-permute-done((bf16[512,512]{1,0:T(8,128)(2,1)S(1)}, bf16[512,512]{1,0:T(8,128)(2,1)S(1)}, u32[]{:S(2)}, u32[]{:S(2)}) %collective-permute-start.67) | collective-permute-done | bytes 524320 | tf_op jit(solution)/shard_map/ppermute | solution.py:33
  604.2 16.8 %collective-permute-start.73 = (bf16[256,512]{1,0:T(8,128)(2,1)}, bf16[256,512]{1,0:T(8,128)(2,1)}, u32[]{:S(2)}, u32[]{:S(2)}) collective-permute-start(bf16[256,512]{1,0:T(8,128)(2,1)} %fusion.8), channel_id=1, source_target_pairs={{0,2},{1,3},{2,0},{3,1},{4,6},{5,7},{6,4},{7,5},{8,10},{9,11},{10,... | collective-permute-start | bytes 786440 | tf_op jit(solution)/shard_map/ppermute | solution.py:33
  632.0 21.6 %prompt_backward.1 = (f32[2,256,512]{2,1,0:T(8,128)}, f32[2,1024,128]{2,1,0:T(8,128)}, f32[2,1024,128]{2,1,0:T(8,128)}) custom-call(s32[1]{0:T(128)} %bitcast.5.start, bf16[2,256,512]{2,1,0:T(8,128)(2,1)} %bitcast.179, bf16[2,1024,256]{2,1,0:T(8,128)(2,1)} %copy-done.69, bf16[2,256,512]{2,1,0:T(8,128)(2,1)} %get-tuple-element.128.o_ref, ...), custom_call_target="tpu_custom_call" | custom-call | flops 5368709120 | bytes 5767168 | tf_op jit(solution)/shard_map/prompt_backward/pallas_call | solution.py:575
  716.8 8.8 collective-permute-done.100
  775.5 11.8 %collective-permute-done.84 = bf16[256,2048]{1,0:T(8,128)(2,1)} collective-permute-done((bf16[256,2048]{1,0:T(8,128)(2,1)}, bf16[256,2048]{1,0:T(8,128)(2,1)}, u32[]{:S(2)}, u32[]{:S(2)}) %collective-permute-start.84) | collective-permute-done | bytes 1048608 | tf_op jit(solution)/shard_map/ppermute | solution.py:33
  814.6 16.8 %collective-permute-done.114 = bf16[2048,256]{1,0:T(8,128)(2,1)S(1)} collective-permute-done((bf16[2048,256]{1,0:T(8,128)(2,1)}, bf16[2048,256]{1,0:T(8,128)(2,1)S(1)}, u32[]{:S(2)}, u32[]{:S(2)}) %collective-permute-start.114) | collective-permute-done | bytes 1048608 | tf_op jit(solution)/shard_map/ppermute | solution.py:33
  847.3 22.3 %collective-permute-done.92 = bf16[512,512]{1,0:T(8,128)(2,1)} collective-permute-done((bf16[512,512]{1,0:T(8,128)(2,1)}, bf16[512,512]{1,0:T(8,128)(2,1)}, u32[]{:S(2)}, u32[]{:S(2)}) %collective-permute-start.92) | collective-permute-done | bytes 524320 | tf_op jit(solution)/shard_map/ppermute | solution.py:33
  (719 shorter events, 560.9 us)
Async XLA Ops:
  7.3 753.6 %reduce-scatter.4.cloned.1.call-start = ((), (), s32[]{:S(2)}) async-start(), calls=%async_computation.3 | async-start | bytes 9437184 | tf_op jit(solution)/shard_map/reduce_scatter | solution.py:182
  29.7 61.8 %collective-permute-start.15 = (bf16[256,2048]{1,0:T(8,128)(2,1)S(1)}, bf16[256,2048]{1,0:T(8,128)(2,1)S(1)}, u32[]{:S(2)}, u32[]{:S(2)}) collective-permute-start(bf16[256,2048]{1,0:T(8,128)(2,1)S(1)} %constant_dynamic-slice_fusion.4), channel_id=1, source_target_pairs={{0,16},{16,0},{1,17},{17,1},{2,18},{18,2},{3,19},{19,3},{4,20},{20... | collective-permute-start | bytes 3145736 | tf_op jit(solution)/shard_map/ppermute | solution.py:33
  98.1 55.0 %collective-permute-start.31 = (bf16[256,2048]{1,0:T(8,128)(2,1)S(1)}, bf16[256,2048]{1,0:T(8,128)(2,1)}, u32[]{:S(2)}, u32[]{:S(2)}) collective-permute-start(bf16[256,2048]{1,0:T(8,128)(2,1)S(1)} %collective-permute-done.15), channel_id=1, source_target_pairs={{0,8},{4,12},{8,0},{12,4},{1,9},{5,13},{9,1},{13,5},{2,10},{6,14},... | collective-permute-start | bytes 3145736 | tf_op jit(solution)/shard_map/ppermute | solution.py:33
  99.8 56.4 %collective-permute-start.32 = (bf16[256,2048]{1,0:T(8,128)(2,1)S(1)}, bf16[256,2048]{1,0:T(8,128)(2,1)}, u32[]{:S(2)}, u32[]{:S(2)}) collective-permute-start(bf16[256,2048]{1,0:T(8,128)(2,1)S(1)} %collective-permute-done.15), channel_id=1, source_target_pairs={{0,4},{4,0},{8,12},{12,8},{1,5},{5,1},{9,13},{13,9},{2,6},{6,2},{1... | collective-permute-start | bytes 3145736 | tf_op jit(solution)/shard_map/ppermute | solution.py:33
  126.9 46.9 %collective-permute-start.24 = (bf16[2048,256]{1,0:T(8,128)(2,1)}, bf16[2048,256]{1,0:T(8,128)(2,1)}, u32[]{:S(2)}, u32[]{:S(2)}) collective-permute-start(bf16[2048,256]{1,0:T(8,128)(2,1)} %get-tuple-element.296), channel_id=1, source_target_pairs={{0,16},{16,0},{1,17},{17,1},{2,18},{18,2},{3,19},{19,3},{4,20},{20... | collective-permute-start | bytes 3145736 | tf_op jit(solution)/shard_map/ppermute | solution.py:33
  255.6 47.0 %collective-permute-start.48 = (bf16[256,512]{1,0:T(8,128)(2,1)S(1)}, bf16[256,512]{1,0:T(8,128)(2,1)S(1)}, u32[]{:S(2)}, u32[]{:S(2)}) collective-permute-start(bf16[256,512]{1,0:T(8,128)(2,1)S(1)} %bitcast.152), channel_id=1, source_target_pairs={{1,2},{2,1},{5,6},{6,5},{9,10},{10,9},{13,14},{14,13},{17,18},{18,... | collective-permute-start | bytes 786440 | tf_op jit(solution)/shard_map/ppermute | solution.py:55
  260.1 74.6 %collective-permute-start.56 = (bf16[2048,256]{1,0:T(8,128)(2,1)}, bf16[2048,256]{1,0:T(8,128)(2,1)S(1)}, u32[]{:S(2)}, u32[]{:S(2)}) collective-permute-start(bf16[2048,256]{1,0:T(8,128)(2,1)} %collective-permute-done.50), channel_id=1, source_target_pairs={{0,4},{4,0},{8,12},{12,8},{1,5},{5,1},{9,13},{13,9},{2,6},{6,2},{1... | collective-permute-start | bytes 3145736 | tf_op jit(solution)/shard_map/ppermute | solution.py:33
  306.7 62.2 %collective-permute-start.53 = (bf16[512,512]{1,0:T(8,128)(2,1)S(1)}, bf16[512,512]{1,0:T(8,128)(2,1)}, u32[]{:S(2)}, u32[]{:S(2)}) collective-permute-start(bf16[512,512]{1,0:T(8,128)(2,1)S(1)} %bitcast.147), channel_id=1, source_target_pairs={{1,2},{2,1},{5,6},{6,5},{9,10},{10,9},{13,14},{14,13},{17,18},{18,... | collective-permute-start | bytes 1572872 | tf_op jit(solution)/shard_map/ppermute | solution.py:55
  361.4 59.5 %collective-permute-start.59 = (bf16[256,512]{1,0:T(8,128)(2,1)}, bf16[256,512]{1,0:T(8,128)(2,1)S(1)}, u32[]{:S(2)}, u32[]{:S(2)}) collective-permute-start(bf16[256,512]{1,0:T(8,128)(2,1)} %fusion.103), channel_id=1, source_target_pairs={{0,3},{1,2},{2,1},{3,0},{4,7},{5,6},{6,5},{7,4},{8,11},{9,10},{10,... | collective-permute-start | bytes 786440 | tf_op jit(solution)/shard_map/ppermute | solution.py:33
  363.1 57.7 %collective-permute-start.58 = (bf16[256,512]{1,0:T(8,128)(2,1)}, bf16[256,512]{1,0:T(8,128)(2,1)}, u32[]{:S(2)}, u32[]{:S(2)}) collective-permute-start(bf16[256,512]{1,0:T(8,128)(2,1)} %fusion.97), channel_id=1, source_target_pairs={{0,2},{1,3},{2,0},{3,1},{4,6},{5,7},{6,4},{7,5},{8,10},{9,11},{10,... | collective-permute-start | bytes 786440 | tf_op jit(solution)/shard_map/ppermute | solution.py:33
  365.5 56.1 %collective-permute-start.57 = (bf16[256,512]{1,0:T(8,128)(2,1)}, bf16[256,512]{1,0:T(8,128)(2,1)}, u32[]{:S(2)}, u32[]{:S(2)}) collective-permute-start(bf16[256,512]{1,0:T(8,128)(2,1)} %fusion.106), channel_id=1, source_target_pairs={{0,1},{1,0},{2,3},{3,2},{4,5},{5,4},{6,7},{7,6},{8,9},{9,8},{10,11... | collective-permute-start | bytes 786440 | tf_op jit(solution)/shard_map/ppermute | solution.py:33
  432.9 340.5 %reduce-scatter.6.cloned.1.call-start = ((), (), s32[]{:S(2)}) async-start(), calls=%async_computation.4 | async-start | bytes 9437184 | tf_op jit(solution)/shard_map/reduce_scatter | solution.py:182
  444.6 330.0 %reduce-scatter.8.cloned.1.call-start = ((), (), s32[]{:S(2)}) async-start(), calls=%async_computation.5 | async-start | bytes 9437184 | tf_op jit(solution)/shard_map/reduce_scatter | solution.py:182
  450.2 107.4 %collective-permute-start.62 = (bf16[512,512]{1,0:T(8,128)(2,1)}, bf16[512,512]{1,0:T(8,128)(2,1)}, u32[]{:S(2)}, u32[]{:S(2)}) collective-permute-start(bf16[512,512]{1,0:T(8,128)(2,1)} %fusion.85), channel_id=1, source_target_pairs={{0,3},{1,2},{2,1},{3,0},{4,7},{5,6},{6,5},{7,4},{8,11},{9,10},{10,... | collective-permute-start | bytes 1572872 | tf_op jit(solution)/shard_map/ppermute | solution.py:33
  452.2 105.5 %collective-permute-start.61 = (bf16[512,512]{1,0:T(8,128)(2,1)}, bf16[512,512]{1,0:T(8,128)(2,1)}, u32[]{:S(2)}, u32[]{:S(2)}) collective-permute-start(bf16[512,512]{1,0:T(8,128)(2,1)} %fusion.67), channel_id=1, source_target_pairs={{0,2},{1,3},{2,0},{3,1},{4,6},{5,7},{6,4},{7,5},{8,10},{9,11},{10,... | collective-permute-start | bytes 1572872 | tf_op jit(solution)/shard_map/ppermute | solution.py:33
  454.6 60.3 %collective-permute-start.64 = (bf16[256,512]{1,0:T(8,128)(2,1)S(1)}, bf16[256,512]{1,0:T(8,128)(2,1)}, u32[]{:S(2)}, u32[]{:S(2)}) collective-permute-start(bf16[256,512]{1,0:T(8,128)(2,1)S(1)} %get-tuple-element.234.refs_4_), channel_id=1, source_target_pairs={{0,2},{1,3},{2,0},{3,1},{4,6},{5,7},{6,4},{7,5},{8,10},{9,11},{10,... | collective-permute-start | bytes 786440 | tf_op jit(solution)/shard_map/ppermute | solution.py:33
  456.8 58.1 %collective-permute-start.65 = (bf16[256,512]{1,0:T(8,128)(2,1)S(1)}, bf16[256,512]{1,0:T(8,128)(2,1)}, u32[]{:S(2)}, u32[]{:S(2)}) collective-permute-start(bf16[256,512]{1,0:T(8,128)(2,1)S(1)} %get-tuple-element.234.refs_4_), channel_id=1, source_target_pairs={{0,3},{1,2},{2,1},{3,0},{4,7},{5,6},{6,5},{7,4},{8,11},{9,10},{10,... | collective-permute-start | bytes 786440 | tf_op jit(solution)/shard_map/ppermute | solution.py:33
  496.0 61.7 %collective-permute-start.60 = (bf16[512,512]{1,0:T(8,128)(2,1)S(1)}, bf16[512,512]{1,0:T(8,128)(2,1)S(1)}, u32[]{:S(2)}, u32[]{:S(2)}) collective-permute-start(bf16[512,512]{1,0:T(8,128)(2,1)S(1)} %copy-done.124), channel_id=1, source_target_pairs={{0,1},{1,0},{2,3},{3,2},{4,5},{5,4},{6,7},{7,6},{8,9},{9,8},{10,11... | collective-permute-start | bytes 1572872 | tf_op jit(solution)/shard_map/ppermute | solution.py:33
  603.4 55.6 %collective-permute-start.74 = (bf16[256,512]{1,0:T(8,128)(2,1)}, bf16[256,512]{1,0:T(8,128)(2,1)}, u32[]{:S(2)}, u32[]{:S(2)}) collective-permute-start(bf16[256,512]{1,0:T(8,128)(2,1)} %fusion.115), channel_id=1, source_target_pairs={{0,3},{1,2},{2,1},{3,0},{4,7},{5,6},{6,5},{7,4},{8,11},{9,10},{10,... | collective-permute-start | bytes 786440 | tf_op jit(solution)/shard_map/ppermute | solution.py:33
  604.2 55.9 %collective-permute-start.73 = (bf16[256,512]{1,0:T(8,128)(2,1)}, bf16[256,512]{1,0:T(8,128)(2,1)}, u32[]{:S(2)}, u32[]{:S(2)}) collective-permute-start(bf16[256,512]{1,0:T(8,128)(2,1)} %fusion.8), channel_id=1, source_target_pairs={{0,2},{1,3},{2,0},{3,1},{4,6},{5,7},{6,4},{7,5},{8,10},{9,11},{10,... | collective-permute-start | bytes 786440 | tf_op jit(solution)/shard_map/ppermute | solution.py:33
  699.3 50.9 %collective-permute-start.69 = (bf16[512,512]{1,0:T(8,128)(2,1)}, bf16[512,512]{1,0:T(8,128)(2,1)}, u32[]{:S(2)}, u32[]{:S(2)}) collective-permute-start(bf16[512,512]{1,0:T(8,128)(2,1)} %fusion.73), channel_id=1, source_target_pairs={{0,1},{1,0},{2,3},{3,2},{4,5},{5,4},{6,7},{7,6},{8,9},{9,8},{10,11... | collective-permute-start | bytes 1572872 | tf_op jit(solution)/shard_map/ppermute | solution.py:33
  703.1 47.1 %collective-permute-start.70 = (bf16[512,512]{1,0:T(8,128)(2,1)}, bf16[512,512]{1,0:T(8,128)(2,1)}, u32[]{:S(2)}, u32[]{:S(2)}) collective-permute-start(bf16[512,512]{1,0:T(8,128)(2,1)} %fusion.10), channel_id=1, source_target_pairs={{0,2},{1,3},{2,0},{3,1},{4,6},{5,7},{6,4},{7,5},{8,10},{9,11},{10,... | collective-permute-start | bytes 1572872 | tf_op jit(solution)/shard_map/ppermute | solution.py:33
  774.6 56.8 %collective-permute-start.114 = (bf16[2048,256]{1,0:T(8,128)(2,1)}, bf16[2048,256]{1,0:T(8,128)(2,1)S(1)}, u32[]{:S(2)}, u32[]{:S(2)}) collective-permute-start(bf16[2048,256]{1,0:T(8,128)(2,1)} %reduce-scatter.8.cloned.1.call-done), channel_id=1, source_target_pairs={{0,8},{4,12},{8,0},{12,4},{1,9},{5,13},{9,1},{13,5},{2,10},{6,14},... | collective-permute-start | bytes 3145736 | tf_op jit(solution)/shard_map/ppermute | solution.py:33
  789.5 50.7 %collective-permute-start.85 = (bf16[512,512]{1,0:T(8,128)(2,1)}, bf16[512,512]{1,0:T(8,128)(2,1)}, u32[]{:S(2)}, u32[]{:S(2)}) collective-permute-start(bf16[512,512]{1,0:T(8,128)(2,1)} %convolution_convert_fusion.5), channel_id=1, source_target_pairs={{3,2},{0,1},{7,6},{4,5},{11,10},{8,9},{15,14},{12,13},{19,18},{16,... | collective-permute-start | bytes 1572872 | tf_op jit(solution)/shard_map/ppermute | solution.py:98
  (229 other events, 4079.0 us)
Sparse Core Ops, SparseCore 0:
  433.0 71.2 reduce-scatter.3
  507.8 71.5 reduce-scatter.5
  582.8 71.2 reduce-scatter.7
